TPU v7x, 32 devices: a whole 2x2x4 slice. The times are simulated.
32 devices in a mesh: date: 4 (over y, x), tile: 8 (over z, core).
Axes of the slice: x: 2, y: 2, z: 4, core: 2. Of those that a mesh axis runs over, the one named last changes fastest.
Arguments:
- swath_intensities: bfloat16 [4, 128, 64, 2, 512], P('date', 'tile'), may hold values from 0.0099487305 to 1
- destination_patch: int32 [128, 1], P('tile'), may hold values from 0 to 7; in each aligned block of 16 rows (0 to 15, 16 to 31, ...) at most 4 rows name the same one
- swath_leading_scanline: int32 [128], P('tile'), may hold values from 0 to 64
- receiver_floor_intensity: float32 [4, 1024, 2, 512], P('date', 'tile'), may hold values from 0.1 to 1
Outputs:
- filtered: bfloat16 [4, 1024, 2, 512], P('date', 'tile')
Inputs may be any that keep to these rules, and one draw needn't show every extreme that they name: `destination_patch`: among the 16 blocks of one device no owner is named more than 4 times.
All inputs are finite; a program needn't handle non-finite values.
Results may differ from a plain program's by a relative error of at most 0.008.
Values may be sent and summed in bfloat16 or wider, within the bound.
No kernel may reach another device: no remote copies, remote signals or barrier semaphores. Data moves between devices by JAX's collectives and lax.ppermute only.
A program may use at most 128 MiB of HBM per device.

v0:
```python
import functools

import jax
import jax.numpy as jnp
from jax import lax
from jax.experimental import pallas as pl
from jax.experimental.pallas import tpu as pltpu
from jax.sharding import PartitionSpec as P


LANES = 128
REACH = 3
STEP = 8
VMEM = pl.BlockSpec(memory_space=pltpu.VMEM)
HBM = pl.BlockSpec(memory_space=pltpu.HBM)
F32, BF16 = jnp.float32, jnp.bfloat16


def pack(array):
    *lead, pols, cols = array.shape
    axis = len(lead)
    array = array.reshape(*lead, pols, cols // LANES, LANES)
    return jnp.swapaxes(array, axis, axis + 1).reshape(*lead, pols * cols // LANES, LANES)


def unpack(array, pols):
    *lead, subs, _ = array.shape
    axis = len(lead)
    array = array.reshape(*lead, subs // pols, pols, LANES)
    return jnp.swapaxes(array, axis, axis + 1).reshape(*lead, pols, subs // pols * LANES)


def rows_loop(count, body, unroll=1):
    lax.fori_loop(0, count // STEP, lambda i, c: (body(pl.multiple_of(i * STEP, STEP)), c)[1], 0, unroll=unroll)


def slot_of(relay, chips, owner_chip, chip):
    return owner_chip ^ chip if relay else lax.rem(owner_chip - chip + chips, chips)


def place_kernel(relay, chips, early, owner_hbm, lead_hbm, swath_hbm, *refs):
    early_ref, other_ref, own_ref, acc, swath, owner, lead, sems = refs
    blocks, scan, _, _ = swath.shape
    rows = own_ref.shape[1]
    me = lax.axis_index("tile")
    core, chip = me % 2, me // 2
    small = (
        pltpu.make_async_copy(owner_hbm, owner, sems.at[blocks]),
        pltpu.make_async_copy(lead_hbm, lead, sems.at[blocks + 1]),
    )
    for copy in small:
        copy.start()

    def fetch(block):
        return pltpu.make_async_copy(swath_hbm.at[block], swath.at[block], sems.at[block])

    for block in range(blocks):
        fetch(block).start()

    def clear(at):
        zero = jnp.zeros((STEP,) + acc.shape[2:], F32)
        for slot in range(chips):
            acc[slot, pl.ds(at, STEP)] = zero
            own_ref[slot, pl.ds(at, STEP)] = zero

    rows_loop(rows, clear)
    for copy in small:
        copy.wait()

    def add_into(ref, slot, block, base):
        for row in range(0, scan, STEP):
            span = pl.ds(base + row, STEP)
            ref[slot, span] = ref[slot, span] + swath[block, pl.ds(row, STEP)].astype(F32)

    def insert(block, carry):
        target = owner[block]
        base = lead[block]
        slot = slot_of(relay, chips, target // 2, chip)
        fetch(block).wait()

        @pl.when(target % 2 == core)
        def _():
            add_into(own_ref, slot, block, base)

        @pl.when(target % 2 != core)
        def _():
            add_into(acc, slot, block, base)

        return carry

    lax.fori_loop(0, blocks, insert, 0)
    others = [slot for slot in range(chips) if slot != early]

    def emit(at):
        span = pl.ds(at, STEP)
        early_ref[span] = acc[early, span].astype(BF16)
        for place, slot in enumerate(others):
            other_ref[place, span] = acc[slot, span].astype(BF16)

    rows_loop(rows, emit)


def merge_early_kernel(early, own_ref, came_ref, send_ref):
    def part(at):
        span = pl.ds(at, STEP)
        send_ref[span] = (own_ref[early, span] + came_ref[span].astype(F32)).astype(BF16)

    rows_loop(send_ref.shape[0], part)


def merge_kernel(slots, own_ref, floor_ref, came_ref, keep_ref, *send_refs):
    def part(at):
        span = pl.ds(at, STEP)
        for place, slot in enumerate(slots):
            total = own_ref[slot, span] + came_ref[place, span].astype(F32)
            if place:
                send_refs[place - 1][span] = total.astype(BF16)
            else:
                keep_ref[span] = total + floor_ref[span]

    rows_loop(keep_ref.shape[0], part)


def relay_kernel(far_ref, passing_ref, send_ref):
    def part(at):
        span = pl.ds(at, STEP)
        send_ref[span] = (far_ref[span].astype(F32) + passing_ref[span].astype(F32)).astype(BF16)

    rows_loop(send_ref.shape[0], part)


def box_kernel(relay, pols, keep_ref, *refs):
    *came_refs, means_ref, ratio_ref, upper_ref, lower_ref, canvas = refs
    rows, subs, _ = keep_ref.shape
    zero = jnp.zeros((STEP, subs, LANES), F32)
    canvas[pl.ds(0, STEP)] = zero
    canvas[pl.ds(rows + STEP, STEP)] = zero

    def gather(refs):
        def part(at):
            span = pl.ds(at, STEP)
            total = keep_ref[span]
            for came in refs:
                total = total + came[span].astype(F32)
            canvas[pl.ds(at + STEP, STEP)] = total

        rows_loop(rows, part)

    if relay:
        first, direct, passed, near = came_refs
        chip = lax.axis_index("tile") // 2
        ends = (chip == 0) | (chip == 3)
        pl.when(ends)(lambda: gather((first, direct, near)))
        pl.when(jnp.logical_not(ends))(lambda: gather((passed, near)))
    else:
        gather(came_refs)

    shape = (STEP, subs, LANES)
    sub = lax.broadcasted_iota(jnp.int32, shape, 1)
    lane = lax.broadcasted_iota(jnp.int32, shape, 2)
    cols = subs // pols * LANES

    def counted(place, length):
        return jnp.minimum(place + REACH, length - 1) - jnp.maximum(place - REACH, 0) + 1

    col_scale = 1.0 / counted(sub // pols * LANES + lane, cols).astype(F32)

    def ahead(x, by):
        after = jnp.where(sub < subs - pols, pltpu.roll(x, subs - pols, 1), 0.0)
        return pltpu.roll(jnp.where(lane < by, after, x), LANES - by, 2)

    def behind(x, by):
        before = jnp.where(sub >= pols, pltpu.roll(x, pols, 1), 0.0)
        return pltpu.roll(jnp.where(lane >= LANES - by, before, x), by, 2)

    edge_ahead = (sub >= subs - pols) & (lane == LANES - 2)
    edge_behind = (sub < pols) & (lane == 1)

    def box(at, scale, send_ref):
        x = canvas[pl.ds(at + STEP - REACH, STEP + 2 * REACH)]
        two = x[:-1] + x[1:]
        four = two[:-2] + two[2:]
        total = four[:STEP] + two[4 : 4 + STEP] + x[6 : 6 + STEP]
        right, left = ahead(total, 1), behind(total, 1)
        triple = left + total + right
        edge = jnp.where(edge_ahead, right, jnp.where(edge_behind, left, 0.0))
        total = behind(triple, 2) + (total + edge) + ahead(triple, 2)
        means = total * scale
        ratio = x[REACH : REACH + STEP] / means
        span = pl.ds(at, STEP)
        means_ref[span] = means
        ratio_ref[span] = ratio
        send_ref[pl.ds(at % (rows // 2), STEP)] = ratio.astype(BF16)

    row = lax.broadcasted_iota(jnp.int32, shape, 0)
    inner = col_scale * (1.0 / (2 * REACH + 1))
    for at in range(0, rows, STEP):
        outer = at in (0, rows - STEP)
        scale = col_scale / counted(row + at, rows).astype(F32) if outer else inner
        box(at, scale, (upper_ref, lower_ref)[2 * at // rows])


def add_kernel(start, ratio_ref, came_ref, sum_ref, send_ref):
    def part(at):
        span = pl.ds(at, STEP)
        total = ratio_ref[pl.ds(at + start, STEP)] + came_ref[span].astype(F32)
        sum_ref[span] = total
        send_ref[span] = total.astype(BF16)

    rows_loop(sum_ref.shape[0], part, unroll=True)


def scale_kernel(dates, start, means_ref, sum_ref, came_ref, *refs):
    out_hbm, out, sems = refs[-3:]
    rows = sum_ref.shape[0]
    pieces = 2
    size = rows // pieces

    def copy(piece):
        here = pl.ds(piece * size, size)
        return pltpu.make_async_copy(out.at[here], out_hbm.at[pl.ds(start + piece * size, size)], sems.at[piece])

    for piece in range(pieces):
        for at in range(piece * size, piece * size + size, STEP):
            span = pl.ds(at, STEP)
            total = (sum_ref[span] + came_ref[span].astype(F32)) * (1.0 / dates)
            out[span] = (means_ref[pl.ds(start + at, STEP)] * total).astype(BF16)
        copy(piece).start()
    for piece in range(pieces):
        copy(piece).wait()


def call(kernel, outs, ins, specs=None, mib=8, scratch=(), out_specs=None, aliases=None):
    return pl.pallas_call(
        kernel,
        out_shape=outs,
        in_specs=specs or [VMEM] * len(ins),
        out_specs=out_specs or jax.tree.map(lambda _: VMEM, outs),
        scratch_shapes=scratch,
        input_output_aliases=aliases or {},
        compiler_params=pltpu.CompilerParams(vmem_limit_bytes=mib << 20),
    )(*ins)


def permute(array, axes, pairs):
    return lax.ppermute(array, axes, pairs)


def per_device(tiles, dates, swaths, patch, lead, floor):
    chips = tiles // 2
    relay = chips == 4
    pols = swaths.shape[3]
    swaths, floor = pack(swaths[0]), pack(floor[0])
    blocks = swaths.shape[0]
    rows, subs, _ = floor.shape
    full = (rows, subs, LANES)
    wide = jax.ShapeDtypeStruct(full, F32)
    thin = jax.ShapeDtypeStruct(full, BF16)

    early = 2 if relay else 1
    canvases = 4 * rows * subs * LANES * chips
    early_out, other, own = call(
        functools.partial(place_kernel, relay, chips, early),
        (thin, jax.ShapeDtypeStruct((chips - 1,) + full, BF16), jax.ShapeDtypeStruct((chips,) + full, F32)),
        tuple(pltpu.with_memory_space_constraint(a, pltpu.HBM) for a in (patch[:, 0], lead, swaths)),
        specs=[HBM] * 3,
        mib=(3 * canvases >> 20) + 4,
        scratch=[
            pltpu.VMEM((chips,) + full, F32),
            pltpu.VMEM(swaths.shape, BF16),
            pltpu.SMEM((blocks,), jnp.int32),
            pltpu.SMEM((blocks,), jnp.int32),
            pltpu.SemaphoreType.DMA((blocks + 2,)),
        ],
    )
    partner = [(t, t ^ 1) for t in range(tiles)]
    early_came = permute(early_out, "tile", partner)
    came = permute(other, "tile", partner)
    early_send = call(functools.partial(merge_early_kernel, early), thin, (own, early_came))

    def along(array, moves):
        return permute(array, "tile", [(2 * a + core, 2 * b + core) for a, b in moves for core in range(2)])

    ordered = [s for s in range(chips) if s != early]
    if relay:
        first = along(early_send, [(0, 1), (3, 2), (1, 3), (2, 0)])
    else:
        first = along(early_send, [(c, (c + early) % chips) for c in range(chips)])
    keep, *sends = call(
        functools.partial(merge_kernel, ordered),
        (wide,) + (thin,) * (chips - 2),
        (own, floor, came),
        mib=(2 * canvases >> 20) + 4,
    )
    if relay:
        near_send, far_send = sends
        direct = along(far_send, [(0, 3), (3, 0), (1, 1), (2, 2)])
        near = along(near_send, [(0, 1), (1, 0), (2, 3), (3, 2)])
        passing = call(relay_kernel, thin, (far_send, first))
        passed = along(passing, [(1, 2), (2, 1), (0, 0), (3, 3)])
        arrived = [first, direct, passed, near]
    else:
        arrived = [first]
        for shift, send in zip(ordered[1:], sends):
            arrived.append(along(send, [(c, (c + shift) % chips) for c in range(chips)]))

    half = (rows // 2, subs, LANES)
    wide_half, thin_half = jax.ShapeDtypeStruct(half, F32), jax.ShapeDtypeStruct(half, BF16)
    means, ratio, *sends = call(
        functools.partial(box_kernel, relay, pols),
        (wide, wide, thin_half, thin_half),
        (keep, *arrived),
        mib=8 if relay else 16,
        scratch=[pltpu.VMEM((rows + 2 * STEP, subs, LANES), F32)],
    )

    bits = [1 << b for b in range(dates.bit_length() - 1)]
    starts = (0, rows // 2)
    totals = [ratio, ratio]
    for step in range(len(bits)):
        came = []
        for side in range(2):
            pairs = []
            for d in range(dates):
                for t in range(tiles):
                    bit = bits[step] if (t + side) % 2 == 0 else bits[-1 - step]
                    pairs.append((d * tiles + t, (d ^ bit) * tiles + t))
            came.append(permute(sends[side], ("date", "tile"), pairs))
        if step + 1 < len(bits):
            for side in range(2):
                totals[side], sends[side] = call(
                    functools.partial(add_kernel, starts[side] if step == 0 else 0),
                    (wide_half, thin_half),
                    (totals[side], came[side]),
                    mib=4,
                )
    out = None
    for side in range(2):
        ins = (means, totals[side], came[side]) + (() if out is None else (out,))
        out = call(
            functools.partial(scale_kernel, float(dates), starts[side]),
            thin,
            ins,
            specs=[VMEM] * 3 + [HBM] * (len(ins) - 3),
            out_specs=HBM,
            aliases={3: 0} if len(ins) > 3 else {},
            mib=4,
            scratch=[pltpu.VMEM(half, BF16), pltpu.SemaphoreType.DMA((2,))],
        )
    return unpack(out, pols)[None]


def device_step(tiles, dates, *arrays):
    return per_device(tiles, dates, *arrays)


def solution(mesh):
    return jax.shard_map(
        functools.partial(device_step, mesh.shape["tile"], mesh.shape["date"]),
        mesh=mesh,
        in_specs=(
            P("date", "tile", None, None, None),
            P("tile", None),
            P("tile"),
            P("date", "tile", None, None),
        ),
        out_specs=P("date", "tile", None, None),
        check_vma=False,
    )
```

profile of v0, /device:TPU:0, one launch (start us, length us, event | category | flops | bytes accessed | tf_op | source)
XLA Modules:
  0.0 46.4 jit_solution(2847018328334221706)
XLA Ops:
  0.0 0.0 copy-start
  0.0 2.1 %shard_map.46 = (bf16[128,8,128]{2,1,0:T(8,128)(2,1)S(1)}, bf16[3,128,8,128]{3,2,1,0:T(8,128)(2,1)S(1)}, f32[4,128,8,128]{3,2,1,0:T(8,128)S(1)}) custom-call(s32[16]{0:T(128)} %bitcast.18, s32[16]{0:T(128)} %lead_hbm.1, bf16[16,64,8,128]{3,2,1,0:T(8,128)(2,1)} %bitcast.17), custom_call_target="tpu_custom_call" | custom-call | tf_op jit(solution)/shard_map/pallas_call | solution.py:234
  2.1 0.6 %collective-permute-start = (bf16[3,128,8,128]{3,2,1,0:T(8,128)(2,1)S(1)}, bf16[3,128,8,128]{3,2,1,0:T(8,128)(2,1)S(1)}, u32[]{:S(2)}, u32[]{:S(2)}) collective-permute-start(bf16[3,128,8,128]{3,2,1,0:T(8,128)(2,1)S(1)} %get-tuple-element.20), channel_id=1, source_target_pairs={{0,1},{1,0},{2,3},{3,2},{4,5},{5,4},{6,7},{7,6},{8,9},{9,8},{10,11... | collective-permute-start | bytes 2359304 | tf_op jit(solution)/shard_map/ppermute | solution.py:246
  2.7 0.1 collective-permute-start.1
  2.7 2.2 %collective-permute-done.1.came_ref = bf16[128,8,128]{2,1,0:T(8,128)(2,1)S(1)} collective-permute-done((bf16[128,8,128]{2,1,0:T(8,128)(2,1)S(1)}, bf16[128,8,128]{2,1,0:T(8,128)(2,1)S(1)}, u32[]{:S(2)}, u32[]{:S(2)}) %collective-permute-start.1) | collective-permute-done | bytes 262176 | tf_op jit(solution)/shard_map/ppermute | solution.py:246
  5.0 0.1 shard_map.48
  5.1 3.0 %collective-permute-start.2 = (bf16[128,8,128]{2,1,0:T(8,128)(2,1)S(1)}, bf16[128,8,128]{2,1,0:T(8,128)(2,1)S(1)}, u32[]{:S(2)}, u32[]{:S(2)}) collective-permute-start(bf16[128,8,128]{2,1,0:T(8,128)(2,1)S(1)} %shard_map.48), channel_id=1, source_target_pairs={{0,2},{1,3},{6,4},{7,5},{2,6},{3,7},{4,0},{5,1},{8,10},{9,11},{14,... | collective-permute-start | bytes 786440 | tf_op jit(solution)/shard_map/ppermute | solution.py:246
  8.1 0.0 collective-permute-done.came_ref
  8.1 0.0 copy-done
  8.1 0.2 shard_map.47
  8.3 7.4 %collective-permute-done.2.passing_ref.refs_0_ = bf16[128,8,128]{2,1,0:T(8,128)(2,1)S(1)} collective-permute-done((bf16[128,8,128]{2,1,0:T(8,128)(2,1)S(1)}, bf16[128,8,128]{2,1,0:T(8,128)(2,1)S(1)}, u32[]{:S(2)}, u32[]{:S(2)}) %collective-permute-start.2) | collective-permute-done | bytes 262176 | tf_op jit(solution)/shard_map/ppermute | solution.py:246
  15.7 0.1 shard_map.49
  15.8 0.7 %collective-permute-start.4 = (bf16[128,8,128]{2,1,0:T(8,128)(2,1)S(1)}, bf16[128,8,128]{2,1,0:T(8,128)(2,1)S(1)}, u32[]{:S(2)}, u32[]{:S(2)}) collective-permute-start(bf16[128,8,128]{2,1,0:T(8,128)(2,1)S(1)} %shard_map.49), channel_id=1, source_target_pairs={{2,4},{3,5},{4,2},{5,3},{0,0},{1,1},{6,6},{7,7},{10,12},{11,13},{1... | collective-permute-start | bytes 786440 | tf_op jit(solution)/shard_map/ppermute | solution.py:246
  16.5 3.6 %collective-permute-start.5 = (bf16[128,8,128]{2,1,0:T(8,128)(2,1)S(1)}, bf16[128,8,128]{2,1,0:T(8,128)(2,1)S(1)}, u32[]{:S(2)}, u32[]{:S(2)}) collective-permute-start(bf16[128,8,128]{2,1,0:T(8,128)(2,1)S(1)} %get-tuple-element.24), channel_id=1, source_target_pairs={{0,2},{1,3},{2,0},{3,1},{4,6},{5,7},{6,4},{7,5},{8,10},{9,11},{10,... | collective-permute-start | bytes 786440 | tf_op jit(solution)/shard_map/ppermute | solution.py:246
  20.1 3.4 %collective-permute-start.3 = (bf16[128,8,128]{2,1,0:T(8,128)(2,1)S(1)}, bf16[128,8,128]{2,1,0:T(8,128)(2,1)S(1)}, u32[]{:S(2)}, u32[]{:S(2)}) collective-permute-start(bf16[128,8,128]{2,1,0:T(8,128)(2,1)S(1)} %get-tuple-element.23.far_ref), channel_id=1, source_target_pairs={{0,6},{1,7},{6,0},{7,1},{2,2},{3,3},{4,4},{5,5},{8,14},{9,15},{14,... | collective-permute-start | bytes 786440 | tf_op jit(solution)/shard_map/ppermute | solution.py:246
  23.4 0.0 collective-permute-done.4.refs_2_
  23.5 3.3 %collective-permute-done.5.refs_3_ = bf16[128,8,128]{2,1,0:T(8,128)(2,1)S(1)} collective-permute-done((bf16[128,8,128]{2,1,0:T(8,128)(2,1)S(1)}, bf16[128,8,128]{2,1,0:T(8,128)(2,1)S(1)}, u32[]{:S(2)}, u32[]{:S(2)}) %collective-permute-start.5) | collective-permute-done | bytes 262176 | tf_op jit(solution)/shard_map/ppermute | solution.py:246
  26.8 5.6 %collective-permute-done.3.refs_1_ = bf16[128,8,128]{2,1,0:T(8,128)(2,1)S(1)} collective-permute-done((bf16[128,8,128]{2,1,0:T(8,128)(2,1)S(1)}, bf16[128,8,128]{2,1,0:T(8,128)(2,1)S(1)}, u32[]{:S(2)}, u32[]{:S(2)}) %collective-permute-start.3) | collective-permute-done | bytes 262176 | tf_op jit(solution)/shard_map/ppermute | solution.py:246
  32.3 1.6 %shard_map.50 = (f32[128,8,128]{2,1,0:T(8,128)S(1)}, f32[128,8,128]{2,1,0:T(8,128)S(1)}, bf16[64,8,128]{2,1,0:T(8,128)(2,1)S(1)}, bf16[64,8,128]{2,1,0:T(8,128)(2,1)S(1)}) custom-call(f32[128,8,128]{2,1,0:T(8,128)S(1)} %get-tuple-element.21.keep_ref, bf16[128,8,128]{2,1,0:T(8,128)(2,1)S(1)} %collective-permute-done.2.passing_ref.refs_0_, ...), custom_call_target="tpu_custom_call" | custom-call | tf_op jit(solution)/shard_map/pallas_call | solution.py:234
  34.0 1.6 %collective-permute-start.8 = (bf16[64,8,128]{2,1,0:T(8,128)(2,1)S(1)}, bf16[64,8,128]{2,1,0:T(8,128)(2,1)S(1)}, u32[]{:S(2)}, u32[]{:S(2)}) collective-permute-start(bf16[64,8,128]{2,1,0:T(8,128)(2,1)S(1)} %get-tuple-element.30), channel_id=1, source_target_pairs={{0,8},{1,17},{2,10},{3,19},{4,12},{5,21},{6,14},{7,23},{8,0},{9,25... | collective-permute-start | bytes 393224 | tf_op jit(solution)/shard_map/ppermute | solution.py:246
  35.5 1.5 %collective-permute-start.6 = (bf16[64,8,128]{2,1,0:T(8,128)(2,1)S(1)}, bf16[64,8,128]{2,1,0:T(8,128)(2,1)S(1)}, u32[]{:S(2)}, u32[]{:S(2)}) collective-permute-start(bf16[64,8,128]{2,1,0:T(8,128)(2,1)S(1)} %get-tuple-element.27), channel_id=1, source_target_pairs={{0,16},{1,9},{2,18},{3,11},{4,20},{5,13},{6,22},{7,15},{8,24},{9,1... | collective-permute-start | bytes 393224 | tf_op jit(solution)/shard_map/ppermute | solution.py:246
  37.1 2.2 %collective-permute-done.8.came_ref = bf16[64,8,128]{2,1,0:T(8,128)(2,1)S(1)} collective-permute-done((bf16[64,8,128]{2,1,0:T(8,128)(2,1)S(1)}, bf16[64,8,128]{2,1,0:T(8,128)(2,1)S(1)}, u32[]{:S(2)}, u32[]{:S(2)}) %collective-permute-start.8) | collective-permute-done | bytes 131104 | tf_op jit(solution)/shard_map/ppermute | solution.py:246
  39.3 1.3 %collective-permute-start.9 = (bf16[64,8,128]{2,1,0:T(8,128)(2,1)S(1)}, bf16[64,8,128]{2,1,0:T(8,128)(2,1)S(1)}, u32[]{:S(2)}, u32[]{:S(2)}) collective-permute-start(bf16[64,8,128]{2,1,0:T(8,128)(2,1)S(1)} %get-tuple-element.32), channel_id=1, source_target_pairs={{0,16},{1,9},{2,18},{3,11},{4,20},{5,13},{6,22},{7,15},{8,24},{9,1... | collective-permute-start | bytes 393224 | tf_op jit(solution)/shard_map/ppermute | solution.py:246
  40.6 0.0 collective-permute-done.6.came_ref
  40.7 1.6 %collective-permute-start.7 = (bf16[64,8,128]{2,1,0:T(8,128)(2,1)S(1)}, bf16[64,8,128]{2,1,0:T(8,128)(2,1)S(1)}, u32[]{:S(2)}, u32[]{:S(2)}) collective-permute-start(bf16[64,8,128]{2,1,0:T(8,128)(2,1)S(1)} %get-tuple-element.29), channel_id=1, source_target_pairs={{0,8},{1,17},{2,10},{3,19},{4,12},{5,21},{6,14},{7,23},{8,0},{9,25... | collective-permute-start | bytes 393224 | tf_op jit(solution)/shard_map/ppermute | solution.py:246
  42.2 2.1 %collective-permute-done.9.came_ref = bf16[64,8,128]{2,1,0:T(8,128)(2,1)S(1)} collective-permute-done((bf16[64,8,128]{2,1,0:T(8,128)(2,1)S(1)}, bf16[64,8,128]{2,1,0:T(8,128)(2,1)S(1)}, u32[]{:S(2)}, u32[]{:S(2)}) %collective-permute-start.9) | collective-permute-done | bytes 131104 | tf_op jit(solution)/shard_map/ppermute | solution.py:246
  44.4 0.7 %shard_map.53.refs_0_ = bf16[128,8,128]{2,1,0:T(8,128)(2,1)} custom-call(f32[128,8,128]{2,1,0:T(8,128)S(1)} %get-tuple-element.25.means_ref, f32[64,8,128]{2,1,0:T(8,128)S(1)} %get-tuple-element.31.sum_ref, bf16[64,8,128]{2,1,0:T(8,128)(2,1)S(1)} %collective-permute-done.9.came_ref), custom_call_target="tpu_custom_call" | custom-call | tf_op jit(solution)/shard_map/pallas_call | solution.py:234
  45.1 0.7 %collective-permute-done.7.came_ref = bf16[64,8,128]{2,1,0:T(8,128)(2,1)S(1)} collective-permute-done((bf16[64,8,128]{2,1,0:T(8,128)(2,1)S(1)}, bf16[64,8,128]{2,1,0:T(8,128)(2,1)S(1)}, u32[]{:S(2)}, u32[]{:S(2)}) %collective-permute-start.7) | collective-permute-done | bytes 131104 | tf_op jit(solution)/shard_map/ppermute | solution.py:246
  45.7 0.7 %shard_map.54 = bf16[128,8,128]{2,1,0:T(8,128)(2,1)} custom-call(f32[128,8,128]{2,1,0:T(8,128)S(1)} %get-tuple-element.25.means_ref, f32[64,8,128]{2,1,0:T(8,128)S(1)} %get-tuple-element.28.sum_ref, bf16[64,8,128]{2,1,0:T(8,128)(2,1)S(1)} %collective-permute-done.7.came_ref, bf16[128,8,128]{2,1,0:T(8,128)(2,1)} %shard_map.53.refs_0_), custom_call_target="tpu_custom_call", output_to_operand_aliasing={{}: (3, {})} | custom-call | tf_op jit(solution)/shard_map/pallas_call | solution.py:234
  (2 shorter events, 0.1 us)
Async XLA Ops:
  0.0 8.1 %copy-start = (f32[1,128,2,512]{3,2,1,0:T(2,128)S(1)}, f32[1,128,2,512]{3,2,1,0:T(2,128)}, u32[]{:S(2)}) copy-start(f32[1,128,2,512]{3,2,1,0:T(2,128)} %param.7) | copy-start | bytes 1572868
  2.1 6.0 %collective-permute-start = (bf16[3,128,8,128]{3,2,1,0:T(8,128)(2,1)S(1)}, bf16[3,128,8,128]{3,2,1,0:T(8,128)(2,1)S(1)}, u32[]{:S(2)}, u32[]{:S(2)}) collective-permute-start(bf16[3,128,8,128]{3,2,1,0:T(8,128)(2,1)S(1)} %get-tuple-element.20), channel_id=1, source_target_pairs={{0,1},{1,0},{2,3},{3,2},{4,5},{5,4},{6,7},{7,6},{8,9},{9,8},{10,11... | collective-permute-start | bytes 2359304 | tf_op jit(solution)/shard_map/ppermute | solution.py:246
  2.7 2.3 %collective-permute-start.1 = (bf16[128,8,128]{2,1,0:T(8,128)(2,1)S(1)}, bf16[128,8,128]{2,1,0:T(8,128)(2,1)S(1)}, u32[]{:S(2)}, u32[]{:S(2)}) collective-permute-start(bf16[128,8,128]{2,1,0:T(8,128)(2,1)S(1)} %get-tuple-element.22), channel_id=1, source_target_pairs={{0,1},{1,0},{2,3},{3,2},{4,5},{5,4},{6,7},{7,6},{8,9},{9,8},{10,11... | collective-permute-start | bytes 786440 | tf_op jit(solution)/shard_map/ppermute | solution.py:246
  5.1 10.6 %collective-permute-start.2 = (bf16[128,8,128]{2,1,0:T(8,128)(2,1)S(1)}, bf16[128,8,128]{2,1,0:T(8,128)(2,1)S(1)}, u32[]{:S(2)}, u32[]{:S(2)}) collective-permute-start(bf16[128,8,128]{2,1,0:T(8,128)(2,1)S(1)} %shard_map.48), channel_id=1, source_target_pairs={{0,2},{1,3},{6,4},{7,5},{2,6},{3,7},{4,0},{5,1},{8,10},{9,11},{14,... | collective-permute-start | bytes 786440 | tf_op jit(solution)/shard_map/ppermute | solution.py:246
  15.8 7.6 %collective-permute-start.4 = (bf16[128,8,128]{2,1,0:T(8,128)(2,1)S(1)}, bf16[128,8,128]{2,1,0:T(8,128)(2,1)S(1)}, u32[]{:S(2)}, u32[]{:S(2)}) collective-permute-start(bf16[128,8,128]{2,1,0:T(8,128)(2,1)S(1)} %shard_map.49), channel_id=1, source_target_pairs={{2,4},{3,5},{4,2},{5,3},{0,0},{1,1},{6,6},{7,7},{10,12},{11,13},{1... | collective-permute-start | bytes 786440 | tf_op jit(solution)/shard_map/ppermute | solution.py:246
  16.5 10.3 %collective-permute-start.5 = (bf16[128,8,128]{2,1,0:T(8,128)(2,1)S(1)}, bf16[128,8,128]{2,1,0:T(8,128)(2,1)S(1)}, u32[]{:S(2)}, u32[]{:S(2)}) collective-permute-start(bf16[128,8,128]{2,1,0:T(8,128)(2,1)S(1)} %get-tuple-element.24), channel_id=1, source_target_pairs={{0,2},{1,3},{2,0},{3,1},{4,6},{5,7},{6,4},{7,5},{8,10},{9,11},{10,... | collective-permute-start | bytes 786440 | tf_op jit(solution)/shard_map/ppermute | solution.py:246
  20.1 12.3 %collective-permute-start.3 = (bf16[128,8,128]{2,1,0:T(8,128)(2,1)S(1)}, bf16[128,8,128]{2,1,0:T(8,128)(2,1)S(1)}, u32[]{:S(2)}, u32[]{:S(2)}) collective-permute-start(bf16[128,8,128]{2,1,0:T(8,128)(2,1)S(1)} %get-tuple-element.23.far_ref), channel_id=1, source_target_pairs={{0,6},{1,7},{6,0},{7,1},{2,2},{3,3},{4,4},{5,5},{8,14},{9,15},{14,... | collective-permute-start | bytes 786440 | tf_op jit(solution)/shard_map/ppermute | solution.py:246
  34.0 5.3 %collective-permute-start.8 = (bf16[64,8,128]{2,1,0:T(8,128)(2,1)S(1)}, bf16[64,8,128]{2,1,0:T(8,128)(2,1)S(1)}, u32[]{:S(2)}, u32[]{:S(2)}) collective-permute-start(bf16[64,8,128]{2,1,0:T(8,128)(2,1)S(1)} %get-tuple-element.30), channel_id=1, source_target_pairs={{0,8},{1,17},{2,10},{3,19},{4,12},{5,21},{6,14},{7,23},{8,0},{9,25... | collective-permute-start | bytes 393224 | tf_op jit(solution)/shard_map/ppermute | solution.py:246
  35.5 5.1 %collective-permute-start.6 = (bf16[64,8,128]{2,1,0:T(8,128)(2,1)S(1)}, bf16[64,8,128]{2,1,0:T(8,128)(2,1)S(1)}, u32[]{:S(2)}, u32[]{:S(2)}) collective-permute-start(bf16[64,8,128]{2,1,0:T(8,128)(2,1)S(1)} %get-tuple-element.27), channel_id=1, source_target_pairs={{0,16},{1,9},{2,18},{3,11},{4,20},{5,13},{6,22},{7,15},{8,24},{9,1... | collective-permute-start | bytes 393224 | tf_op jit(solution)/shard_map/ppermute | solution.py:246
  39.3 5.0 %collective-permute-start.9 = (bf16[64,8,128]{2,1,0:T(8,128)(2,1)S(1)}, bf16[64,8,128]{2,1,0:T(8,128)(2,1)S(1)}, u32[]{:S(2)}, u32[]{:S(2)}) collective-permute-start(bf16[64,8,128]{2,1,0:T(8,128)(2,1)S(1)} %get-tuple-element.32), channel_id=1, source_target_pairs={{0,16},{1,9},{2,18},{3,11},{4,20},{5,13},{6,22},{7,15},{8,24},{9,1... | collective-permute-start | bytes 393224 | tf_op jit(solution)/shard_map/ppermute | solution.py:246
  40.7 5.0 %collective-permute-start.7 = (bf16[64,8,128]{2,1,0:T(8,128)(2,1)S(1)}, bf16[64,8,128]{2,1,0:T(8,128)(2,1)S(1)}, u32[]{:S(2)}, u32[]{:S(2)}) collective-permute-start(bf16[64,8,128]{2,1,0:T(8,128)(2,1)S(1)} %get-tuple-element.29), channel_id=1, source_target_pairs={{0,8},{1,17},{2,10},{3,19},{4,12},{5,21},{6,14},{7,23},{8,0},{9,25... | collective-permute-start | bytes 393224 | tf_op jit(solution)/shard_map/ppermute | solution.py:246
where the time goes:
time: 46.6 us; the launch traced here: 46.4 us
  waiting for transfers between devices  23.5 us (50%)
  starting transfers between devices  17.2 us (37%)
  Pallas kernels  5.62 us (12%)
    ppermute x10, waiting for transfers between devices, permute(): return lax.ppermute(array, axes, pairs)  23.5 us
    ppermute x10, starting transfers between devices, permute(): return lax.ppermute(array, axes, pairs)  17.2 us
    pallas_call x9, Pallas kernels, call(): pl.pallas_call(kernel, out_shape=outs, in_specs=specs or [VMEM] * len(ins...  5.62 us
  transfers between devices with their start and end apart: 10, of which 7 were waited for; matrix products, arithmetic and copies ran while one was open for 0% of the time, Pallas kernels for 2%

commit v1 on v0

--- a/solution.py
+++ b/solution.py
@@ -11,6 +11,7 @@
 LANES = 128
 REACH = 3
 STEP = 8
+CUT = 8
 VMEM = pl.BlockSpec(memory_space=pltpu.VMEM)
 HBM = pl.BlockSpec(memory_space=pltpu.HBM)
 F32, BF16 = jnp.float32, jnp.bfloat16
@@ -100,60 +101,62 @@
     rows_loop(rows, emit)
 
 
-def merge_early_kernel(early, own_ref, came_ref, send_ref):
-    def part(at):
-        span = pl.ds(at, STEP)
-        send_ref[span] = (own_ref[early, span] + came_ref[span].astype(F32)).astype(BF16)
-
-    rows_loop(send_ref.shape[0], part)
-
-
-def merge_kernel(slots, own_ref, floor_ref, came_ref, keep_ref, *send_refs):
-    def part(at):
+def store_rows(refs, at, value):
+    for ref in refs:
+        if at < ref.shape[0]:
+            ref[pl.ds(at, STEP)] = value.astype(ref.dtype)
+            return
+        at -= ref.shape[0]
+
+
+def load_rows(refs, at):
+    for ref in refs:
+        if at < ref.shape[0]:
+            return ref[pl.ds(at, STEP)].astype(F32)
+        at -= ref.shape[0]
+
+
+def merge_early_kernel(early, own_ref, came_ref, *send_refs):
+    for at in range(0, came_ref.shape[0], STEP):
+        span = pl.ds(at, STEP)
+        store_rows(send_refs, at, own_ref[early, span] + came_ref[span].astype(F32))
+
+
+def merge_kernel(slots, pieces, own_ref, floor_ref, came_ref, keep_ref, *send_refs):
+    send_refs = iter(send_refs)
+    sends = [[next(send_refs) for _ in range(count)] for count in pieces]
+    for at in range(0, keep_ref.shape[0], STEP):
         span = pl.ds(at, STEP)
         for place, slot in enumerate(slots):
             total = own_ref[slot, span] + came_ref[place, span].astype(F32)
             if place:
-                send_refs[place - 1][span] = total.astype(BF16)
+                store_rows(sends[place - 1], at, total)
             else:
                 keep_ref[span] = total + floor_ref[span]
 
-    rows_loop(keep_ref.shape[0], part)
-
-
-def relay_kernel(far_ref, passing_ref, send_ref):
-    def part(at):
-        span = pl.ds(at, STEP)
-        send_ref[span] = (far_ref[span].astype(F32) + passing_ref[span].astype(F32)).astype(BF16)
-
-    rows_loop(send_ref.shape[0], part)
-
-
-def box_kernel(relay, pols, keep_ref, *refs):
-    *came_refs, means_ref, ratio_ref, upper_ref, lower_ref, canvas = refs
+
+def relay_kernel(start, mine_ref, passing_ref, send_ref):
+    for at in range(0, send_ref.shape[0], STEP):
+        span = pl.ds(at, STEP)
+        total = mine_ref[pl.ds(start + at, STEP)].astype(F32) + passing_ref[span].astype(F32)
+        send_ref[span] = total.astype(BF16)
+
+
+def box_kernel(pieces, pols, first, last, keep_ref, *refs):
+    *came_refs, means_ref, ratio_ref, send_ref, canvas = refs
     rows, subs, _ = keep_ref.shape
+    low, high = max(first - STEP, 0), min(last + STEP, rows)
+    origin = first - STEP
     zero = jnp.zeros((STEP, subs, LANES), F32)
-    canvas[pl.ds(0, STEP)] = zero
-    canvas[pl.ds(rows + STEP, STEP)] = zero
-
-    def gather(refs):
-        def part(at):
-            span = pl.ds(at, STEP)
-            total = keep_ref[span]
-            for came in refs:
-                total = total + came[span].astype(F32)
-            canvas[pl.ds(at + STEP, STEP)] = total
-
-        rows_loop(rows, part)
-
-    if relay:
-        first, direct, passed, near = came_refs
-        chip = lax.axis_index("tile") // 2
-        ends = (chip == 0) | (chip == 3)
-        pl.when(ends)(lambda: gather((first, direct, near)))
-        pl.when(jnp.logical_not(ends))(lambda: gather((passed, near)))
-    else:
-        gather(came_refs)
+    came = iter(came_refs)
+    groups = [[next(came) for _ in range(count)] for count in pieces]
+    for at in range(origin, last + STEP, STEP):
+        total = zero
+        if low <= at < high:
+            total = keep_ref[pl.ds(at, STEP)]
+            for group in groups:
+                total = total + load_rows(group, at)
+        canvas[pl.ds(at - origin, STEP)] = total
 
     shape = (STEP, subs, LANES)
     sub = lax.broadcasted_iota(jnp.int32, shape, 1)
@@ -176,8 +179,8 @@
     edge_ahead = (sub >= subs - pols) & (lane == LANES - 2)
     edge_behind = (sub < pols) & (lane == 1)
 
-    def box(at, scale, send_ref):
-        x = canvas[pl.ds(at + STEP - REACH, STEP + 2 * REACH)]
+    def box(at, scale):
+        x = canvas[pl.ds(at - origin - REACH, STEP + 2 * REACH)]
         two = x[:-1] + x[1:]
         four = two[:-2] + two[2:]
         total = four[:STEP] + two[4 : 4 + STEP] + x[6 : 6 + STEP]
@@ -187,23 +190,23 @@
         total = behind(triple, 2) + (total + edge) + ahead(triple, 2)
         means = total * scale
         ratio = x[REACH : REACH + STEP] / means
-        span = pl.ds(at, STEP)
+        span = pl.ds(at - first, STEP)
         means_ref[span] = means
         ratio_ref[span] = ratio
-        send_ref[pl.ds(at % (rows // 2), STEP)] = ratio.astype(BF16)
+        send_ref[span] = ratio.astype(BF16)
 
     row = lax.broadcasted_iota(jnp.int32, shape, 0)
     inner = col_scale * (1.0 / (2 * REACH + 1))
-    for at in range(0, rows, STEP):
+    for at in range(first, last, STEP):
         outer = at in (0, rows - STEP)
         scale = col_scale / counted(row + at, rows).astype(F32) if outer else inner
-        box(at, scale, (upper_ref, lower_ref)[2 * at // rows])
-
-
-def add_kernel(start, ratio_ref, came_ref, sum_ref, send_ref):
+        box(at, scale)
+
+
+def add_kernel(ratio_ref, came_ref, sum_ref, send_ref):
     def part(at):
         span = pl.ds(at, STEP)
-        total = ratio_ref[pl.ds(at + start, STEP)] + came_ref[span].astype(F32)
+        total = ratio_ref[span] + came_ref[span].astype(F32)
         sum_ref[span] = total
         send_ref[span] = total.astype(BF16)
 
@@ -224,7 +227,7 @@
         for at in range(piece * size, piece * size + size, STEP):
             span = pl.ds(at, STEP)
             total = (sum_ref[span] + came_ref[span].astype(F32)) * (1.0 / dates)
-            out[span] = (means_ref[pl.ds(start + at, STEP)] * total).astype(BF16)
+            out[span] = (means_ref[span] * total).astype(BF16)
         copy(piece).start()
     for piece in range(pieces):
         copy(piece).wait()
@@ -257,7 +260,12 @@
     wide = jax.ShapeDtypeStruct(full, F32)
     thin = jax.ShapeDtypeStruct(full, BF16)
 
-    early = 2 if relay else 1
+    early = 3 if relay else 1
+    slots = [s for s in range(chips) if s != early]
+    cut = rows * CUT // 16 // STEP * STEP
+    pieces = (cut + STEP, rows - cut - STEP) if relay else (rows,)
+    starts = (0, cut + STEP)
+    piece_shapes = tuple(jax.ShapeDtypeStruct((size, subs, LANES), BF16) for size in pieces)
     canvases = 4 * rows * subs * LANES * chips
     early_out, other, own = call(
         functools.partial(place_kernel, relay, chips, early),
@@ -276,76 +284,69 @@
     partner = [(t, t ^ 1) for t in range(tiles)]
     early_came = permute(early_out, "tile", partner)
     came = permute(other, "tile", partner)
-    early_send = call(functools.partial(merge_early_kernel, early), thin, (own, early_came))
+    early_sends = call(functools.partial(merge_early_kernel, early), piece_shapes, (own, early_came))
 
     def along(array, moves):
         return permute(array, "tile", [(2 * a + core, 2 * b + core) for a, b in moves for core in range(2)])
 
-    ordered = [s for s in range(chips) if s != early]
     if relay:
-        first = along(early_send, [(0, 1), (3, 2), (1, 3), (2, 0)])
+        passing = [along(send, [(c, c ^ 1) for c in range(chips)]) for send in early_sends]
+        split = (len(pieces), 1)
+        outs = piece_shapes + (thin,)
     else:
-        first = along(early_send, [(c, (c + early) % chips) for c in range(chips)])
+        arrived = [[along(early_sends[0], [(c, (c + early) % chips) for c in range(chips)])]]
+        split = (1,) * (chips - 2)
+        outs = (thin,) * (chips - 2)
     keep, *sends = call(
-        functools.partial(merge_kernel, ordered),
-        (wide,) + (thin,) * (chips - 2),
-        (own, floor, came),
-        mib=(2 * canvases >> 20) + 4,
+        functools.partial(merge_kernel, slots, split), (wide,) + outs, (own, floor, came), mib=(2 * canvases >> 20) + 4
     )
     if relay:
-        near_send, far_send = sends
-        direct = along(far_send, [(0, 3), (3, 0), (1, 1), (2, 2)])
-        near = along(near_send, [(0, 1), (1, 0), (2, 3), (3, 2)])
-        passing = call(relay_kernel, thin, (far_send, first))
-        passed = along(passing, [(1, 2), (2, 1), (0, 0), (3, 3)])
-        arrived = [first, direct, passed, near]
+        *near_sends, far_send = sends
+        far, near = [], []
+        for i, passed in enumerate(passing):
+            send = call(functools.partial(relay_kernel, starts[i]), piece_shapes[i], (far_send, passed))
+            far.append(along(send, [(c, c ^ 2) for c in range(chips)]))
+            near.append(along(near_sends[i], [(c, c ^ 1) for c in range(chips)]))
+        arrived = [far, near]
     else:
-        arrived = [first]
-        for shift, send in zip(ordered[1:], sends):
-            arrived.append(along(send, [(c, (c + shift) % chips) for c in range(chips)]))
-
-    half = (rows // 2, subs, LANES)
-    wide_half, thin_half = jax.ShapeDtypeStruct(half, F32), jax.ShapeDtypeStruct(half, BF16)
-    means, ratio, *sends = call(
-        functools.partial(box_kernel, relay, pols),
-        (wide, wide, thin_half, thin_half),
-        (keep, *arrived),
-        mib=8 if relay else 16,
-        scratch=[pltpu.VMEM((rows + 2 * STEP, subs, LANES), F32)],
-    )
+        for shift, send in zip(slots[1:], sends):
+            arrived.append([along(send, [(c, (c + shift) % chips) for c in range(chips)])])
 
     bits = [1 << b for b in range(dates.bit_length() - 1)]
-    starts = (0, rows // 2)
-    totals = [ratio, ratio]
+    swaps = []
     for step in range(len(bits)):
-        came = []
-        for side in range(2):
-            pairs = []
-            for d in range(dates):
-                for t in range(tiles):
-                    bit = bits[step] if (t + side) % 2 == 0 else bits[-1 - step]
-                    pairs.append((d * tiles + t, (d ^ bit) * tiles + t))
-            came.append(permute(sends[side], ("date", "tile"), pairs))
-        if step + 1 < len(bits):
-            for side in range(2):
-                totals[side], sends[side] = call(
-                    functools.partial(add_kernel, starts[side] if step == 0 else 0),
-                    (wide_half, thin_half),
-                    (totals[side], came[side]),
-                    mib=4,
-                )
+        swaps.append([])
+        for d in range(dates):
+            for t in range(tiles):
+                bit = bits[-1 - step] if t % 2 else bits[step]
+                swaps[step].append((d * tiles + t, (d ^ bit) * tiles + t))
+
     out = None
-    for side in range(2):
-        ins = (means, totals[side], came[side]) + (() if out is None else (out,))
+    for first, last in ((0, cut), (cut, rows)):
+        shape = (last - first, subs, LANES)
+        wide_part, thin_part = jax.ShapeDtypeStruct(shape, F32), jax.ShapeDtypeStruct(shape, BF16)
+        used = [group[: 1 if last + STEP <= pieces[0] else None] for group in arrived]
+        means, total, send = call(
+            functools.partial(box_kernel, tuple(map(len, used)), pols, first, last),
+            (wide_part, wide_part, thin_part),
+            (keep, *(piece for group in used for piece in group)),
+            mib=8 if relay else 16,
+            scratch=[pltpu.VMEM((last - first + 2 * STEP, subs, LANES), F32)],
+        )
+        for step, pairs in enumerate(swaps):
+            came = permute(send, ("date", "tile"), pairs)
+            if step + 1 < len(swaps):
+                total, send = call(add_kernel, (wide_part, thin_part), (total, came), mib=4)
+        ins = (means, total, came) + (() if out is None else (out,))
         out = call(
-            functools.partial(scale_kernel, float(dates), starts[side]),
+            functools.partial(scale_kernel, float(dates), first),
             thin,
             ins,
             specs=[VMEM] * 3 + [HBM] * (len(ins) - 3),
             out_specs=HBM,
             aliases={3: 0} if len(ins) > 3 else {},
             mib=4,
-            scratch=[pltpu.VMEM(half, BF16), pltpu.SemaphoreType.DMA((2,))],
+            scratch=[pltpu.VMEM(shape, BF16), pltpu.SemaphoreType.DMA((2,))],
         )
     return unpack(out, pols)[None]
 

time: 46.6 us -> 38.7 us (0.83)
  waiting for transfers between devices: 23.5 us -> 16.6 us
  Pallas kernels: 5.62 us -> 5.03 us
    ppermute x10 -> x12, waiting for transfers between devices: 23.5 us -> 16.6 us  [permute(): return lax.ppermute(array, axes, pairs)]
    pallas_call x9 -> x11, Pallas kernels: 5.62 us -> 5.03 us  [call(): pl.pallas_call(kernel, out_shape=outs, in_specs=specs or [VMEM] * len(ins...]
    ppermute x10 -> x12, starting transfers between devices: 17.2 us -> 16.9 us  [permute(): return lax.ppermute(array, axes, pairs)]
  transfers between devices with their start and end apart: 10 -> 12, of which waited for: 7 -> 7; matrix products, arithmetic and copies ran while one was open for 0% -> 0% of each run, Pallas kernels for 2% -> 6%
where the time goes in v1:
time: 38.7 us; the launch traced here: 38.6 us
  starting transfers between devices  16.9 us (44%)
  waiting for transfers between devices  16.6 us (43%)
  Pallas kernels  5.03 us (13%)
    ppermute x12, starting transfers between devices, permute(): return lax.ppermute(array, axes, pairs)  16.9 us
    ppermute x12, waiting for transfers between devices, permute(): return lax.ppermute(array, axes, pairs)  16.6 us
    pallas_call x11, Pallas kernels, call(): pl.pallas_call(kernel, out_shape=outs, in_specs=specs or [VMEM] * len(ins...  5.03 us
  transfers between devices with their start and end apart: 12, of which 7 were waited for; matrix products, arithmetic and copies ran while one was open for 0% of the time, Pallas kernels for 6%

profile of v1, /device:TPU:0, one launch (start us, length us, event | category | flops | bytes accessed | tf_op | source)
XLA Modules:
  0.0 38.6 jit_solution(1320301737626568545)
XLA Ops:
  0.0 0.0 copy-start
  0.0 2.1 %shard_map.46 = (bf16[128,8,128]{2,1,0:T(8,128)(2,1)S(1)}, bf16[3,128,8,128]{3,2,1,0:T(8,128)(2,1)S(1)}, f32[4,128,8,128]{3,2,1,0:T(8,128)S(1)}) custom-call(s32[16]{0:T(128)} %bitcast.18, s32[16]{0:T(128)} %lead_hbm.1, bf16[16,64,8,128]{3,2,1,0:T(8,128)(2,1)} %bitcast.17), custom_call_target="tpu_custom_call" | custom-call | tf_op jit(solution)/shard_map/pallas_call | solution.py:237
  2.1 0.6 %collective-permute-start = (bf16[3,128,8,128]{3,2,1,0:T(8,128)(2,1)S(1)}, bf16[3,128,8,128]{3,2,1,0:T(8,128)(2,1)S(1)}, u32[]{:S(2)}, u32[]{:S(2)}) collective-permute-start(bf16[3,128,8,128]{3,2,1,0:T(8,128)(2,1)S(1)} %get-tuple-element.25), channel_id=1, source_target_pairs={{0,1},{1,0},{2,3},{3,2},{4,5},{5,4},{6,7},{7,6},{8,9},{9,8},{10,11... | collective-permute-start | bytes 2359304 | tf_op jit(solution)/shard_map/ppermute | solution.py:249
  2.7 0.1 collective-permute-start.1
  2.7 2.2 %collective-permute-done.1.came_ref = bf16[128,8,128]{2,1,0:T(8,128)(2,1)S(1)} collective-permute-done((bf16[128,8,128]{2,1,0:T(8,128)(2,1)S(1)}, bf16[128,8,128]{2,1,0:T(8,128)(2,1)S(1)}, u32[]{:S(2)}, u32[]{:S(2)}) %collective-permute-start.1) | collective-permute-done | bytes 262176 | tf_op jit(solution)/shard_map/ppermute | solution.py:249
  5.0 3.0 %collective-permute-start.2 = (bf16[72,8,128]{2,1,0:T(8,128)(2,1)S(1)}, bf16[72,8,128]{2,1,0:T(8,128)(2,1)S(1)}, u32[]{:S(2)}, u32[]{:S(2)}) collective-permute-start(bf16[72,8,128]{2,1,0:T(8,128)(2,1)S(1)} %get-tuple-element.29), channel_id=1, source_target_pairs={{0,2},{1,3},{2,0},{3,1},{4,6},{5,7},{6,4},{7,5},{8,10},{9,11},{10,... | collective-permute-start | bytes 442376 | tf_op jit(solution)/shard_map/ppermute | solution.py:249
  8.0 0.1 collective-permute-start.4
  8.1 0.0 collective-permute-done.came_ref
  8.1 0.0 copy-done
  8.1 0.1 shard_map.47
  8.2 2.0 %collective-permute-start.6 = (bf16[72,8,128]{2,1,0:T(8,128)(2,1)S(1)}, bf16[72,8,128]{2,1,0:T(8,128)(2,1)S(1)}, u32[]{:S(2)}, u32[]{:S(2)}) collective-permute-start(bf16[72,8,128]{2,1,0:T(8,128)(2,1)S(1)} %get-tuple-element.31), channel_id=1, source_target_pairs={{0,2},{1,3},{2,0},{3,1},{4,6},{5,7},{6,4},{7,5},{8,10},{9,11},{10,... | collective-permute-start | bytes 442376 | tf_op jit(solution)/shard_map/ppermute | solution.py:249
  10.2 2.5 %collective-permute-done.2.passing_ref = bf16[72,8,128]{2,1,0:T(8,128)(2,1)S(1)} collective-permute-done((bf16[72,8,128]{2,1,0:T(8,128)(2,1)S(1)}, bf16[72,8,128]{2,1,0:T(8,128)(2,1)S(1)}, u32[]{:S(2)}, u32[]{:S(2)}) %collective-permute-start.2) | collective-permute-done | bytes 147488 | tf_op jit(solution)/shard_map/ppermute | solution.py:249
  12.7 3.1 %collective-permute-start.3 = (bf16[72,8,128]{2,1,0:T(8,128)(2,1)S(1)}, bf16[72,8,128]{2,1,0:T(8,128)(2,1)S(1)}, u32[]{:S(2)}, u32[]{:S(2)}) collective-permute-start(bf16[72,8,128]{2,1,0:T(8,128)(2,1)S(1)} %shard_map.49), channel_id=1, source_target_pairs={{0,4},{1,5},{2,6},{3,7},{4,0},{5,1},{6,2},{7,3},{8,12},{9,13},{10,... | collective-permute-start | bytes 442376 | tf_op jit(solution)/shard_map/ppermute | solution.py:249
  15.8 1.6 %collective-permute-start.7 = (bf16[56,8,128]{2,1,0:T(8,128)(2,1)S(1)}, bf16[56,8,128]{2,1,0:T(8,128)(2,1)S(1)}, u32[]{:S(2)}, u32[]{:S(2)}) collective-permute-start(bf16[56,8,128]{2,1,0:T(8,128)(2,1)S(1)} %get-tuple-element.32), channel_id=1, source_target_pairs={{0,2},{1,3},{2,0},{3,1},{4,6},{5,7},{6,4},{7,5},{8,10},{9,11},{10,... | collective-permute-start | bytes 344072 | tf_op jit(solution)/shard_map/ppermute | solution.py:249
  17.4 0.0 collective-permute-done.4.passing_ref
  17.4 0.8 %collective-permute-start.5 = (bf16[56,8,128]{2,1,0:T(8,128)(2,1)S(1)}, bf16[56,8,128]{2,1,0:T(8,128)(2,1)S(1)}, u32[]{:S(2)}, u32[]{:S(2)}) collective-permute-start(bf16[56,8,128]{2,1,0:T(8,128)(2,1)S(1)} %shard_map.50), channel_id=1, source_target_pairs={{0,4},{1,5},{2,6},{3,7},{4,0},{5,1},{6,2},{7,3},{8,12},{9,13},{10,... | collective-permute-start | bytes 344072 | tf_op jit(solution)/shard_map/ppermute | solution.py:249
  18.3 4.4 %collective-permute-done.6.refs_2_.refs_1_ = bf16[72,8,128]{2,1,0:T(8,128)(2,1)S(1)} collective-permute-done((bf16[72,8,128]{2,1,0:T(8,128)(2,1)S(1)}, bf16[72,8,128]{2,1,0:T(8,128)(2,1)S(1)}, u32[]{:S(2)}, u32[]{:S(2)}) %collective-permute-start.6) | collective-permute-done | bytes 147488 | tf_op jit(solution)/shard_map/ppermute | solution.py:249
  22.7 0.0 collective-permute-done.3.refs_0_
  22.7 0.6 %shard_map.53 = (f32[64,8,128]{2,1,0:T(8,128)S(1)}, f32[64,8,128]{2,1,0:T(8,128)S(1)}, bf16[64,8,128]{2,1,0:T(8,128)(2,1)S(1)}) custom-call(f32[128,8,128]{2,1,0:T(8,128)S(1)} %get-tuple-element.26.keep_ref, bf16[72,8,128]{2,1,0:T(8,128)(2,1)S(1)} %collective-permute-done.3.refs_0_, bf16[72,8,128]{2,1,0:T(8,128)(2,1)S(1)} %collective-permute-done.6.refs_2_.refs_1_), custom_call_target="tpu_custom_call" | custom-call | tf_op jit(solution)/shard_map/pallas_call | solution.py:237
  23.3 1.7 %collective-permute-start.10 = (bf16[64,8,128]{2,1,0:T(8,128)(2,1)S(1)}, bf16[64,8,128]{2,1,0:T(8,128)(2,1)S(1)}, u32[]{:S(2)}, u32[]{:S(2)}) collective-permute-start(bf16[64,8,128]{2,1,0:T(8,128)(2,1)S(1)} %get-tuple-element.40), channel_id=1, source_target_pairs={{0,8},{1,17},{2,10},{3,19},{4,12},{5,21},{6,14},{7,23},{8,0},{9,25... | collective-permute-start | bytes 393224 | tf_op jit(solution)/shard_map/ppermute | solution.py:249
  25.0 0.8 %collective-permute-done.7.refs_3_ = bf16[56,8,128]{2,1,0:T(8,128)(2,1)S(1)} collective-permute-done((bf16[56,8,128]{2,1,0:T(8,128)(2,1)S(1)}, bf16[56,8,128]{2,1,0:T(8,128)(2,1)S(1)}, u32[]{:S(2)}, u32[]{:S(2)}) %collective-permute-start.7) | collective-permute-done | bytes 114720 | tf_op jit(solution)/shard_map/ppermute | solution.py:249
  25.8 0.0 collective-permute-done.5.refs_1_
  25.8 0.6 %shard_map.51 = (f32[64,8,128]{2,1,0:T(8,128)S(1)}, f32[64,8,128]{2,1,0:T(8,128)S(1)}, bf16[64,8,128]{2,1,0:T(8,128)(2,1)S(1)}) custom-call(f32[128,8,128]{2,1,0:T(8,128)S(1)} %get-tuple-element.26.keep_ref, bf16[72,8,128]{2,1,0:T(8,128)(2,1)S(1)} %collective-permute-done.3.refs_0_, bf16[56,8,128]{2,1,0:T(8,128)(2,1)S(1)} %collective-permute-done.5.refs_1_, ...), custom_call_target="tpu_custom_call" | custom-call | tf_op jit(solution)/shard_map/pallas_call | solution.py:237
  26.5 1.7 %collective-permute-start.8 = (bf16[64,8,128]{2,1,0:T(8,128)(2,1)S(1)}, bf16[64,8,128]{2,1,0:T(8,128)(2,1)S(1)}, u32[]{:S(2)}, u32[]{:S(2)}) collective-permute-start(bf16[64,8,128]{2,1,0:T(8,128)(2,1)S(1)} %get-tuple-element.35), channel_id=1, source_target_pairs={{0,8},{1,17},{2,10},{3,19},{4,12},{5,21},{6,14},{7,23},{8,0},{9,25... | collective-permute-start | bytes 393224 | tf_op jit(solution)/shard_map/ppermute | solution.py:249
  28.2 0.2 collective-permute-done.10.came_ref
  28.4 1.7 %collective-permute-start.11 = (bf16[64,8,128]{2,1,0:T(8,128)(2,1)S(1)}, bf16[64,8,128]{2,1,0:T(8,128)(2,1)S(1)}, u32[]{:S(2)}, u32[]{:S(2)}) collective-permute-start(bf16[64,8,128]{2,1,0:T(8,128)(2,1)S(1)} %get-tuple-element.42), channel_id=1, source_target_pairs={{0,16},{1,9},{2,18},{3,11},{4,20},{5,13},{6,22},{7,15},{8,24},{9,1... | collective-permute-start | bytes 393224 | tf_op jit(solution)/shard_map/ppermute | solution.py:249
  30.1 2.7 %collective-permute-done.8.came_ref = bf16[64,8,128]{2,1,0:T(8,128)(2,1)S(1)} collective-permute-done((bf16[64,8,128]{2,1,0:T(8,128)(2,1)S(1)}, bf16[64,8,128]{2,1,0:T(8,128)(2,1)S(1)}, u32[]{:S(2)}, u32[]{:S(2)}) %collective-permute-start.8) | collective-permute-done | bytes 131104 | tf_op jit(solution)/shard_map/ppermute | solution.py:249
  32.9 0.6 %collective-permute-start.9 = (bf16[64,8,128]{2,1,0:T(8,128)(2,1)S(1)}, bf16[64,8,128]{2,1,0:T(8,128)(2,1)S(1)}, u32[]{:S(2)}, u32[]{:S(2)}) collective-permute-start(bf16[64,8,128]{2,1,0:T(8,128)(2,1)S(1)} %get-tuple-element.37), channel_id=1, source_target_pairs={{0,16},{1,9},{2,18},{3,11},{4,20},{5,13},{6,22},{7,15},{8,24},{9,1... | collective-permute-start | bytes 393224 | tf_op jit(solution)/shard_map/ppermute | solution.py:249
  33.4 0.0 collective-permute-done.11.came_ref
  33.4 0.7 %shard_map.55.refs_0_ = bf16[128,8,128]{2,1,0:T(8,128)(2,1)} custom-call(f32[64,8,128]{2,1,0:T(8,128)S(1)} %get-tuple-element.38.means_ref, f32[64,8,128]{2,1,0:T(8,128)S(1)} %get-tuple-element.41.sum_ref, bf16[64,8,128]{2,1,0:T(8,128)(2,1)S(1)} %collective-permute-done.11.came_ref), custom_call_target="tpu_custom_call" | custom-call | tf_op jit(solution)/shard_map/pallas_call | solution.py:237
  34.1 3.8 %collective-permute-done.9.came_ref = bf16[64,8,128]{2,1,0:T(8,128)(2,1)S(1)} collective-permute-done((bf16[64,8,128]{2,1,0:T(8,128)(2,1)S(1)}, bf16[64,8,128]{2,1,0:T(8,128)(2,1)S(1)}, u32[]{:S(2)}, u32[]{:S(2)}) %collective-permute-start.9) | collective-permute-done | bytes 131104 | tf_op jit(solution)/shard_map/ppermute | solution.py:249
  37.9 0.7 %shard_map.56 = bf16[128,8,128]{2,1,0:T(8,128)(2,1)} custom-call(f32[64,8,128]{2,1,0:T(8,128)S(1)} %get-tuple-element.33.means_ref, f32[64,8,128]{2,1,0:T(8,128)S(1)} %get-tuple-element.36.sum_ref, bf16[64,8,128]{2,1,0:T(8,128)(2,1)S(1)} %collective-permute-done.9.came_ref, bf16[128,8,128]{2,1,0:T(8,128)(2,1)} %shard_map.55.refs_0_), custom_call_target="tpu_custom_call", output_to_operand_aliasing={{}: (3, {})} | custom-call | tf_op jit(solution)/shard_map/pallas_call | solution.py:237
  (5 shorter events, 0.2 us)
Async XLA Ops:
  0.0 8.1 %copy-start = (f32[1,128,2,512]{3,2,1,0:T(2,128)S(1)}, f32[1,128,2,512]{3,2,1,0:T(2,128)}, u32[]{:S(2)}) copy-start(f32[1,128,2,512]{3,2,1,0:T(2,128)} %param.7) | copy-start | bytes 1572868
  2.1 6.0 %collective-permute-start = (bf16[3,128,8,128]{3,2,1,0:T(8,128)(2,1)S(1)}, bf16[3,128,8,128]{3,2,1,0:T(8,128)(2,1)S(1)}, u32[]{:S(2)}, u32[]{:S(2)}) collective-permute-start(bf16[3,128,8,128]{3,2,1,0:T(8,128)(2,1)S(1)} %get-tuple-element.25), channel_id=1, source_target_pairs={{0,1},{1,0},{2,3},{3,2},{4,5},{5,4},{6,7},{7,6},{8,9},{9,8},{10,11... | collective-permute-start | bytes 2359304 | tf_op jit(solution)/shard_map/ppermute | solution.py:249
  2.7 2.3 %collective-permute-start.1 = (bf16[128,8,128]{2,1,0:T(8,128)(2,1)S(1)}, bf16[128,8,128]{2,1,0:T(8,128)(2,1)S(1)}, u32[]{:S(2)}, u32[]{:S(2)}) collective-permute-start(bf16[128,8,128]{2,1,0:T(8,128)(2,1)S(1)} %get-tuple-element.28), channel_id=1, source_target_pairs={{0,1},{1,0},{2,3},{3,2},{4,5},{5,4},{6,7},{7,6},{8,9},{9,8},{10,11... | collective-permute-start | bytes 786440 | tf_op jit(solution)/shard_map/ppermute | solution.py:249
  5.0 7.7 %collective-permute-start.2 = (bf16[72,8,128]{2,1,0:T(8,128)(2,1)S(1)}, bf16[72,8,128]{2,1,0:T(8,128)(2,1)S(1)}, u32[]{:S(2)}, u32[]{:S(2)}) collective-permute-start(bf16[72,8,128]{2,1,0:T(8,128)(2,1)S(1)} %get-tuple-element.29), channel_id=1, source_target_pairs={{0,2},{1,3},{2,0},{3,1},{4,6},{5,7},{6,4},{7,5},{8,10},{9,11},{10,... | collective-permute-start | bytes 442376 | tf_op jit(solution)/shard_map/ppermute | solution.py:249
  8.0 9.4 %collective-permute-start.4 = (bf16[56,8,128]{2,1,0:T(8,128)(2,1)S(1)}, bf16[56,8,128]{2,1,0:T(8,128)(2,1)S(1)}, u32[]{:S(2)}, u32[]{:S(2)}) collective-permute-start(bf16[56,8,128]{2,1,0:T(8,128)(2,1)S(1)} %get-tuple-element.30), channel_id=1, source_target_pairs={{0,2},{1,3},{2,0},{3,1},{4,6},{5,7},{6,4},{7,5},{8,10},{9,11},{10,... | collective-permute-start | bytes 344072 | tf_op jit(solution)/shard_map/ppermute | solution.py:249
  8.2 14.5 %collective-permute-start.6 = (bf16[72,8,128]{2,1,0:T(8,128)(2,1)S(1)}, bf16[72,8,128]{2,1,0:T(8,128)(2,1)S(1)}, u32[]{:S(2)}, u32[]{:S(2)}) collective-permute-start(bf16[72,8,128]{2,1,0:T(8,128)(2,1)S(1)} %get-tuple-element.31), channel_id=1, source_target_pairs={{0,2},{1,3},{2,0},{3,1},{4,6},{5,7},{6,4},{7,5},{8,10},{9,11},{10,... | collective-permute-start | bytes 442376 | tf_op jit(solution)/shard_map/ppermute | solution.py:249
  12.7 10.0 %collective-permute-start.3 = (bf16[72,8,128]{2,1,0:T(8,128)(2,1)S(1)}, bf16[72,8,128]{2,1,0:T(8,128)(2,1)S(1)}, u32[]{:S(2)}, u32[]{:S(2)}) collective-permute-start(bf16[72,8,128]{2,1,0:T(8,128)(2,1)S(1)} %shard_map.49), channel_id=1, source_target_pairs={{0,4},{1,5},{2,6},{3,7},{4,0},{5,1},{6,2},{7,3},{8,12},{9,13},{10,... | collective-permute-start | bytes 442376 | tf_op jit(solution)/shard_map/ppermute | solution.py:249
  15.8 10.0 %collective-permute-start.7 = (bf16[56,8,128]{2,1,0:T(8,128)(2,1)S(1)}, bf16[56,8,128]{2,1,0:T(8,128)(2,1)S(1)}, u32[]{:S(2)}, u32[]{:S(2)}) collective-permute-start(bf16[56,8,128]{2,1,0:T(8,128)(2,1)S(1)} %get-tuple-element.32), channel_id=1, source_target_pairs={{0,2},{1,3},{2,0},{3,1},{4,6},{5,7},{6,4},{7,5},{8,10},{9,11},{10,... | collective-permute-start | bytes 344072 | tf_op jit(solution)/shard_map/ppermute | solution.py:249
  17.4 8.4 %collective-permute-start.5 = (bf16[56,8,128]{2,1,0:T(8,128)(2,1)S(1)}, bf16[56,8,128]{2,1,0:T(8,128)(2,1)S(1)}, u32[]{:S(2)}, u32[]{:S(2)}) collective-permute-start(bf16[56,8,128]{2,1,0:T(8,128)(2,1)S(1)} %shard_map.50), channel_id=1, source_target_pairs={{0,4},{1,5},{2,6},{3,7},{4,0},{5,1},{6,2},{7,3},{8,12},{9,13},{10,... | collective-permute-start | bytes 344072 | tf_op jit(solution)/shard_map/ppermute | solution.py:249
  23.3 5.0 %collective-permute-start.10 = (bf16[64,8,128]{2,1,0:T(8,128)(2,1)S(1)}, bf16[64,8,128]{2,1,0:T(8,128)(2,1)S(1)}, u32[]{:S(2)}, u32[]{:S(2)}) collective-permute-start(bf16[64,8,128]{2,1,0:T(8,128)(2,1)S(1)} %get-tuple-element.40), channel_id=1, source_target_pairs={{0,8},{1,17},{2,10},{3,19},{4,12},{5,21},{6,14},{7,23},{8,0},{9,25... | collective-permute-start | bytes 393224 | tf_op jit(solution)/shard_map/ppermute | solution.py:249
  26.5 6.4 %collective-permute-start.8 = (bf16[64,8,128]{2,1,0:T(8,128)(2,1)S(1)}, bf16[64,8,128]{2,1,0:T(8,128)(2,1)S(1)}, u32[]{:S(2)}, u32[]{:S(2)}) collective-permute-start(bf16[64,8,128]{2,1,0:T(8,128)(2,1)S(1)} %get-tuple-element.35), channel_id=1, source_target_pairs={{0,8},{1,17},{2,10},{3,19},{4,12},{5,21},{6,14},{7,23},{8,0},{9,25... | collective-permute-start | bytes 393224 | tf_op jit(solution)/shard_map/ppermute | solution.py:249
  28.4 5.1 %collective-permute-start.11 = (bf16[64,8,128]{2,1,0:T(8,128)(2,1)S(1)}, bf16[64,8,128]{2,1,0:T(8,128)(2,1)S(1)}, u32[]{:S(2)}, u32[]{:S(2)}) collective-permute-start(bf16[64,8,128]{2,1,0:T(8,128)(2,1)S(1)} %get-tuple-element.42), channel_id=1, source_target_pairs={{0,16},{1,9},{2,18},{3,11},{4,20},{5,13},{6,22},{7,15},{8,24},{9,1... | collective-permute-start | bytes 393224 | tf_op jit(solution)/shard_map/ppermute | solution.py:249
  32.9 5.0 %collective-permute-start.9 = (bf16[64,8,128]{2,1,0:T(8,128)(2,1)S(1)}, bf16[64,8,128]{2,1,0:T(8,128)(2,1)S(1)}, u32[]{:S(2)}, u32[]{:S(2)}) collective-permute-start(bf16[64,8,128]{2,1,0:T(8,128)(2,1)S(1)} %get-tuple-element.37), channel_id=1, source_target_pairs={{0,16},{1,9},{2,18},{3,11},{4,20},{5,13},{6,22},{7,15},{8,24},{9,1... | collective-permute-start | bytes 393224 | tf_op jit(solution)/shard_map/ppermute | solution.py:249

commit v2 on v1

--- a/solution.py
+++ b/solution.py
@@ -135,7 +135,10 @@
                 keep_ref[span] = total + floor_ref[span]
 
 
-def relay_kernel(start, mine_ref, passing_ref, send_ref):
+def relay_kernel(start, mine_ref, passing_ref, *refs):
+    send_ref = refs[-1] if start else refs[0]
+    if not start:
+        refs[1][...] = jnp.zeros(refs[1].shape, BF16)
     for at in range(0, send_ref.shape[0], STEP):
         span = pl.ds(at, STEP)
         total = mine_ref[pl.ds(start + at, STEP)].astype(F32) + passing_ref[span].astype(F32)
@@ -303,26 +306,35 @@
     if relay:
         *near_sends, far_send = sends
         far, near = [], []
+        ready = jax.ShapeDtypeStruct((1, subs, LANES), BF16)
+        waits = ()
         for i, passed in enumerate(passing):
-            send = call(functools.partial(relay_kernel, starts[i]), piece_shapes[i], (far_send, passed))
+            send, *ready_out = call(
+                functools.partial(relay_kernel, starts[i]),
+                (piece_shapes[i],) + (ready,) * (i == 0),
+                (far_send, passed, *waits),
+            )
             far.append(along(send, [(c, c ^ 2) for c in range(chips)]))
             near.append(along(near_sends[i], [(c, c ^ 1) for c in range(chips)]))
+            if i == 0:
+                waits = (permute(ready_out[0], "tile", partner),)
         arrived = [far, near]
     else:
         for shift, send in zip(slots[1:], sends):
             arrived.append([along(send, [(c, (c + shift) % chips) for c in range(chips)])])
 
     bits = [1 << b for b in range(dates.bit_length() - 1)]
-    swaps = []
-    for step in range(len(bits)):
-        swaps.append([])
+
+    def across(step, part):
+        pairs = []
         for d in range(dates):
             for t in range(tiles):
-                bit = bits[-1 - step] if t % 2 else bits[step]
-                swaps[step].append((d * tiles + t, (d ^ bit) * tiles + t))
+                bit = bits[-1 - step] if (t + part) % 2 else bits[step]
+                pairs.append((d * tiles + t, (d ^ bit) * tiles + t))
+        return pairs
 
     out = None
-    for first, last in ((0, cut), (cut, rows)):
+    for part, (first, last) in enumerate(((0, cut), (cut, rows))):
         shape = (last - first, subs, LANES)
         wide_part, thin_part = jax.ShapeDtypeStruct(shape, F32), jax.ShapeDtypeStruct(shape, BF16)
         used = [group[: 1 if last + STEP <= pieces[0] else None] for group in arrived]
@@ -333,9 +345,9 @@
             mib=8 if relay else 16,
             scratch=[pltpu.VMEM((last - first + 2 * STEP, subs, LANES), F32)],
         )
-        for step, pairs in enumerate(swaps):
-            came = permute(send, ("date", "tile"), pairs)
-            if step + 1 < len(swaps):
+        for step in range(len(bits)):
+            came = permute(send, ("date", "tile"), across(step, part))
+            if step + 1 < len(bits):
                 total, send = call(add_kernel, (wide_part, thin_part), (total, came), mib=4)
         ins = (means, total, came) + (() if out is None else (out,))
         out = call(

time: 38.7 us -> 39.3 us (1.016)
  waiting for transfers between devices: 16.6 us -> 19.1 us
  starting transfers between devices: 16.9 us -> 15 us
    ppermute x12 -> x13, waiting for transfers between devices: 16.6 us -> 19.1 us  [permute(): return lax.ppermute(array, axes, pairs)]
    ppermute x12 -> x13, starting transfers between devices: 16.9 us -> 15 us  [permute(): return lax.ppermute(array, axes, pairs)]
  transfers between devices with their start and end apart: 12 -> 13, of which waited for: 7 -> 8; matrix products, arithmetic and copies ran while one was open for 0% -> 0% of each run, Pallas kernels for 6% -> 6%
where the time goes in v2:
time: 39.3 us; the launch traced here: 39.1 us
  waiting for transfers between devices  19.1 us (49%)
  starting transfers between devices  15 us (38%)
  Pallas kernels  5.03 us (13%)
    ppermute x13, waiting for transfers between devices, permute(): return lax.ppermute(array, axes, pairs)  19.1 us
    ppermute x13, starting transfers between devices, permute(): return lax.ppermute(array, axes, pairs)  15 us
    pallas_call x11, Pallas kernels, call(): pl.pallas_call(kernel, out_shape=outs, in_specs=specs or [VMEM] * len(ins...  5.03 us
  transfers between devices with their start and end apart: 13, of which 8 were waited for; matrix products, arithmetic and copies ran while one was open for 0% of the time, Pallas kernels for 6%

profile of v2, /device:TPU:0, one launch (start us, length us, event | category | flops | bytes accessed | tf_op | source)
XLA Modules:
  0.0 39.1 jit_solution(11266574329321977297)
XLA Ops:
  0.0 2.1 %shard_map.46 = (bf16[128,8,128]{2,1,0:T(8,128)(2,1)S(1)}, bf16[3,128,8,128]{3,2,1,0:T(8,128)(2,1)S(1)}, f32[4,128,8,128]{3,2,1,0:T(8,128)S(1)}) custom-call(s32[16]{0:T(128)} %bitcast.18, s32[16]{0:T(128)} %lead_hbm.1, bf16[16,64,8,128]{3,2,1,0:T(8,128)(2,1)} %bitcast.17), custom_call_target="tpu_custom_call" | custom-call | tf_op jit(solution)/shard_map/pallas_call | solution.py:240
  2.1 0.6 %collective-permute-start = (bf16[3,128,8,128]{3,2,1,0:T(8,128)(2,1)S(1)}, bf16[3,128,8,128]{3,2,1,0:T(8,128)(2,1)S(1)}, u32[]{:S(2)}, u32[]{:S(2)}) collective-permute-start(bf16[3,128,8,128]{3,2,1,0:T(8,128)(2,1)S(1)} %get-tuple-element.27), channel_id=1, source_target_pairs={{0,1},{1,0},{2,3},{3,2},{4,5},{5,4},{6,7},{7,6},{8,9},{9,8},{10,11... | collective-permute-start | bytes 2359304 | tf_op jit(solution)/shard_map/ppermute | solution.py:252
  2.7 0.1 collective-permute-start.1
  2.7 2.2 %collective-permute-done.1.came_ref = bf16[128,8,128]{2,1,0:T(8,128)(2,1)S(1)} collective-permute-done((bf16[128,8,128]{2,1,0:T(8,128)(2,1)S(1)}, bf16[128,8,128]{2,1,0:T(8,128)(2,1)S(1)}, u32[]{:S(2)}, u32[]{:S(2)}) %collective-permute-start.1) | collective-permute-done | bytes 262176 | tf_op jit(solution)/shard_map/ppermute | solution.py:252
  5.0 3.0 %collective-permute-start.2 = (bf16[72,8,128]{2,1,0:T(8,128)(2,1)S(1)}, bf16[72,8,128]{2,1,0:T(8,128)(2,1)S(1)}, u32[]{:S(2)}, u32[]{:S(2)}) collective-permute-start(bf16[72,8,128]{2,1,0:T(8,128)(2,1)S(1)} %get-tuple-element.31), channel_id=1, source_target_pairs={{0,2},{1,3},{2,0},{3,1},{4,6},{5,7},{6,4},{7,5},{8,10},{9,11},{10,... | collective-permute-start | bytes 442376 | tf_op jit(solution)/shard_map/ppermute | solution.py:252
  8.0 0.1 collective-permute-start.4
  8.1 0.0 collective-permute-done.came_ref
  8.1 0.1 shard_map.47
  8.2 4.5 %collective-permute-done.2.passing_ref = bf16[72,8,128]{2,1,0:T(8,128)(2,1)S(1)} collective-permute-done((bf16[72,8,128]{2,1,0:T(8,128)(2,1)S(1)}, bf16[72,8,128]{2,1,0:T(8,128)(2,1)S(1)}, u32[]{:S(2)}, u32[]{:S(2)}) %collective-permute-start.2) | collective-permute-done | bytes 147488 | tf_op jit(solution)/shard_map/ppermute | solution.py:252
  12.7 3.1 %collective-permute-start.3 = (bf16[72,8,128]{2,1,0:T(8,128)(2,1)S(1)}, bf16[72,8,128]{2,1,0:T(8,128)(2,1)S(1)}, u32[]{:S(2)}, u32[]{:S(2)}) collective-permute-start(bf16[72,8,128]{2,1,0:T(8,128)(2,1)S(1)} %get-tuple-element.32), channel_id=1, source_target_pairs={{0,4},{1,5},{2,6},{3,7},{4,0},{5,1},{6,2},{7,3},{8,12},{9,13},{10,... | collective-permute-start | bytes 442376 | tf_op jit(solution)/shard_map/ppermute | solution.py:252
  15.8 1.6 %collective-permute-start.7 = (bf16[72,8,128]{2,1,0:T(8,128)(2,1)S(1)}, bf16[72,8,128]{2,1,0:T(8,128)(2,1)S(1)}, u32[]{:S(2)}, u32[]{:S(2)}) collective-permute-start(bf16[72,8,128]{2,1,0:T(8,128)(2,1)S(1)} %get-tuple-element.35), channel_id=1, source_target_pairs={{0,2},{1,3},{2,0},{3,1},{4,6},{5,7},{6,4},{7,5},{8,10},{9,11},{10,... | collective-permute-start | bytes 442376 | tf_op jit(solution)/shard_map/ppermute | solution.py:252
  17.4 0.0 collective-permute-start.5
  17.4 0.5 %collective-permute-start.8 = (bf16[56,8,128]{2,1,0:T(8,128)(2,1)S(1)}, bf16[56,8,128]{2,1,0:T(8,128)(2,1)S(1)}, u32[]{:S(2)}, u32[]{:S(2)}) collective-permute-start(bf16[56,8,128]{2,1,0:T(8,128)(2,1)S(1)} %get-tuple-element.36), channel_id=1, source_target_pairs={{0,2},{1,3},{2,0},{3,1},{4,6},{5,7},{6,4},{7,5},{8,10},{9,11},{10,... | collective-permute-start | bytes 344072 | tf_op jit(solution)/shard_map/ppermute | solution.py:252
  17.9 0.0 collective-permute-done.4.passing_ref
  17.9 0.7 %collective-permute-done.5.refs_0_ = bf16[1,8,128]{2,1,0:T(8,128)(2,1)S(1)} collective-permute-done((bf16[1,8,128]{2,1,0:T(8,128)(2,1)S(1)}, bf16[1,8,128]{2,1,0:T(8,128)(2,1)S(1)}, u32[]{:S(2)}, u32[]{:S(2)}) %collective-permute-start.5) | collective-permute-done | bytes 2080 | tf_op jit(solution)/shard_map/ppermute | solution.py:252
  18.6 0.4 %collective-permute-start.6 = (bf16[56,8,128]{2,1,0:T(8,128)(2,1)S(1)}, bf16[56,8,128]{2,1,0:T(8,128)(2,1)S(1)}, u32[]{:S(2)}, u32[]{:S(2)}) collective-permute-start(bf16[56,8,128]{2,1,0:T(8,128)(2,1)S(1)} %shard_map.50), channel_id=1, source_target_pairs={{0,4},{1,5},{2,6},{3,7},{4,0},{5,1},{6,2},{7,3},{8,12},{9,13},{10,... | collective-permute-start | bytes 344072 | tf_op jit(solution)/shard_map/ppermute | solution.py:252
  19.0 2.4 %collective-permute-done.3.refs_0_ = bf16[72,8,128]{2,1,0:T(8,128)(2,1)S(1)} collective-permute-done((bf16[72,8,128]{2,1,0:T(8,128)(2,1)S(1)}, bf16[72,8,128]{2,1,0:T(8,128)(2,1)S(1)}, u32[]{:S(2)}, u32[]{:S(2)}) %collective-permute-start.3) | collective-permute-done | bytes 147488 | tf_op jit(solution)/shard_map/ppermute | solution.py:252
  21.4 3.6 %collective-permute-done.7.refs_2_.refs_1_ = bf16[72,8,128]{2,1,0:T(8,128)(2,1)S(1)} collective-permute-done((bf16[72,8,128]{2,1,0:T(8,128)(2,1)S(1)}, bf16[72,8,128]{2,1,0:T(8,128)(2,1)S(1)}, u32[]{:S(2)}, u32[]{:S(2)}) %collective-permute-start.7) | collective-permute-done | bytes 147488 | tf_op jit(solution)/shard_map/ppermute | solution.py:252
  25.0 0.6 %shard_map.53 = (f32[64,8,128]{2,1,0:T(8,128)S(1)}, f32[64,8,128]{2,1,0:T(8,128)S(1)}, bf16[64,8,128]{2,1,0:T(8,128)(2,1)S(1)}) custom-call(f32[128,8,128]{2,1,0:T(8,128)S(1)} %get-tuple-element.28.keep_ref, bf16[72,8,128]{2,1,0:T(8,128)(2,1)S(1)} %collective-permute-done.3.refs_0_, bf16[72,8,128]{2,1,0:T(8,128)(2,1)S(1)} %collective-permute-done.7.refs_2_.refs_1_), custom_call_target="tpu_custom_call" | custom-call | tf_op jit(solution)/shard_map/pallas_call | solution.py:240
  25.6 1.3 %collective-permute-start.11 = (bf16[64,8,128]{2,1,0:T(8,128)(2,1)S(1)}, bf16[64,8,128]{2,1,0:T(8,128)(2,1)S(1)}, u32[]{:S(2)}, u32[]{:S(2)}) collective-permute-start(bf16[64,8,128]{2,1,0:T(8,128)(2,1)S(1)} %get-tuple-element.44), channel_id=1, source_target_pairs={{0,8},{1,17},{2,10},{3,19},{4,12},{5,21},{6,14},{7,23},{8,0},{9,25... | collective-permute-start | bytes 393224 | tf_op jit(solution)/shard_map/ppermute | solution.py:252
  26.9 0.0 collective-permute-done.8.refs_3_
  26.9 0.0 collective-permute-done.6.refs_1_
  26.9 0.6 %shard_map.51 = (f32[64,8,128]{2,1,0:T(8,128)S(1)}, f32[64,8,128]{2,1,0:T(8,128)S(1)}, bf16[64,8,128]{2,1,0:T(8,128)(2,1)S(1)}) custom-call(f32[128,8,128]{2,1,0:T(8,128)S(1)} %get-tuple-element.28.keep_ref, bf16[72,8,128]{2,1,0:T(8,128)(2,1)S(1)} %collective-permute-done.3.refs_0_, bf16[56,8,128]{2,1,0:T(8,128)(2,1)S(1)} %collective-permute-done.6.refs_1_, ...), custom_call_target="tpu_custom_call" | custom-call | tf_op jit(solution)/shard_map/pallas_call | solution.py:240
  27.5 1.6 %collective-permute-start.9 = (bf16[64,8,128]{2,1,0:T(8,128)(2,1)S(1)}, bf16[64,8,128]{2,1,0:T(8,128)(2,1)S(1)}, u32[]{:S(2)}, u32[]{:S(2)}) collective-permute-start(bf16[64,8,128]{2,1,0:T(8,128)(2,1)S(1)} %get-tuple-element.39), channel_id=1, source_target_pairs={{0,16},{1,9},{2,18},{3,11},{4,20},{5,13},{6,22},{7,15},{8,24},{9,1... | collective-permute-start | bytes 393224 | tf_op jit(solution)/shard_map/ppermute | solution.py:252
  29.1 2.9 %collective-permute-done.11.came_ref = bf16[64,8,128]{2,1,0:T(8,128)(2,1)S(1)} collective-permute-done((bf16[64,8,128]{2,1,0:T(8,128)(2,1)S(1)}, bf16[64,8,128]{2,1,0:T(8,128)(2,1)S(1)}, u32[]{:S(2)}, u32[]{:S(2)}) %collective-permute-start.11) | collective-permute-done | bytes 131104 | tf_op jit(solution)/shard_map/ppermute | solution.py:252
  32.1 1.3 %collective-permute-start.12 = (bf16[64,8,128]{2,1,0:T(8,128)(2,1)S(1)}, bf16[64,8,128]{2,1,0:T(8,128)(2,1)S(1)}, u32[]{:S(2)}, u32[]{:S(2)}) collective-permute-start(bf16[64,8,128]{2,1,0:T(8,128)(2,1)S(1)} %get-tuple-element.46), channel_id=1, source_target_pairs={{0,16},{1,9},{2,18},{3,11},{4,20},{5,13},{6,22},{7,15},{8,24},{9,1... | collective-permute-start | bytes 393224 | tf_op jit(solution)/shard_map/ppermute | solution.py:252
  33.4 0.0 collective-permute-done.9.came_ref
  33.4 1.6 %collective-permute-start.10 = (bf16[64,8,128]{2,1,0:T(8,128)(2,1)S(1)}, bf16[64,8,128]{2,1,0:T(8,128)(2,1)S(1)}, u32[]{:S(2)}, u32[]{:S(2)}) collective-permute-start(bf16[64,8,128]{2,1,0:T(8,128)(2,1)S(1)} %get-tuple-element.41), channel_id=1, source_target_pairs={{0,8},{1,17},{2,10},{3,19},{4,12},{5,21},{6,14},{7,23},{8,0},{9,25... | collective-permute-start | bytes 393224 | tf_op jit(solution)/shard_map/ppermute | solution.py:252
  35.0 2.6 %collective-permute-done.12.came_ref = bf16[64,8,128]{2,1,0:T(8,128)(2,1)S(1)} collective-permute-done((bf16[64,8,128]{2,1,0:T(8,128)(2,1)S(1)}, bf16[64,8,128]{2,1,0:T(8,128)(2,1)S(1)}, u32[]{:S(2)}, u32[]{:S(2)}) %collective-permute-start.12) | collective-permute-done | bytes 131104 | tf_op jit(solution)/shard_map/ppermute | solution.py:252
  37.6 0.7 %shard_map.55.refs_0_ = bf16[128,8,128]{2,1,0:T(8,128)(2,1)} custom-call(f32[64,8,128]{2,1,0:T(8,128)S(1)} %get-tuple-element.42.means_ref, f32[64,8,128]{2,1,0:T(8,128)S(1)} %get-tuple-element.45.sum_ref, bf16[64,8,128]{2,1,0:T(8,128)(2,1)S(1)} %collective-permute-done.12.came_ref), custom_call_target="tpu_custom_call" | custom-call | tf_op jit(solution)/shard_map/pallas_call | solution.py:240
  38.3 0.1 collective-permute-done.10.came_ref
  38.4 0.7 %shard_map.56 = bf16[128,8,128]{2,1,0:T(8,128)(2,1)} custom-call(f32[64,8,128]{2,1,0:T(8,128)S(1)} %get-tuple-element.37.means_ref, f32[64,8,128]{2,1,0:T(8,128)S(1)} %get-tuple-element.40.sum_ref, bf16[64,8,128]{2,1,0:T(8,128)(2,1)S(1)} %collective-permute-done.10.came_ref, bf16[128,8,128]{2,1,0:T(8,128)(2,1)} %shard_map.55.refs_0_), custom_call_target="tpu_custom_call", output_to_operand_aliasing={{}: (3, {})} | custom-call | tf_op jit(solution)/shard_map/pallas_call | solution.py:240
  (7 shorter events, 0.2 us)
Async XLA Ops:
  0.0 8.1 %copy-start = (f32[1,128,2,512]{3,2,1,0:T(2,128)S(1)}, f32[1,128,2,512]{3,2,1,0:T(2,128)}, u32[]{:S(2)}) copy-start(f32[1,128,2,512]{3,2,1,0:T(2,128)} %param.7) | copy-start | bytes 1572868
  2.1 6.0 %collective-permute-start = (bf16[3,128,8,128]{3,2,1,0:T(8,128)(2,1)S(1)}, bf16[3,128,8,128]{3,2,1,0:T(8,128)(2,1)S(1)}, u32[]{:S(2)}, u32[]{:S(2)}) collective-permute-start(bf16[3,128,8,128]{3,2,1,0:T(8,128)(2,1)S(1)} %get-tuple-element.27), channel_id=1, source_target_pairs={{0,1},{1,0},{2,3},{3,2},{4,5},{5,4},{6,7},{7,6},{8,9},{9,8},{10,11... | collective-permute-start | bytes 2359304 | tf_op jit(solution)/shard_map/ppermute | solution.py:252
  2.7 2.3 %collective-permute-start.1 = (bf16[128,8,128]{2,1,0:T(8,128)(2,1)S(1)}, bf16[128,8,128]{2,1,0:T(8,128)(2,1)S(1)}, u32[]{:S(2)}, u32[]{:S(2)}) collective-permute-start(bf16[128,8,128]{2,1,0:T(8,128)(2,1)S(1)} %get-tuple-element.30), channel_id=1, source_target_pairs={{0,1},{1,0},{2,3},{3,2},{4,5},{5,4},{6,7},{7,6},{8,9},{9,8},{10,11... | collective-permute-start | bytes 786440 | tf_op jit(solution)/shard_map/ppermute | solution.py:252
  5.0 7.7 %collective-permute-start.2 = (bf16[72,8,128]{2,1,0:T(8,128)(2,1)S(1)}, bf16[72,8,128]{2,1,0:T(8,128)(2,1)S(1)}, u32[]{:S(2)}, u32[]{:S(2)}) collective-permute-start(bf16[72,8,128]{2,1,0:T(8,128)(2,1)S(1)} %get-tuple-element.31), channel_id=1, source_target_pairs={{0,2},{1,3},{2,0},{3,1},{4,6},{5,7},{6,4},{7,5},{8,10},{9,11},{10,... | collective-permute-start | bytes 442376 | tf_op jit(solution)/shard_map/ppermute | solution.py:252
  8.0 9.9 %collective-permute-start.4 = (bf16[56,8,128]{2,1,0:T(8,128)(2,1)S(1)}, bf16[56,8,128]{2,1,0:T(8,128)(2,1)S(1)}, u32[]{:S(2)}, u32[]{:S(2)}) collective-permute-start(bf16[56,8,128]{2,1,0:T(8,128)(2,1)S(1)} %get-tuple-element.33), channel_id=1, source_target_pairs={{0,2},{1,3},{2,0},{3,1},{4,6},{5,7},{6,4},{7,5},{8,10},{9,11},{10,... | collective-permute-start | bytes 344072 | tf_op jit(solution)/shard_map/ppermute | solution.py:252
  12.7 8.6 %collective-permute-start.3 = (bf16[72,8,128]{2,1,0:T(8,128)(2,1)S(1)}, bf16[72,8,128]{2,1,0:T(8,128)(2,1)S(1)}, u32[]{:S(2)}, u32[]{:S(2)}) collective-permute-start(bf16[72,8,128]{2,1,0:T(8,128)(2,1)S(1)} %get-tuple-element.32), channel_id=1, source_target_pairs={{0,4},{1,5},{2,6},{3,7},{4,0},{5,1},{6,2},{7,3},{8,12},{9,13},{10,... | collective-permute-start | bytes 442376 | tf_op jit(solution)/shard_map/ppermute | solution.py:252
  15.8 9.1 %collective-permute-start.7 = (bf16[72,8,128]{2,1,0:T(8,128)(2,1)S(1)}, bf16[72,8,128]{2,1,0:T(8,128)(2,1)S(1)}, u32[]{:S(2)}, u32[]{:S(2)}) collective-permute-start(bf16[72,8,128]{2,1,0:T(8,128)(2,1)S(1)} %get-tuple-element.35), channel_id=1, source_target_pairs={{0,2},{1,3},{2,0},{3,1},{4,6},{5,7},{6,4},{7,5},{8,10},{9,11},{10,... | collective-permute-start | bytes 442376 | tf_op jit(solution)/shard_map/ppermute | solution.py:252
  17.4 1.2 %collective-permute-start.5 = (bf16[1,8,128]{2,1,0:T(8,128)(2,1)S(1)}, bf16[1,8,128]{2,1,0:T(8,128)(2,1)S(1)}, u32[]{:S(2)}, u32[]{:S(2)}) collective-permute-start(bf16[1,8,128]{2,1,0:T(8,128)(2,1)S(1)} %get-tuple-element.34), channel_id=1, source_target_pairs={{0,1},{1,0},{2,3},{3,2},{4,5},{5,4},{6,7},{7,6},{8,9},{9,8},{10,11... | collective-permute-start | bytes 6152 | tf_op jit(solution)/shard_map/ppermute | solution.py:252
  17.4 9.5 %collective-permute-start.8 = (bf16[56,8,128]{2,1,0:T(8,128)(2,1)S(1)}, bf16[56,8,128]{2,1,0:T(8,128)(2,1)S(1)}, u32[]{:S(2)}, u32[]{:S(2)}) collective-permute-start(bf16[56,8,128]{2,1,0:T(8,128)(2,1)S(1)} %get-tuple-element.36), channel_id=1, source_target_pairs={{0,2},{1,3},{2,0},{3,1},{4,6},{5,7},{6,4},{7,5},{8,10},{9,11},{10,... | collective-permute-start | bytes 344072 | tf_op jit(solution)/shard_map/ppermute | solution.py:252
  18.6 8.3 %collective-permute-start.6 = (bf16[56,8,128]{2,1,0:T(8,128)(2,1)S(1)}, bf16[56,8,128]{2,1,0:T(8,128)(2,1)S(1)}, u32[]{:S(2)}, u32[]{:S(2)}) collective-permute-start(bf16[56,8,128]{2,1,0:T(8,128)(2,1)S(1)} %shard_map.50), channel_id=1, source_target_pairs={{0,4},{1,5},{2,6},{3,7},{4,0},{5,1},{6,2},{7,3},{8,12},{9,13},{10,... | collective-permute-start | bytes 344072 | tf_op jit(solution)/shard_map/ppermute | solution.py:252
  25.6 6.4 %collective-permute-start.11 = (bf16[64,8,128]{2,1,0:T(8,128)(2,1)S(1)}, bf16[64,8,128]{2,1,0:T(8,128)(2,1)S(1)}, u32[]{:S(2)}, u32[]{:S(2)}) collective-permute-start(bf16[64,8,128]{2,1,0:T(8,128)(2,1)S(1)} %get-tuple-element.44), channel_id=1, source_target_pairs={{0,8},{1,17},{2,10},{3,19},{4,12},{5,21},{6,14},{7,23},{8,0},{9,25... | collective-permute-start | bytes 393224 | tf_op jit(solution)/shard_map/ppermute | solution.py:252
  27.5 5.9 %collective-permute-start.9 = (bf16[64,8,128]{2,1,0:T(8,128)(2,1)S(1)}, bf16[64,8,128]{2,1,0:T(8,128)(2,1)S(1)}, u32[]{:S(2)}, u32[]{:S(2)}) collective-permute-start(bf16[64,8,128]{2,1,0:T(8,128)(2,1)S(1)} %get-tuple-element.39), channel_id=1, source_target_pairs={{0,16},{1,9},{2,18},{3,11},{4,20},{5,13},{6,22},{7,15},{8,24},{9,1... | collective-permute-start | bytes 393224 | tf_op jit(solution)/shard_map/ppermute | solution.py:252
  32.1 5.5 %collective-permute-start.12 = (bf16[64,8,128]{2,1,0:T(8,128)(2,1)S(1)}, bf16[64,8,128]{2,1,0:T(8,128)(2,1)S(1)}, u32[]{:S(2)}, u32[]{:S(2)}) collective-permute-start(bf16[64,8,128]{2,1,0:T(8,128)(2,1)S(1)} %get-tuple-element.46), channel_id=1, source_target_pairs={{0,16},{1,9},{2,18},{3,11},{4,20},{5,13},{6,22},{7,15},{8,24},{9,1... | collective-permute-start | bytes 393224 | tf_op jit(solution)/shard_map/ppermute | solution.py:252
  33.4 5.0 %collective-permute-start.10 = (bf16[64,8,128]{2,1,0:T(8,128)(2,1)S(1)}, bf16[64,8,128]{2,1,0:T(8,128)(2,1)S(1)}, u32[]{:S(2)}, u32[]{:S(2)}) collective-permute-start(bf16[64,8,128]{2,1,0:T(8,128)(2,1)S(1)} %get-tuple-element.41), channel_id=1, source_target_pairs={{0,8},{1,17},{2,10},{3,19},{4,12},{5,21},{6,14},{7,23},{8,0},{9,25... | collective-permute-start | bytes 393224 | tf_op jit(solution)/shard_map/ppermute | solution.py:252

commit v3 on v2

--- a/solution.py
+++ b/solution.py
@@ -40,7 +40,7 @@
 
 
 def place_kernel(relay, chips, early, owner_hbm, lead_hbm, swath_hbm, *refs):
-    early_ref, other_ref, own_ref, acc, swath, owner, lead, sems = refs
+    early_ref, acc, own_ref, swath, owner, lead, sems = refs
     blocks, scan, _, _ = swath.shape
     rows = own_ref.shape[1]
     me = lax.axis_index("tile")
@@ -90,15 +90,22 @@
         return carry
 
     lax.fori_loop(0, blocks, insert, 0)
-    others = [slot for slot in range(chips) if slot != early]
-
-    def emit(at):
-        span = pl.ds(at, STEP)
-        early_ref[span] = acc[early, span].astype(BF16)
-        for place, slot in enumerate(others):
-            other_ref[place, span] = acc[slot, span].astype(BF16)
-
-    rows_loop(rows, emit)
+    for at in range(0, early_ref.shape[0], STEP):
+        early_ref[pl.ds(at, STEP)] = acc[early, pl.ds(at, STEP)].astype(BF16)
+
+
+def round_kernel(slots, early, acc, rest_ref):
+    rows = acc.shape[1]
+
+    def part(at):
+        for place, slot in enumerate(slots):
+            rest_ref[pl.ds(place * rows + at, STEP)] = acc[slot, pl.ds(at, STEP)].astype(BF16)
+
+    rows_loop(rows, part)
+    base = len(slots) * rows
+    skipped = rows - (rest_ref.shape[0] - base)
+    for at in range(skipped, rows, STEP):
+        rest_ref[pl.ds(base + at - skipped, STEP)] = acc[early, pl.ds(at, STEP)].astype(BF16)
 
 
 def store_rows(refs, at, value):
@@ -116,19 +123,25 @@
         at -= ref.shape[0]
 
 
-def merge_early_kernel(early, own_ref, came_ref, *send_refs):
-    for at in range(0, came_ref.shape[0], STEP):
+def merge_early_kernel(early, own_ref, came_ref, send_ref):
+    for at in range(0, send_ref.shape[0], STEP):
         span = pl.ds(at, STEP)
-        store_rows(send_refs, at, own_ref[early, span] + came_ref[span].astype(F32))
-
-
-def merge_kernel(slots, pieces, own_ref, floor_ref, came_ref, keep_ref, *send_refs):
+        send_ref[span] = (own_ref[early, span] + came_ref[span].astype(F32)).astype(BF16)
+
+
+def merge_kernel(slots, early, pieces, own_ref, floor_ref, came_ref, keep_ref, *send_refs):
     send_refs = iter(send_refs)
     sends = [[next(send_refs) for _ in range(count)] for count in pieces]
-    for at in range(0, keep_ref.shape[0], STEP):
+    rows = keep_ref.shape[0]
+    base = len(slots) * rows
+    skipped = rows - (came_ref.shape[0] - base)
+    for at in range(0, rows, STEP):
         span = pl.ds(at, STEP)
+        if at >= skipped:
+            total = own_ref[early, span] + came_ref[pl.ds(base + at - skipped, STEP)].astype(F32)
+            sends[-1][0][pl.ds(at - skipped, STEP)] = total.astype(BF16)
         for place, slot in enumerate(slots):
-            total = own_ref[slot, span] + came_ref[place, span].astype(F32)
+            total = own_ref[slot, span] + came_ref[pl.ds(place * rows + at, STEP)].astype(F32)
             if place:
                 store_rows(sends[place - 1], at, total)
             else:
@@ -270,14 +283,14 @@
     starts = (0, cut + STEP)
     piece_shapes = tuple(jax.ShapeDtypeStruct((size, subs, LANES), BF16) for size in pieces)
     canvases = 4 * rows * subs * LANES * chips
-    early_out, other, own = call(
+    canvas_shape = jax.ShapeDtypeStruct((chips,) + full, F32)
+    early_out, acc, own = call(
         functools.partial(place_kernel, relay, chips, early),
-        (thin, jax.ShapeDtypeStruct((chips - 1,) + full, BF16), jax.ShapeDtypeStruct((chips,) + full, F32)),
+        (piece_shapes[0], canvas_shape, canvas_shape),
         tuple(pltpu.with_memory_space_constraint(a, pltpu.HBM) for a in (patch[:, 0], lead, swaths)),
         specs=[HBM] * 3,
-        mib=(3 * canvases >> 20) + 4,
+        mib=(2 * canvases >> 20) + 4,
         scratch=[
-            pltpu.VMEM((chips,) + full, F32),
             pltpu.VMEM(swaths.shape, BF16),
             pltpu.SMEM((blocks,), jnp.int32),
             pltpu.SMEM((blocks,), jnp.int32),
@@ -285,26 +298,37 @@
         ],
     )
     partner = [(t, t ^ 1) for t in range(tiles)]
-    early_came = permute(early_out, "tile", partner)
-    came = permute(other, "tile", partner)
-    early_sends = call(functools.partial(merge_early_kernel, early), piece_shapes, (own, early_came))
+    came_early = permute(early_out, "tile", partner)
+    rest = call(
+        functools.partial(round_kernel, slots, early),
+        jax.ShapeDtypeStruct((chips * rows - pieces[0], subs, LANES), BF16),
+        (acc,),
+        mib=(2 * canvases >> 20) + 4,
+    )
+    came = permute(rest, "tile", partner)
+    early_send = call(functools.partial(merge_early_kernel, early), piece_shapes[0], (own, came_early))
 
     def along(array, moves):
         return permute(array, "tile", [(2 * a + core, 2 * b + core) for a, b in moves for core in range(2)])
 
+    shift = 1 if relay else early
+    first_pass = [(c, c ^ shift if relay else (c + shift) % chips) for c in range(chips)]
+    passing = [along(early_send, first_pass)]
     if relay:
-        passing = [along(send, [(c, c ^ 1) for c in range(chips)]) for send in early_sends]
-        split = (len(pieces), 1)
-        outs = piece_shapes + (thin,)
+        split = (2, 1, 1)
+        outs = piece_shapes + (thin, piece_shapes[1])
     else:
-        arrived = [[along(early_sends[0], [(c, (c + early) % chips) for c in range(chips)])]]
         split = (1,) * (chips - 2)
         outs = (thin,) * (chips - 2)
     keep, *sends = call(
-        functools.partial(merge_kernel, slots, split), (wide,) + outs, (own, floor, came), mib=(2 * canvases >> 20) + 4
+        functools.partial(merge_kernel, slots, early, split),
+        (wide,) + outs,
+        (own, floor, came),
+        mib=(2 * canvases >> 20) + 4,
     )
     if relay:
-        *near_sends, far_send = sends
+        *near_sends, far_send, late_send = sends
+        passing.append(along(late_send, first_pass))
         far, near = [], []
         ready = jax.ShapeDtypeStruct((1, subs, LANES), BF16)
         waits = ()
@@ -320,6 +344,7 @@
                 waits = (permute(ready_out[0], "tile", partner),)
         arrived = [far, near]
     else:
+        arrived = [passing]
         for shift, send in zip(slots[1:], sends):
             arrived.append([along(send, [(c, (c + shift) % chips) for c in range(chips)])])
 

time: 39.3 us -> 39.2 us (level)
    pallas_call x11 -> x12, Pallas kernels: 5.03 us -> 4.98 us  [call(): pl.pallas_call(kernel, out_shape=outs, in_specs=specs or [VMEM] * len(ins...]
where the time goes in v3:
time: 39.2 us; the launch traced here: 39.1 us
  waiting for transfers between devices  19 us (48%)
  starting transfers between devices  15 us (38%)
  Pallas kernels  4.98 us (13%)
    ppermute x13, waiting for transfers between devices, permute(): return lax.ppermute(array, axes, pairs)  19 us
    ppermute x13, starting transfers between devices, permute(): return lax.ppermute(array, axes, pairs)  15 us
    pallas_call x12, Pallas kernels, call(): pl.pallas_call(kernel, out_shape=outs, in_specs=specs or [VMEM] * len(ins...  4.98 us
  transfers between devices with their start and end apart: 13, of which 8 were waited for; matrix products, arithmetic and copies ran while one was open for 0% of the time, Pallas kernels for 6%

profile of v3, /device:TPU:0, one launch (start us, length us, event | category | flops | bytes accessed | tf_op | source)
XLA Modules:
  0.0 39.1 jit_solution(17449008626417765117)
XLA Ops:
  0.0 1.9 %shard_map.46 = (bf16[72,8,128]{2,1,0:T(8,128)(2,1)S(1)}, f32[4,128,8,128]{3,2,1,0:T(8,128)S(1)}, f32[4,128,8,128]{3,2,1,0:T(8,128)S(1)}) custom-call(s32[16]{0:T(128)} %bitcast.18, s32[16]{0:T(128)} %lead_hbm.1, bf16[16,64,8,128]{3,2,1,0:T(8,128)(2,1)} %bitcast.17), custom_call_target="tpu_custom_call" | custom-call | tf_op jit(solution)/shard_map/pallas_call | solution.py:253
  1.9 0.0 copy-start
  1.9 0.1 shard_map.47
  2.1 0.6 %collective-permute-start = (bf16[440,8,128]{2,1,0:T(8,128)(2,1)S(1)}, bf16[440,8,128]{2,1,0:T(8,128)(2,1)S(1)}, u32[]{:S(2)}, u32[]{:S(2)}) collective-permute-start(bf16[440,8,128]{2,1,0:T(8,128)(2,1)S(1)} %shard_map.47), channel_id=1, source_target_pairs={{0,1},{1,0},{2,3},{3,2},{4,5},{5,4},{6,7},{7,6},{8,9},{9,8},{10,11... | collective-permute-start | bytes 2703368 | tf_op jit(solution)/shard_map/ppermute | solution.py:265
  2.6 0.1 collective-permute-start.1
  2.7 2.2 %collective-permute-done.1.came_ref = bf16[72,8,128]{2,1,0:T(8,128)(2,1)S(1)} collective-permute-done((bf16[72,8,128]{2,1,0:T(8,128)(2,1)S(1)}, bf16[72,8,128]{2,1,0:T(8,128)(2,1)S(1)}, u32[]{:S(2)}, u32[]{:S(2)}) %collective-permute-start.1) | collective-permute-done | bytes 147488 | tf_op jit(solution)/shard_map/ppermute | solution.py:265
  5.0 3.0 %collective-permute-start.2 = (bf16[72,8,128]{2,1,0:T(8,128)(2,1)S(1)}, bf16[72,8,128]{2,1,0:T(8,128)(2,1)S(1)}, u32[]{:S(2)}, u32[]{:S(2)}) collective-permute-start(bf16[72,8,128]{2,1,0:T(8,128)(2,1)S(1)} %shard_map.49), channel_id=1, source_target_pairs={{0,2},{1,3},{2,0},{3,1},{4,6},{5,7},{6,4},{7,5},{8,10},{9,11},{10,... | collective-permute-start | bytes 442376 | tf_op jit(solution)/shard_map/ppermute | solution.py:265
  7.9 0.0 collective-permute-done.came_ref
  7.9 0.2 shard_map.48
  8.1 0.1 collective-permute-start.4
  8.2 4.4 %collective-permute-done.2.passing_ref = bf16[72,8,128]{2,1,0:T(8,128)(2,1)S(1)} collective-permute-done((bf16[72,8,128]{2,1,0:T(8,128)(2,1)S(1)}, bf16[72,8,128]{2,1,0:T(8,128)(2,1)S(1)}, u32[]{:S(2)}, u32[]{:S(2)}) %collective-permute-start.2) | collective-permute-done | bytes 147488 | tf_op jit(solution)/shard_map/ppermute | solution.py:265
  12.7 3.1 %collective-permute-start.3 = (bf16[72,8,128]{2,1,0:T(8,128)(2,1)S(1)}, bf16[72,8,128]{2,1,0:T(8,128)(2,1)S(1)}, u32[]{:S(2)}, u32[]{:S(2)}) collective-permute-start(bf16[72,8,128]{2,1,0:T(8,128)(2,1)S(1)} %get-tuple-element.30), channel_id=1, source_target_pairs={{0,4},{1,5},{2,6},{3,7},{4,0},{5,1},{6,2},{7,3},{8,12},{9,13},{10,... | collective-permute-start | bytes 442376 | tf_op jit(solution)/shard_map/ppermute | solution.py:265
  15.8 1.6 %collective-permute-start.7 = (bf16[72,8,128]{2,1,0:T(8,128)(2,1)S(1)}, bf16[72,8,128]{2,1,0:T(8,128)(2,1)S(1)}, u32[]{:S(2)}, u32[]{:S(2)}) collective-permute-start(bf16[72,8,128]{2,1,0:T(8,128)(2,1)S(1)} %get-tuple-element.33), channel_id=1, source_target_pairs={{0,2},{1,3},{2,0},{3,1},{4,6},{5,7},{6,4},{7,5},{8,10},{9,11},{10,... | collective-permute-start | bytes 442376 | tf_op jit(solution)/shard_map/ppermute | solution.py:265
  17.4 0.0 collective-permute-start.5
  17.4 0.5 %collective-permute-start.8 = (bf16[56,8,128]{2,1,0:T(8,128)(2,1)S(1)}, bf16[56,8,128]{2,1,0:T(8,128)(2,1)S(1)}, u32[]{:S(2)}, u32[]{:S(2)}) collective-permute-start(bf16[56,8,128]{2,1,0:T(8,128)(2,1)S(1)} %get-tuple-element.34), channel_id=1, source_target_pairs={{0,2},{1,3},{2,0},{3,1},{4,6},{5,7},{6,4},{7,5},{8,10},{9,11},{10,... | collective-permute-start | bytes 344072 | tf_op jit(solution)/shard_map/ppermute | solution.py:265
  17.8 0.7 %collective-permute-done.5.refs_0_ = bf16[1,8,128]{2,1,0:T(8,128)(2,1)S(1)} collective-permute-done((bf16[1,8,128]{2,1,0:T(8,128)(2,1)S(1)}, bf16[1,8,128]{2,1,0:T(8,128)(2,1)S(1)}, u32[]{:S(2)}, u32[]{:S(2)}) %collective-permute-start.5) | collective-permute-done | bytes 2080 | tf_op jit(solution)/shard_map/ppermute | solution.py:265
  18.5 0.0 collective-permute-done.4.passing_ref
  18.6 0.4 %collective-permute-start.6 = (bf16[56,8,128]{2,1,0:T(8,128)(2,1)S(1)}, bf16[56,8,128]{2,1,0:T(8,128)(2,1)S(1)}, u32[]{:S(2)}, u32[]{:S(2)}) collective-permute-start(bf16[56,8,128]{2,1,0:T(8,128)(2,1)S(1)} %shard_map.51), channel_id=1, source_target_pairs={{0,4},{1,5},{2,6},{3,7},{4,0},{5,1},{6,2},{7,3},{8,12},{9,13},{10,... | collective-permute-start | bytes 344072 | tf_op jit(solution)/shard_map/ppermute | solution.py:265
  19.0 2.4 %collective-permute-done.3.refs_0_ = bf16[72,8,128]{2,1,0:T(8,128)(2,1)S(1)} collective-permute-done((bf16[72,8,128]{2,1,0:T(8,128)(2,1)S(1)}, bf16[72,8,128]{2,1,0:T(8,128)(2,1)S(1)}, u32[]{:S(2)}, u32[]{:S(2)}) %collective-permute-start.3) | collective-permute-done | bytes 147488 | tf_op jit(solution)/shard_map/ppermute | solution.py:265
  21.3 3.6 %collective-permute-done.7.refs_2_.refs_1_ = bf16[72,8,128]{2,1,0:T(8,128)(2,1)S(1)} collective-permute-done((bf16[72,8,128]{2,1,0:T(8,128)(2,1)S(1)}, bf16[72,8,128]{2,1,0:T(8,128)(2,1)S(1)}, u32[]{:S(2)}, u32[]{:S(2)}) %collective-permute-start.7) | collective-permute-done | bytes 147488 | tf_op jit(solution)/shard_map/ppermute | solution.py:265
  24.9 0.6 %shard_map.54 = (f32[64,8,128]{2,1,0:T(8,128)S(1)}, f32[64,8,128]{2,1,0:T(8,128)S(1)}, bf16[64,8,128]{2,1,0:T(8,128)(2,1)S(1)}) custom-call(f32[128,8,128]{2,1,0:T(8,128)S(1)} %get-tuple-element.27.keep_ref, bf16[72,8,128]{2,1,0:T(8,128)(2,1)S(1)} %collective-permute-done.3.refs_0_, bf16[72,8,128]{2,1,0:T(8,128)(2,1)S(1)} %collective-permute-done.7.refs_2_.refs_1_), custom_call_target="tpu_custom_call" | custom-call | tf_op jit(solution)/shard_map/pallas_call | solution.py:253
  25.5 1.3 %collective-permute-start.11 = (bf16[64,8,128]{2,1,0:T(8,128)(2,1)S(1)}, bf16[64,8,128]{2,1,0:T(8,128)(2,1)S(1)}, u32[]{:S(2)}, u32[]{:S(2)}) collective-permute-start(bf16[64,8,128]{2,1,0:T(8,128)(2,1)S(1)} %get-tuple-element.42), channel_id=1, source_target_pairs={{0,8},{1,17},{2,10},{3,19},{4,12},{5,21},{6,14},{7,23},{8,0},{9,25... | collective-permute-start | bytes 393224 | tf_op jit(solution)/shard_map/ppermute | solution.py:265
  26.8 0.6 %shard_map.52 = (f32[64,8,128]{2,1,0:T(8,128)S(1)}, f32[64,8,128]{2,1,0:T(8,128)S(1)}, bf16[64,8,128]{2,1,0:T(8,128)(2,1)S(1)}) custom-call(f32[128,8,128]{2,1,0:T(8,128)S(1)} %get-tuple-element.27.keep_ref, bf16[72,8,128]{2,1,0:T(8,128)(2,1)S(1)} %collective-permute-done.3.refs_0_, bf16[56,8,128]{2,1,0:T(8,128)(2,1)S(1)} %collective-permute-done.6.refs_1_, ...), custom_call_target="tpu_custom_call" | custom-call | tf_op jit(solution)/shard_map/pallas_call | solution.py:253
  27.5 1.6 %collective-permute-start.9 = (bf16[64,8,128]{2,1,0:T(8,128)(2,1)S(1)}, bf16[64,8,128]{2,1,0:T(8,128)(2,1)S(1)}, u32[]{:S(2)}, u32[]{:S(2)}) collective-permute-start(bf16[64,8,128]{2,1,0:T(8,128)(2,1)S(1)} %get-tuple-element.37), channel_id=1, source_target_pairs={{0,16},{1,9},{2,18},{3,11},{4,20},{5,13},{6,22},{7,15},{8,24},{9,1... | collective-permute-start | bytes 393224 | tf_op jit(solution)/shard_map/ppermute | solution.py:265
  29.1 2.9 %collective-permute-done.11.came_ref = bf16[64,8,128]{2,1,0:T(8,128)(2,1)S(1)} collective-permute-done((bf16[64,8,128]{2,1,0:T(8,128)(2,1)S(1)}, bf16[64,8,128]{2,1,0:T(8,128)(2,1)S(1)}, u32[]{:S(2)}, u32[]{:S(2)}) %collective-permute-start.11) | collective-permute-done | bytes 131104 | tf_op jit(solution)/shard_map/ppermute | solution.py:265
  32.0 1.3 %collective-permute-start.12 = (bf16[64,8,128]{2,1,0:T(8,128)(2,1)S(1)}, bf16[64,8,128]{2,1,0:T(8,128)(2,1)S(1)}, u32[]{:S(2)}, u32[]{:S(2)}) collective-permute-start(bf16[64,8,128]{2,1,0:T(8,128)(2,1)S(1)} %get-tuple-element.44), channel_id=1, source_target_pairs={{0,16},{1,9},{2,18},{3,11},{4,20},{5,13},{6,22},{7,15},{8,24},{9,1... | collective-permute-start | bytes 393224 | tf_op jit(solution)/shard_map/ppermute | solution.py:265
  33.3 0.0 collective-permute-done.9.came_ref
  33.4 1.6 %collective-permute-start.10 = (bf16[64,8,128]{2,1,0:T(8,128)(2,1)S(1)}, bf16[64,8,128]{2,1,0:T(8,128)(2,1)S(1)}, u32[]{:S(2)}, u32[]{:S(2)}) collective-permute-start(bf16[64,8,128]{2,1,0:T(8,128)(2,1)S(1)} %get-tuple-element.39), channel_id=1, source_target_pairs={{0,8},{1,17},{2,10},{3,19},{4,12},{5,21},{6,14},{7,23},{8,0},{9,25... | collective-permute-start | bytes 393224 | tf_op jit(solution)/shard_map/ppermute | solution.py:265
  34.9 2.6 %collective-permute-done.12.came_ref = bf16[64,8,128]{2,1,0:T(8,128)(2,1)S(1)} collective-permute-done((bf16[64,8,128]{2,1,0:T(8,128)(2,1)S(1)}, bf16[64,8,128]{2,1,0:T(8,128)(2,1)S(1)}, u32[]{:S(2)}, u32[]{:S(2)}) %collective-permute-start.12) | collective-permute-done | bytes 131104 | tf_op jit(solution)/shard_map/ppermute | solution.py:265
  37.5 0.7 %shard_map.56.refs_0_ = bf16[128,8,128]{2,1,0:T(8,128)(2,1)} custom-call(f32[64,8,128]{2,1,0:T(8,128)S(1)} %get-tuple-element.40.means_ref, f32[64,8,128]{2,1,0:T(8,128)S(1)} %get-tuple-element.43.sum_ref, bf16[64,8,128]{2,1,0:T(8,128)(2,1)S(1)} %collective-permute-done.12.came_ref), custom_call_target="tpu_custom_call" | custom-call | tf_op jit(solution)/shard_map/pallas_call | solution.py:253
  38.2 0.2 collective-permute-done.10.came_ref
  38.4 0.7 %shard_map.57 = bf16[128,8,128]{2,1,0:T(8,128)(2,1)} custom-call(f32[64,8,128]{2,1,0:T(8,128)S(1)} %get-tuple-element.35.means_ref, f32[64,8,128]{2,1,0:T(8,128)S(1)} %get-tuple-element.38.sum_ref, bf16[64,8,128]{2,1,0:T(8,128)(2,1)S(1)} %collective-permute-done.10.came_ref, bf16[128,8,128]{2,1,0:T(8,128)(2,1)} %shard_map.56.refs_0_), custom_call_target="tpu_custom_call", output_to_operand_aliasing={{}: (3, {})} | custom-call | tf_op jit(solution)/shard_map/pallas_call | solution.py:253
  (8 shorter events, 0.2 us)
Async XLA Ops:
  1.9 6.0 %copy-start = (f32[1,128,2,512]{3,2,1,0:T(2,128)S(1)}, f32[1,128,2,512]{3,2,1,0:T(2,128)}, u32[]{:S(2)}) copy-start(f32[1,128,2,512]{3,2,1,0:T(2,128)} %param.7) | copy-start | bytes 1572868
  2.1 5.9 %collective-permute-start = (bf16[440,8,128]{2,1,0:T(8,128)(2,1)S(1)}, bf16[440,8,128]{2,1,0:T(8,128)(2,1)S(1)}, u32[]{:S(2)}, u32[]{:S(2)}) collective-permute-start(bf16[440,8,128]{2,1,0:T(8,128)(2,1)S(1)} %shard_map.47), channel_id=1, source_target_pairs={{0,1},{1,0},{2,3},{3,2},{4,5},{5,4},{6,7},{7,6},{8,9},{9,8},{10,11... | collective-permute-start | bytes 2703368 | tf_op jit(solution)/shard_map/ppermute | solution.py:265
  2.6 2.3 %collective-permute-start.1 = (bf16[72,8,128]{2,1,0:T(8,128)(2,1)S(1)}, bf16[72,8,128]{2,1,0:T(8,128)(2,1)S(1)}, u32[]{:S(2)}, u32[]{:S(2)}) collective-permute-start(bf16[72,8,128]{2,1,0:T(8,128)(2,1)S(1)} %get-tuple-element.29), channel_id=1, source_target_pairs={{0,1},{1,0},{2,3},{3,2},{4,5},{5,4},{6,7},{7,6},{8,9},{9,8},{10,11... | collective-permute-start | bytes 442376 | tf_op jit(solution)/shard_map/ppermute | solution.py:265
  5.0 7.7 %collective-permute-start.2 = (bf16[72,8,128]{2,1,0:T(8,128)(2,1)S(1)}, bf16[72,8,128]{2,1,0:T(8,128)(2,1)S(1)}, u32[]{:S(2)}, u32[]{:S(2)}) collective-permute-start(bf16[72,8,128]{2,1,0:T(8,128)(2,1)S(1)} %shard_map.49), channel_id=1, source_target_pairs={{0,2},{1,3},{2,0},{3,1},{4,6},{5,7},{6,4},{7,5},{8,10},{9,11},{10,... | collective-permute-start | bytes 442376 | tf_op jit(solution)/shard_map/ppermute | solution.py:265
  8.1 10.4 %collective-permute-start.4 = (bf16[56,8,128]{2,1,0:T(8,128)(2,1)S(1)}, bf16[56,8,128]{2,1,0:T(8,128)(2,1)S(1)}, u32[]{:S(2)}, u32[]{:S(2)}) collective-permute-start(bf16[56,8,128]{2,1,0:T(8,128)(2,1)S(1)} %get-tuple-element.31), channel_id=1, source_target_pairs={{0,2},{1,3},{2,0},{3,1},{4,6},{5,7},{6,4},{7,5},{8,10},{9,11},{10,... | collective-permute-start | bytes 344072 | tf_op jit(solution)/shard_map/ppermute | solution.py:265
  12.7 8.6 %collective-permute-start.3 = (bf16[72,8,128]{2,1,0:T(8,128)(2,1)S(1)}, bf16[72,8,128]{2,1,0:T(8,128)(2,1)S(1)}, u32[]{:S(2)}, u32[]{:S(2)}) collective-permute-start(bf16[72,8,128]{2,1,0:T(8,128)(2,1)S(1)} %get-tuple-element.30), channel_id=1, source_target_pairs={{0,4},{1,5},{2,6},{3,7},{4,0},{5,1},{6,2},{7,3},{8,12},{9,13},{10,... | collective-permute-start | bytes 442376 | tf_op jit(solution)/shard_map/ppermute | solution.py:265
  15.8 9.1 %collective-permute-start.7 = (bf16[72,8,128]{2,1,0:T(8,128)(2,1)S(1)}, bf16[72,8,128]{2,1,0:T(8,128)(2,1)S(1)}, u32[]{:S(2)}, u32[]{:S(2)}) collective-permute-start(bf16[72,8,128]{2,1,0:T(8,128)(2,1)S(1)} %get-tuple-element.33), channel_id=1, source_target_pairs={{0,2},{1,3},{2,0},{3,1},{4,6},{5,7},{6,4},{7,5},{8,10},{9,11},{10,... | collective-permute-start | bytes 442376 | tf_op jit(solution)/shard_map/ppermute | solution.py:265
  17.4 1.2 %collective-permute-start.5 = (bf16[1,8,128]{2,1,0:T(8,128)(2,1)S(1)}, bf16[1,8,128]{2,1,0:T(8,128)(2,1)S(1)}, u32[]{:S(2)}, u32[]{:S(2)}) collective-permute-start(bf16[1,8,128]{2,1,0:T(8,128)(2,1)S(1)} %get-tuple-element.32), channel_id=1, source_target_pairs={{0,1},{1,0},{2,3},{3,2},{4,5},{5,4},{6,7},{7,6},{8,9},{9,8},{10,11... | collective-permute-start | bytes 6152 | tf_op jit(solution)/shard_map/ppermute | solution.py:265
  17.4 9.5 %collective-permute-start.8 = (bf16[56,8,128]{2,1,0:T(8,128)(2,1)S(1)}, bf16[56,8,128]{2,1,0:T(8,128)(2,1)S(1)}, u32[]{:S(2)}, u32[]{:S(2)}) collective-permute-start(bf16[56,8,128]{2,1,0:T(8,128)(2,1)S(1)} %get-tuple-element.34), channel_id=1, source_target_pairs={{0,2},{1,3},{2,0},{3,1},{4,6},{5,7},{6,4},{7,5},{8,10},{9,11},{10,... | collective-permute-start | bytes 344072 | tf_op jit(solution)/shard_map/ppermute | solution.py:265
  18.6 8.3 %collective-permute-start.6 = (bf16[56,8,128]{2,1,0:T(8,128)(2,1)S(1)}, bf16[56,8,128]{2,1,0:T(8,128)(2,1)S(1)}, u32[]{:S(2)}, u32[]{:S(2)}) collective-permute-start(bf16[56,8,128]{2,1,0:T(8,128)(2,1)S(1)} %shard_map.51), channel_id=1, source_target_pairs={{0,4},{1,5},{2,6},{3,7},{4,0},{5,1},{6,2},{7,3},{8,12},{9,13},{10,... | collective-permute-start | bytes 344072 | tf_op jit(solution)/shard_map/ppermute | solution.py:265
  25.5 6.4 %collective-permute-start.11 = (bf16[64,8,128]{2,1,0:T(8,128)(2,1)S(1)}, bf16[64,8,128]{2,1,0:T(8,128)(2,1)S(1)}, u32[]{:S(2)}, u32[]{:S(2)}) collective-permute-start(bf16[64,8,128]{2,1,0:T(8,128)(2,1)S(1)} %get-tuple-element.42), channel_id=1, source_target_pairs={{0,8},{1,17},{2,10},{3,19},{4,12},{5,21},{6,14},{7,23},{8,0},{9,25... | collective-permute-start | bytes 393224 | tf_op jit(solution)/shard_map/ppermute | solution.py:265
  27.5 5.9 %collective-permute-start.9 = (bf16[64,8,128]{2,1,0:T(8,128)(2,1)S(1)}, bf16[64,8,128]{2,1,0:T(8,128)(2,1)S(1)}, u32[]{:S(2)}, u32[]{:S(2)}) collective-permute-start(bf16[64,8,128]{2,1,0:T(8,128)(2,1)S(1)} %get-tuple-element.37), channel_id=1, source_target_pairs={{0,16},{1,9},{2,18},{3,11},{4,20},{5,13},{6,22},{7,15},{8,24},{9,1... | collective-permute-start | bytes 393224 | tf_op jit(solution)/shard_map/ppermute | solution.py:265
  32.0 5.5 %collective-permute-start.12 = (bf16[64,8,128]{2,1,0:T(8,128)(2,1)S(1)}, bf16[64,8,128]{2,1,0:T(8,128)(2,1)S(1)}, u32[]{:S(2)}, u32[]{:S(2)}) collective-permute-start(bf16[64,8,128]{2,1,0:T(8,128)(2,1)S(1)} %get-tuple-element.44), channel_id=1, source_target_pairs={{0,16},{1,9},{2,18},{3,11},{4,20},{5,13},{6,22},{7,15},{8,24},{9,1... | collective-permute-start | bytes 393224 | tf_op jit(solution)/shard_map/ppermute | solution.py:265
  33.4 5.0 %collective-permute-start.10 = (bf16[64,8,128]{2,1,0:T(8,128)(2,1)S(1)}, bf16[64,8,128]{2,1,0:T(8,128)(2,1)S(1)}, u32[]{:S(2)}, u32[]{:S(2)}) collective-permute-start(bf16[64,8,128]{2,1,0:T(8,128)(2,1)S(1)} %get-tuple-element.39), channel_id=1, source_target_pairs={{0,8},{1,17},{2,10},{3,19},{4,12},{5,21},{6,14},{7,23},{8,0},{9,25... | collective-permute-start | bytes 393224 | tf_op jit(solution)/shard_map/ppermute | solution.py:265

commit v4 on v3

--- a/solution.py
+++ b/solution.py
@@ -148,10 +148,7 @@
                 keep_ref[span] = total + floor_ref[span]
 
 
-def relay_kernel(start, mine_ref, passing_ref, *refs):
-    send_ref = refs[-1] if start else refs[0]
-    if not start:
-        refs[1][...] = jnp.zeros(refs[1].shape, BF16)
+def relay_kernel(start, mine_ref, passing_ref, send_ref):
     for at in range(0, send_ref.shape[0], STEP):
         span = pl.ds(at, STEP)
         total = mine_ref[pl.ds(start + at, STEP)].astype(F32) + passing_ref[span].astype(F32)
@@ -232,20 +229,20 @@
 def scale_kernel(dates, start, means_ref, sum_ref, came_ref, *refs):
     out_hbm, out, sems = refs[-3:]
     rows = sum_ref.shape[0]
-    pieces = 2
-    size = rows // pieces
+    ends = (0, rows // (2 * STEP) * STEP, rows)
 
     def copy(piece):
-        here = pl.ds(piece * size, size)
-        return pltpu.make_async_copy(out.at[here], out_hbm.at[pl.ds(start + piece * size, size)], sems.at[piece])
-
-    for piece in range(pieces):
-        for at in range(piece * size, piece * size + size, STEP):
+        here = pl.ds(ends[piece], ends[piece + 1] - ends[piece])
+        there = pl.ds(start + ends[piece], ends[piece + 1] - ends[piece])
+        return pltpu.make_async_copy(out.at[here], out_hbm.at[there], sems.at[piece])
+
+    for piece in range(2):
+        for at in range(ends[piece], ends[piece + 1], STEP):
             span = pl.ds(at, STEP)
             total = (sum_ref[span] + came_ref[span].astype(F32)) * (1.0 / dates)
             out[span] = (means_ref[span] * total).astype(BF16)
         copy(piece).start()
-    for piece in range(pieces):
+    for piece in range(2):
         copy(piece).wait()
 
 
@@ -330,18 +327,10 @@
         *near_sends, far_send, late_send = sends
         passing.append(along(late_send, first_pass))
         far, near = [], []
-        ready = jax.ShapeDtypeStruct((1, subs, LANES), BF16)
-        waits = ()
         for i, passed in enumerate(passing):
-            send, *ready_out = call(
-                functools.partial(relay_kernel, starts[i]),
-                (piece_shapes[i],) + (ready,) * (i == 0),
-                (far_send, passed, *waits),
-            )
+            send = call(functools.partial(relay_kernel, starts[i]), piece_shapes[i], (far_send, passed))
             far.append(along(send, [(c, c ^ 2) for c in range(chips)]))
             near.append(along(near_sends[i], [(c, c ^ 1) for c in range(chips)]))
-            if i == 0:
-                waits = (permute(ready_out[0], "tile", partner),)
         arrived = [far, near]
     else:
         arrived = [passing]

time: 39.2 us -> 37.4 us (0.954)
  waiting for transfers between devices: 19 us -> 14 us
  starting transfers between devices: 15 us -> 18.2 us
    ppermute x13 -> x12, waiting for transfers between devices: 19 us -> 14 us  [permute(): return lax.ppermute(array, axes, pairs)]
    ppermute x13 -> x12, starting transfers between devices: 15 us -> 18.2 us  [permute(): return lax.ppermute(array, axes, pairs)]
  transfers between devices with their start and end apart: 13 -> 12, of which waited for: 8 -> 8; matrix products, arithmetic and copies ran while one was open for 0% -> 0% of each run, Pallas kernels for 6% -> 6%
where the time goes in v4:
time: 37.4 us; the launch traced here: 37.2 us
  starting transfers between devices  18.2 us (49%)
  waiting for transfers between devices  14 us (37%)
  Pallas kernels  4.98 us (13%)
    ppermute x12, starting transfers between devices, permute(): return lax.ppermute(array, axes, pairs)  18.2 us
    ppermute x12, waiting for transfers between devices, permute(): return lax.ppermute(array, axes, pairs)  14 us
    pallas_call x12, Pallas kernels, call(): pl.pallas_call(kernel, out_shape=outs, in_specs=specs or [VMEM] * len(ins...  4.98 us
  transfers between devices with their start and end apart: 12, of which 8 were waited for; matrix products, arithmetic and copies ran while one was open for 0% of the time, Pallas kernels for 6%

profile of v4, /device:TPU:0, one launch (start us, length us, event | category | flops | bytes accessed | tf_op | source)
XLA Modules:
  0.0 37.2 jit_solution(10996562600363071214)
XLA Ops:
  0.0 1.9 %shard_map.46 = (bf16[72,8,128]{2,1,0:T(8,128)(2,1)S(1)}, f32[4,128,8,128]{3,2,1,0:T(8,128)S(1)}, f32[4,128,8,128]{3,2,1,0:T(8,128)S(1)}) custom-call(s32[16]{0:T(128)} %bitcast.18, s32[16]{0:T(128)} %lead_hbm.1, bf16[16,64,8,128]{3,2,1,0:T(8,128)(2,1)} %bitcast.17), custom_call_target="tpu_custom_call" | custom-call | tf_op jit(solution)/shard_map/pallas_call | solution.py:250
  1.9 0.0 copy-start
  1.9 0.1 shard_map.47
  2.1 0.6 %collective-permute-start = (bf16[440,8,128]{2,1,0:T(8,128)(2,1)S(1)}, bf16[440,8,128]{2,1,0:T(8,128)(2,1)S(1)}, u32[]{:S(2)}, u32[]{:S(2)}) collective-permute-start(bf16[440,8,128]{2,1,0:T(8,128)(2,1)S(1)} %shard_map.47), channel_id=1, source_target_pairs={{0,1},{1,0},{2,3},{3,2},{4,5},{5,4},{6,7},{7,6},{8,9},{9,8},{10,11... | collective-permute-start | bytes 2703368 | tf_op jit(solution)/shard_map/ppermute | solution.py:262
  2.6 0.1 collective-permute-start.1
  2.7 2.2 %collective-permute-done.1.came_ref = bf16[72,8,128]{2,1,0:T(8,128)(2,1)S(1)} collective-permute-done((bf16[72,8,128]{2,1,0:T(8,128)(2,1)S(1)}, bf16[72,8,128]{2,1,0:T(8,128)(2,1)S(1)}, u32[]{:S(2)}, u32[]{:S(2)}) %collective-permute-start.1) | collective-permute-done | bytes 147488 | tf_op jit(solution)/shard_map/ppermute | solution.py:262
  5.0 3.0 %collective-permute-start.2 = (bf16[72,8,128]{2,1,0:T(8,128)(2,1)S(1)}, bf16[72,8,128]{2,1,0:T(8,128)(2,1)S(1)}, u32[]{:S(2)}, u32[]{:S(2)}) collective-permute-start(bf16[72,8,128]{2,1,0:T(8,128)(2,1)S(1)} %shard_map.49), channel_id=1, source_target_pairs={{0,2},{1,3},{2,0},{3,1},{4,6},{5,7},{6,4},{7,5},{8,10},{9,11},{10,... | collective-permute-start | bytes 442376 | tf_op jit(solution)/shard_map/ppermute | solution.py:262
  7.9 0.0 collective-permute-done.came_ref
  7.9 0.2 shard_map.48
  8.1 0.1 collective-permute-start.4
  8.2 2.0 %collective-permute-start.6 = (bf16[72,8,128]{2,1,0:T(8,128)(2,1)S(1)}, bf16[72,8,128]{2,1,0:T(8,128)(2,1)S(1)}, u32[]{:S(2)}, u32[]{:S(2)}) collective-permute-start(bf16[72,8,128]{2,1,0:T(8,128)(2,1)S(1)} %get-tuple-element.29), channel_id=1, source_target_pairs={{0,2},{1,3},{2,0},{3,1},{4,6},{5,7},{6,4},{7,5},{8,10},{9,11},{10,... | collective-permute-start | bytes 442376 | tf_op jit(solution)/shard_map/ppermute | solution.py:262
  10.2 2.4 %collective-permute-done.2.passing_ref = bf16[72,8,128]{2,1,0:T(8,128)(2,1)S(1)} collective-permute-done((bf16[72,8,128]{2,1,0:T(8,128)(2,1)S(1)}, bf16[72,8,128]{2,1,0:T(8,128)(2,1)S(1)}, u32[]{:S(2)}, u32[]{:S(2)}) %collective-permute-start.2) | collective-permute-done | bytes 147488 | tf_op jit(solution)/shard_map/ppermute | solution.py:262
  12.7 3.1 %collective-permute-start.3 = (bf16[72,8,128]{2,1,0:T(8,128)(2,1)S(1)}, bf16[72,8,128]{2,1,0:T(8,128)(2,1)S(1)}, u32[]{:S(2)}, u32[]{:S(2)}) collective-permute-start(bf16[72,8,128]{2,1,0:T(8,128)(2,1)S(1)} %shard_map.50), channel_id=1, source_target_pairs={{0,4},{1,5},{2,6},{3,7},{4,0},{5,1},{6,2},{7,3},{8,12},{9,13},{10,... | collective-permute-start | bytes 442376 | tf_op jit(solution)/shard_map/ppermute | solution.py:262
  15.8 1.6 %collective-permute-start.7 = (bf16[56,8,128]{2,1,0:T(8,128)(2,1)S(1)}, bf16[56,8,128]{2,1,0:T(8,128)(2,1)S(1)}, u32[]{:S(2)}, u32[]{:S(2)}) collective-permute-start(bf16[56,8,128]{2,1,0:T(8,128)(2,1)S(1)} %get-tuple-element.30), channel_id=1, source_target_pairs={{0,2},{1,3},{2,0},{3,1},{4,6},{5,7},{6,4},{7,5},{8,10},{9,11},{10,... | collective-permute-start | bytes 344072 | tf_op jit(solution)/shard_map/ppermute | solution.py:262
  17.4 0.0 collective-permute-done.4.passing_ref
  17.4 0.8 %collective-permute-start.5 = (bf16[56,8,128]{2,1,0:T(8,128)(2,1)S(1)}, bf16[56,8,128]{2,1,0:T(8,128)(2,1)S(1)}, u32[]{:S(2)}, u32[]{:S(2)}) collective-permute-start(bf16[56,8,128]{2,1,0:T(8,128)(2,1)S(1)} %shard_map.51), channel_id=1, source_target_pairs={{0,4},{1,5},{2,6},{3,7},{4,0},{5,1},{6,2},{7,3},{8,12},{9,13},{10,... | collective-permute-start | bytes 344072 | tf_op jit(solution)/shard_map/ppermute | solution.py:262
  18.2 4.4 %collective-permute-done.6.refs_2_.refs_1_ = bf16[72,8,128]{2,1,0:T(8,128)(2,1)S(1)} collective-permute-done((bf16[72,8,128]{2,1,0:T(8,128)(2,1)S(1)}, bf16[72,8,128]{2,1,0:T(8,128)(2,1)S(1)}, u32[]{:S(2)}, u32[]{:S(2)}) %collective-permute-start.6) | collective-permute-done | bytes 147488 | tf_op jit(solution)/shard_map/ppermute | solution.py:262
  22.6 0.0 collective-permute-done.3.refs_0_
  22.6 0.6 %shard_map.54 = (f32[64,8,128]{2,1,0:T(8,128)S(1)}, f32[64,8,128]{2,1,0:T(8,128)S(1)}, bf16[64,8,128]{2,1,0:T(8,128)(2,1)S(1)}) custom-call(f32[128,8,128]{2,1,0:T(8,128)S(1)} %get-tuple-element.25.keep_ref, bf16[72,8,128]{2,1,0:T(8,128)(2,1)S(1)} %collective-permute-done.3.refs_0_, bf16[72,8,128]{2,1,0:T(8,128)(2,1)S(1)} %collective-permute-done.6.refs_2_.refs_1_), custom_call_target="tpu_custom_call" | custom-call | tf_op jit(solution)/shard_map/pallas_call | solution.py:250
  23.3 1.7 %collective-permute-start.10 = (bf16[64,8,128]{2,1,0:T(8,128)(2,1)S(1)}, bf16[64,8,128]{2,1,0:T(8,128)(2,1)S(1)}, u32[]{:S(2)}, u32[]{:S(2)}) collective-permute-start(bf16[64,8,128]{2,1,0:T(8,128)(2,1)S(1)} %get-tuple-element.38), channel_id=1, source_target_pairs={{0,8},{1,17},{2,10},{3,19},{4,12},{5,21},{6,14},{7,23},{8,0},{9,25... | collective-permute-start | bytes 393224 | tf_op jit(solution)/shard_map/ppermute | solution.py:262
  25.0 0.8 %collective-permute-done.7.refs_3_ = bf16[56,8,128]{2,1,0:T(8,128)(2,1)S(1)} collective-permute-done((bf16[56,8,128]{2,1,0:T(8,128)(2,1)S(1)}, bf16[56,8,128]{2,1,0:T(8,128)(2,1)S(1)}, u32[]{:S(2)}, u32[]{:S(2)}) %collective-permute-start.7) | collective-permute-done | bytes 114720 | tf_op jit(solution)/shard_map/ppermute | solution.py:262
  25.8 0.0 collective-permute-done.5.refs_1_
  25.8 0.6 %shard_map.52 = (f32[64,8,128]{2,1,0:T(8,128)S(1)}, f32[64,8,128]{2,1,0:T(8,128)S(1)}, bf16[64,8,128]{2,1,0:T(8,128)(2,1)S(1)}) custom-call(f32[128,8,128]{2,1,0:T(8,128)S(1)} %get-tuple-element.25.keep_ref, bf16[72,8,128]{2,1,0:T(8,128)(2,1)S(1)} %collective-permute-done.3.refs_0_, bf16[56,8,128]{2,1,0:T(8,128)(2,1)S(1)} %collective-permute-done.5.refs_1_, ...), custom_call_target="tpu_custom_call" | custom-call | tf_op jit(solution)/shard_map/pallas_call | solution.py:250
  26.4 1.8 %collective-permute-start.8 = (bf16[64,8,128]{2,1,0:T(8,128)(2,1)S(1)}, bf16[64,8,128]{2,1,0:T(8,128)(2,1)S(1)}, u32[]{:S(2)}, u32[]{:S(2)}) collective-permute-start(bf16[64,8,128]{2,1,0:T(8,128)(2,1)S(1)} %get-tuple-element.33), channel_id=1, source_target_pairs={{0,16},{1,9},{2,18},{3,11},{4,20},{5,13},{6,22},{7,15},{8,24},{9,1... | collective-permute-start | bytes 393224 | tf_op jit(solution)/shard_map/ppermute | solution.py:262
  28.2 0.1 collective-permute-done.10.came_ref
  28.3 1.7 %collective-permute-start.11 = (bf16[64,8,128]{2,1,0:T(8,128)(2,1)S(1)}, bf16[64,8,128]{2,1,0:T(8,128)(2,1)S(1)}, u32[]{:S(2)}, u32[]{:S(2)}) collective-permute-start(bf16[64,8,128]{2,1,0:T(8,128)(2,1)S(1)} %get-tuple-element.40), channel_id=1, source_target_pairs={{0,16},{1,9},{2,18},{3,11},{4,20},{5,13},{6,22},{7,15},{8,24},{9,1... | collective-permute-start | bytes 393224 | tf_op jit(solution)/shard_map/ppermute | solution.py:262
  30.1 1.4 %collective-permute-done.8.came_ref = bf16[64,8,128]{2,1,0:T(8,128)(2,1)S(1)} collective-permute-done((bf16[64,8,128]{2,1,0:T(8,128)(2,1)S(1)}, bf16[64,8,128]{2,1,0:T(8,128)(2,1)S(1)}, u32[]{:S(2)}, u32[]{:S(2)}) %collective-permute-start.8) | collective-permute-done | bytes 131104 | tf_op jit(solution)/shard_map/ppermute | solution.py:262
  31.5 1.7 %collective-permute-start.9 = (bf16[64,8,128]{2,1,0:T(8,128)(2,1)S(1)}, bf16[64,8,128]{2,1,0:T(8,128)(2,1)S(1)}, u32[]{:S(2)}, u32[]{:S(2)}) collective-permute-start(bf16[64,8,128]{2,1,0:T(8,128)(2,1)S(1)} %get-tuple-element.35), channel_id=1, source_target_pairs={{0,8},{1,17},{2,10},{3,19},{4,12},{5,21},{6,14},{7,23},{8,0},{9,25... | collective-permute-start | bytes 393224 | tf_op jit(solution)/shard_map/ppermute | solution.py:262
  33.2 1.0 %collective-permute-done.11.came_ref = bf16[64,8,128]{2,1,0:T(8,128)(2,1)S(1)} collective-permute-done((bf16[64,8,128]{2,1,0:T(8,128)(2,1)S(1)}, bf16[64,8,128]{2,1,0:T(8,128)(2,1)S(1)}, u32[]{:S(2)}, u32[]{:S(2)}) %collective-permute-start.11) | collective-permute-done | bytes 131104 | tf_op jit(solution)/shard_map/ppermute | solution.py:262
  34.2 0.7 %shard_map.56.refs_0_ = bf16[128,8,128]{2,1,0:T(8,128)(2,1)} custom-call(f32[64,8,128]{2,1,0:T(8,128)S(1)} %get-tuple-element.36.means_ref, f32[64,8,128]{2,1,0:T(8,128)S(1)} %get-tuple-element.39.sum_ref, bf16[64,8,128]{2,1,0:T(8,128)(2,1)S(1)} %collective-permute-done.11.came_ref), custom_call_target="tpu_custom_call" | custom-call | tf_op jit(solution)/shard_map/pallas_call | solution.py:250
  34.9 1.6 %collective-permute-done.9.came_ref = bf16[64,8,128]{2,1,0:T(8,128)(2,1)S(1)} collective-permute-done((bf16[64,8,128]{2,1,0:T(8,128)(2,1)S(1)}, bf16[64,8,128]{2,1,0:T(8,128)(2,1)S(1)}, u32[]{:S(2)}, u32[]{:S(2)}) %collective-permute-start.9) | collective-permute-done | bytes 131104 | tf_op jit(solution)/shard_map/ppermute | solution.py:262
  36.5 0.7 %shard_map.57 = bf16[128,8,128]{2,1,0:T(8,128)(2,1)} custom-call(f32[64,8,128]{2,1,0:T(8,128)S(1)} %get-tuple-element.31.means_ref, f32[64,8,128]{2,1,0:T(8,128)S(1)} %get-tuple-element.34.sum_ref, bf16[64,8,128]{2,1,0:T(8,128)(2,1)S(1)} %collective-permute-done.9.came_ref, bf16[128,8,128]{2,1,0:T(8,128)(2,1)} %shard_map.56.refs_0_), custom_call_target="tpu_custom_call", output_to_operand_aliasing={{}: (3, {})} | custom-call | tf_op jit(solution)/shard_map/pallas_call | solution.py:250
  (6 shorter events, 0.2 us)
Async XLA Ops:
  1.9 6.0 %copy-start = (f32[1,128,2,512]{3,2,1,0:T(2,128)S(1)}, f32[1,128,2,512]{3,2,1,0:T(2,128)}, u32[]{:S(2)}) copy-start(f32[1,128,2,512]{3,2,1,0:T(2,128)} %param.7) | copy-start | bytes 1572868
  2.1 5.9 %collective-permute-start = (bf16[440,8,128]{2,1,0:T(8,128)(2,1)S(1)}, bf16[440,8,128]{2,1,0:T(8,128)(2,1)S(1)}, u32[]{:S(2)}, u32[]{:S(2)}) collective-permute-start(bf16[440,8,128]{2,1,0:T(8,128)(2,1)S(1)} %shard_map.47), channel_id=1, source_target_pairs={{0,1},{1,0},{2,3},{3,2},{4,5},{5,4},{6,7},{7,6},{8,9},{9,8},{10,11... | collective-permute-start | bytes 2703368 | tf_op jit(solution)/shard_map/ppermute | solution.py:262
  2.6 2.3 %collective-permute-start.1 = (bf16[72,8,128]{2,1,0:T(8,128)(2,1)S(1)}, bf16[72,8,128]{2,1,0:T(8,128)(2,1)S(1)}, u32[]{:S(2)}, u32[]{:S(2)}) collective-permute-start(bf16[72,8,128]{2,1,0:T(8,128)(2,1)S(1)} %get-tuple-element.27), channel_id=1, source_target_pairs={{0,1},{1,0},{2,3},{3,2},{4,5},{5,4},{6,7},{7,6},{8,9},{9,8},{10,11... | collective-permute-start | bytes 442376 | tf_op jit(solution)/shard_map/ppermute | solution.py:262
  5.0 7.7 %collective-permute-start.2 = (bf16[72,8,128]{2,1,0:T(8,128)(2,1)S(1)}, bf16[72,8,128]{2,1,0:T(8,128)(2,1)S(1)}, u32[]{:S(2)}, u32[]{:S(2)}) collective-permute-start(bf16[72,8,128]{2,1,0:T(8,128)(2,1)S(1)} %shard_map.49), channel_id=1, source_target_pairs={{0,2},{1,3},{2,0},{3,1},{4,6},{5,7},{6,4},{7,5},{8,10},{9,11},{10,... | collective-permute-start | bytes 442376 | tf_op jit(solution)/shard_map/ppermute | solution.py:262
  8.1 9.2 %collective-permute-start.4 = (bf16[56,8,128]{2,1,0:T(8,128)(2,1)S(1)}, bf16[56,8,128]{2,1,0:T(8,128)(2,1)S(1)}, u32[]{:S(2)}, u32[]{:S(2)}) collective-permute-start(bf16[56,8,128]{2,1,0:T(8,128)(2,1)S(1)} %get-tuple-element.28), channel_id=1, source_target_pairs={{0,2},{1,3},{2,0},{3,1},{4,6},{5,7},{6,4},{7,5},{8,10},{9,11},{10,... | collective-permute-start | bytes 344072 | tf_op jit(solution)/shard_map/ppermute | solution.py:262
  8.2 14.4 %collective-permute-start.6 = (bf16[72,8,128]{2,1,0:T(8,128)(2,1)S(1)}, bf16[72,8,128]{2,1,0:T(8,128)(2,1)S(1)}, u32[]{:S(2)}, u32[]{:S(2)}) collective-permute-start(bf16[72,8,128]{2,1,0:T(8,128)(2,1)S(1)} %get-tuple-element.29), channel_id=1, source_target_pairs={{0,2},{1,3},{2,0},{3,1},{4,6},{5,7},{6,4},{7,5},{8,10},{9,11},{10,... | collective-permute-start | bytes 442376 | tf_op jit(solution)/shard_map/ppermute | solution.py:262
  12.7 10.0 %collective-permute-start.3 = (bf16[72,8,128]{2,1,0:T(8,128)(2,1)S(1)}, bf16[72,8,128]{2,1,0:T(8,128)(2,1)S(1)}, u32[]{:S(2)}, u32[]{:S(2)}) collective-permute-start(bf16[72,8,128]{2,1,0:T(8,128)(2,1)S(1)} %shard_map.50), channel_id=1, source_target_pairs={{0,4},{1,5},{2,6},{3,7},{4,0},{5,1},{6,2},{7,3},{8,12},{9,13},{10,... | collective-permute-start | bytes 442376 | tf_op jit(solution)/shard_map/ppermute | solution.py:262
  15.8 10.0 %collective-permute-start.7 = (bf16[56,8,128]{2,1,0:T(8,128)(2,1)S(1)}, bf16[56,8,128]{2,1,0:T(8,128)(2,1)S(1)}, u32[]{:S(2)}, u32[]{:S(2)}) collective-permute-start(bf16[56,8,128]{2,1,0:T(8,128)(2,1)S(1)} %get-tuple-element.30), channel_id=1, source_target_pairs={{0,2},{1,3},{2,0},{3,1},{4,6},{5,7},{6,4},{7,5},{8,10},{9,11},{10,... | collective-permute-start | bytes 344072 | tf_op jit(solution)/shard_map/ppermute | solution.py:262
  17.4 8.4 %collective-permute-start.5 = (bf16[56,8,128]{2,1,0:T(8,128)(2,1)S(1)}, bf16[56,8,128]{2,1,0:T(8,128)(2,1)S(1)}, u32[]{:S(2)}, u32[]{:S(2)}) collective-permute-start(bf16[56,8,128]{2,1,0:T(8,128)(2,1)S(1)} %shard_map.51), channel_id=1, source_target_pairs={{0,4},{1,5},{2,6},{3,7},{4,0},{5,1},{6,2},{7,3},{8,12},{9,13},{10,... | collective-permute-start | bytes 344072 | tf_op jit(solution)/shard_map/ppermute | solution.py:262
  23.3 5.0 %collective-permute-start.10 = (bf16[64,8,128]{2,1,0:T(8,128)(2,1)S(1)}, bf16[64,8,128]{2,1,0:T(8,128)(2,1)S(1)}, u32[]{:S(2)}, u32[]{:S(2)}) collective-permute-start(bf16[64,8,128]{2,1,0:T(8,128)(2,1)S(1)} %get-tuple-element.38), channel_id=1, source_target_pairs={{0,8},{1,17},{2,10},{3,19},{4,12},{5,21},{6,14},{7,23},{8,0},{9,25... | collective-permute-start | bytes 393224 | tf_op jit(solution)/shard_map/ppermute | solution.py:262
  26.4 5.0 %collective-permute-start.8 = (bf16[64,8,128]{2,1,0:T(8,128)(2,1)S(1)}, bf16[64,8,128]{2,1,0:T(8,128)(2,1)S(1)}, u32[]{:S(2)}, u32[]{:S(2)}) collective-permute-start(bf16[64,8,128]{2,1,0:T(8,128)(2,1)S(1)} %get-tuple-element.33), channel_id=1, source_target_pairs={{0,16},{1,9},{2,18},{3,11},{4,20},{5,13},{6,22},{7,15},{8,24},{9,1... | collective-permute-start | bytes 393224 | tf_op jit(solution)/shard_map/ppermute | solution.py:262
  28.3 5.8 %collective-permute-start.11 = (bf16[64,8,128]{2,1,0:T(8,128)(2,1)S(1)}, bf16[64,8,128]{2,1,0:T(8,128)(2,1)S(1)}, u32[]{:S(2)}, u32[]{:S(2)}) collective-permute-start(bf16[64,8,128]{2,1,0:T(8,128)(2,1)S(1)} %get-tuple-element.40), channel_id=1, source_target_pairs={{0,16},{1,9},{2,18},{3,11},{4,20},{5,13},{6,22},{7,15},{8,24},{9,1... | collective-permute-start | bytes 393224 | tf_op jit(solution)/shard_map/ppermute | solution.py:262
  31.5 5.0 %collective-permute-start.9 = (bf16[64,8,128]{2,1,0:T(8,128)(2,1)S(1)}, bf16[64,8,128]{2,1,0:T(8,128)(2,1)S(1)}, u32[]{:S(2)}, u32[]{:S(2)}) collective-permute-start(bf16[64,8,128]{2,1,0:T(8,128)(2,1)S(1)} %get-tuple-element.35), channel_id=1, source_target_pairs={{0,8},{1,17},{2,10},{3,19},{4,12},{5,21},{6,14},{7,23},{8,0},{9,25... | collective-permute-start | bytes 393224 | tf_op jit(solution)/shard_map/ppermute | solution.py:262

commit v5 on v4

--- a/solution.py
+++ b/solution.py
@@ -156,7 +156,7 @@
 
 
 def box_kernel(pieces, pols, first, last, keep_ref, *refs):
-    *came_refs, means_ref, ratio_ref, send_ref, canvas = refs
+    *came_refs, means_ref, send_ref, canvas = refs
     rows, subs, _ = keep_ref.shape
     low, high = max(first - STEP, 0), min(last + STEP, rows)
     origin = first - STEP
@@ -205,7 +205,6 @@
         ratio = x[REACH : REACH + STEP] / means
         span = pl.ds(at - first, STEP)
         means_ref[span] = means
-        ratio_ref[span] = ratio
         send_ref[span] = ratio.astype(BF16)
 
     row = lax.broadcasted_iota(jnp.int32, shape, 0)
@@ -219,7 +218,7 @@
 def add_kernel(ratio_ref, came_ref, sum_ref, send_ref):
     def part(at):
         span = pl.ds(at, STEP)
-        total = ratio_ref[span] + came_ref[span].astype(F32)
+        total = ratio_ref[span].astype(F32) + came_ref[span].astype(F32)
         sum_ref[span] = total
         send_ref[span] = total.astype(BF16)
 
@@ -239,7 +238,7 @@
     for piece in range(2):
         for at in range(ends[piece], ends[piece + 1], STEP):
             span = pl.ds(at, STEP)
-            total = (sum_ref[span] + came_ref[span].astype(F32)) * (1.0 / dates)
+            total = (sum_ref[span].astype(F32) + came_ref[span].astype(F32)) * (1.0 / dates)
             out[span] = (means_ref[span] * total).astype(BF16)
         copy(piece).start()
     for piece in range(2):
@@ -339,28 +338,21 @@
 
     bits = [1 << b for b in range(dates.bit_length() - 1)]
 
-    def across(step, part):
-        pairs = []
-        for d in range(dates):
-            for t in range(tiles):
-                bit = bits[-1 - step] if (t + part) % 2 else bits[step]
-                pairs.append((d * tiles + t, (d ^ bit) * tiles + t))
-        return pairs
-
     out = None
-    for part, (first, last) in enumerate(((0, cut), (cut, rows))):
+    for first, last in ((0, cut), (cut, rows)):
         shape = (last - first, subs, LANES)
         wide_part, thin_part = jax.ShapeDtypeStruct(shape, F32), jax.ShapeDtypeStruct(shape, BF16)
         used = [group[: 1 if last + STEP <= pieces[0] else None] for group in arrived]
-        means, total, send = call(
+        means, send = call(
             functools.partial(box_kernel, tuple(map(len, used)), pols, first, last),
-            (wide_part, wide_part, thin_part),
+            (wide_part, thin_part),
             (keep, *(piece for group in used for piece in group)),
             mib=8 if relay else 16,
             scratch=[pltpu.VMEM((last - first + 2 * STEP, subs, LANES), F32)],
         )
-        for step in range(len(bits)):
-            came = permute(send, ("date", "tile"), across(step, part))
+        total = send
+        for step, bit in enumerate(bits):
+            came = permute(send, "date", [(d, d ^ bit) for d in range(dates)])
             if step + 1 < len(bits):
                 total, send = call(add_kernel, (wide_part, thin_part), (total, came), mib=4)
         ins = (means, total, came) + (() if out is None else (out,))

time: 37.4 us -> 37.4 us (level)
  no operation moved by 1% of the time
where the time goes in v5:
time: 37.4 us; the launch traced here: 37.2 us
  starting transfers between devices  18.2 us (49%)
  waiting for transfers between devices  14 us (37%)
  Pallas kernels  4.98 us (13%)
    ppermute x12, starting transfers between devices, permute(): return lax.ppermute(array, axes, pairs)  18.2 us
    ppermute x12, waiting for transfers between devices, permute(): return lax.ppermute(array, axes, pairs)  14 us
    pallas_call x12, Pallas kernels, call(): pl.pallas_call(kernel, out_shape=outs, in_specs=specs or [VMEM] * len(ins...  4.98 us
  transfers between devices with their start and end apart: 12, of which 8 were waited for; matrix products, arithmetic and copies ran while one was open for 0% of the time, Pallas kernels for 6%

profile of v5, /device:TPU:0, one launch (start us, length us, event | category | flops | bytes accessed | tf_op | source)
XLA Modules:
  0.0 37.2 jit_solution(11983815469316142196)
XLA Ops:
  0.0 1.9 %shard_map.46 = (bf16[72,8,128]{2,1,0:T(8,128)(2,1)S(1)}, f32[4,128,8,128]{3,2,1,0:T(8,128)S(1)}, f32[4,128,8,128]{3,2,1,0:T(8,128)S(1)}) custom-call(s32[16]{0:T(128)} %bitcast.18, s32[16]{0:T(128)} %lead_hbm.1, bf16[16,64,8,128]{3,2,1,0:T(8,128)(2,1)} %bitcast.17), custom_call_target="tpu_custom_call" | custom-call | tf_op jit(solution)/shard_map/pallas_call | solution.py:249
  1.9 0.0 copy-start
  1.9 0.1 shard_map.47
  2.1 0.6 %collective-permute-start = (bf16[440,8,128]{2,1,0:T(8,128)(2,1)S(1)}, bf16[440,8,128]{2,1,0:T(8,128)(2,1)S(1)}, u32[]{:S(2)}, u32[]{:S(2)}) collective-permute-start(bf16[440,8,128]{2,1,0:T(8,128)(2,1)S(1)} %shard_map.47), channel_id=1, source_target_pairs={{0,1},{1,0},{2,3},{3,2},{4,5},{5,4},{6,7},{7,6},{8,9},{9,8},{10,11... | collective-permute-start | bytes 2703368 | tf_op jit(solution)/shard_map/ppermute | solution.py:261
  2.6 0.1 collective-permute-start.1
  2.7 2.2 %collective-permute-done.1.came_ref = bf16[72,8,128]{2,1,0:T(8,128)(2,1)S(1)} collective-permute-done((bf16[72,8,128]{2,1,0:T(8,128)(2,1)S(1)}, bf16[72,8,128]{2,1,0:T(8,128)(2,1)S(1)}, u32[]{:S(2)}, u32[]{:S(2)}) %collective-permute-start.1) | collective-permute-done | bytes 147488 | tf_op jit(solution)/shard_map/ppermute | solution.py:261
  5.0 3.0 %collective-permute-start.2 = (bf16[72,8,128]{2,1,0:T(8,128)(2,1)S(1)}, bf16[72,8,128]{2,1,0:T(8,128)(2,1)S(1)}, u32[]{:S(2)}, u32[]{:S(2)}) collective-permute-start(bf16[72,8,128]{2,1,0:T(8,128)(2,1)S(1)} %shard_map.49), channel_id=1, source_target_pairs={{0,2},{1,3},{2,0},{3,1},{4,6},{5,7},{6,4},{7,5},{8,10},{9,11},{10,... | collective-permute-start | bytes 442376 | tf_op jit(solution)/shard_map/ppermute | solution.py:261
  7.9 0.0 collective-permute-done.came_ref
  7.9 0.2 shard_map.48
  8.1 0.1 collective-permute-start.4
  8.2 2.0 %collective-permute-start.6 = (bf16[72,8,128]{2,1,0:T(8,128)(2,1)S(1)}, bf16[72,8,128]{2,1,0:T(8,128)(2,1)S(1)}, u32[]{:S(2)}, u32[]{:S(2)}) collective-permute-start(bf16[72,8,128]{2,1,0:T(8,128)(2,1)S(1)} %get-tuple-element.27), channel_id=1, source_target_pairs={{0,2},{1,3},{2,0},{3,1},{4,6},{5,7},{6,4},{7,5},{8,10},{9,11},{10,... | collective-permute-start | bytes 442376 | tf_op jit(solution)/shard_map/ppermute | solution.py:261
  10.2 2.4 %collective-permute-done.2.passing_ref = bf16[72,8,128]{2,1,0:T(8,128)(2,1)S(1)} collective-permute-done((bf16[72,8,128]{2,1,0:T(8,128)(2,1)S(1)}, bf16[72,8,128]{2,1,0:T(8,128)(2,1)S(1)}, u32[]{:S(2)}, u32[]{:S(2)}) %collective-permute-start.2) | collective-permute-done | bytes 147488 | tf_op jit(solution)/shard_map/ppermute | solution.py:261
  12.7 3.1 %collective-permute-start.3 = (bf16[72,8,128]{2,1,0:T(8,128)(2,1)S(1)}, bf16[72,8,128]{2,1,0:T(8,128)(2,1)S(1)}, u32[]{:S(2)}, u32[]{:S(2)}) collective-permute-start(bf16[72,8,128]{2,1,0:T(8,128)(2,1)S(1)} %shard_map.50), channel_id=1, source_target_pairs={{0,4},{1,5},{2,6},{3,7},{4,0},{5,1},{6,2},{7,3},{8,12},{9,13},{10,... | collective-permute-start | bytes 442376 | tf_op jit(solution)/shard_map/ppermute | solution.py:261
  15.8 1.6 %collective-permute-start.7 = (bf16[56,8,128]{2,1,0:T(8,128)(2,1)S(1)}, bf16[56,8,128]{2,1,0:T(8,128)(2,1)S(1)}, u32[]{:S(2)}, u32[]{:S(2)}) collective-permute-start(bf16[56,8,128]{2,1,0:T(8,128)(2,1)S(1)} %get-tuple-element.28), channel_id=1, source_target_pairs={{0,2},{1,3},{2,0},{3,1},{4,6},{5,7},{6,4},{7,5},{8,10},{9,11},{10,... | collective-permute-start | bytes 344072 | tf_op jit(solution)/shard_map/ppermute | solution.py:261
  17.4 0.0 collective-permute-done.4.passing_ref
  17.4 0.8 %collective-permute-start.5 = (bf16[56,8,128]{2,1,0:T(8,128)(2,1)S(1)}, bf16[56,8,128]{2,1,0:T(8,128)(2,1)S(1)}, u32[]{:S(2)}, u32[]{:S(2)}) collective-permute-start(bf16[56,8,128]{2,1,0:T(8,128)(2,1)S(1)} %shard_map.51), channel_id=1, source_target_pairs={{0,4},{1,5},{2,6},{3,7},{4,0},{5,1},{6,2},{7,3},{8,12},{9,13},{10,... | collective-permute-start | bytes 344072 | tf_op jit(solution)/shard_map/ppermute | solution.py:261
  18.2 4.4 %collective-permute-done.6.refs_2_.refs_1_ = bf16[72,8,128]{2,1,0:T(8,128)(2,1)S(1)} collective-permute-done((bf16[72,8,128]{2,1,0:T(8,128)(2,1)S(1)}, bf16[72,8,128]{2,1,0:T(8,128)(2,1)S(1)}, u32[]{:S(2)}, u32[]{:S(2)}) %collective-permute-start.6) | collective-permute-done | bytes 147488 | tf_op jit(solution)/shard_map/ppermute | solution.py:261
  22.6 0.0 collective-permute-done.3.refs_0_
  22.6 0.6 %shard_map.54 = (f32[64,8,128]{2,1,0:T(8,128)S(1)}, bf16[64,8,128]{2,1,0:T(8,128)(2,1)S(1)}) custom-call(f32[128,8,128]{2,1,0:T(8,128)S(1)} %get-tuple-element.23.keep_ref, bf16[72,8,128]{2,1,0:T(8,128)(2,1)S(1)} %collective-permute-done.3.refs_0_, bf16[72,8,128]{2,1,0:T(8,128)(2,1)S(1)} %collective-permute-done.6.refs_2_.refs_1_), custom_call_target="tpu_custom_call" | custom-call | tf_op jit(solution)/shard_map/pallas_call | solution.py:249
  23.3 1.7 %collective-permute-start.10 = (bf16[64,8,128]{2,1,0:T(8,128)(2,1)S(1)}, bf16[64,8,128]{2,1,0:T(8,128)(2,1)S(1)}, u32[]{:S(2)}, u32[]{:S(2)}) collective-permute-start(bf16[64,8,128]{2,1,0:T(8,128)(2,1)S(1)} %get-tuple-element.34.ratio_ref), channel_id=1, source_target_pairs={{0,8},{8,0},{16,24},{24,16},{1,9},{9,1},{17,25},{25,17},{2,10},{10... | collective-permute-start | bytes 393224 | tf_op jit(solution)/shard_map/ppermute | solution.py:261
  25.0 0.8 %collective-permute-done.7.refs_3_ = bf16[56,8,128]{2,1,0:T(8,128)(2,1)S(1)} collective-permute-done((bf16[56,8,128]{2,1,0:T(8,128)(2,1)S(1)}, bf16[56,8,128]{2,1,0:T(8,128)(2,1)S(1)}, u32[]{:S(2)}, u32[]{:S(2)}) %collective-permute-start.7) | collective-permute-done | bytes 114720 | tf_op jit(solution)/shard_map/ppermute | solution.py:261
  25.8 0.0 collective-permute-done.5.refs_1_
  25.8 0.6 %shard_map.52 = (f32[64,8,128]{2,1,0:T(8,128)S(1)}, bf16[64,8,128]{2,1,0:T(8,128)(2,1)S(1)}) custom-call(f32[128,8,128]{2,1,0:T(8,128)S(1)} %get-tuple-element.23.keep_ref, bf16[72,8,128]{2,1,0:T(8,128)(2,1)S(1)} %collective-permute-done.3.refs_0_, bf16[56,8,128]{2,1,0:T(8,128)(2,1)S(1)} %collective-permute-done.5.refs_1_, ...), custom_call_target="tpu_custom_call" | custom-call | tf_op jit(solution)/shard_map/pallas_call | solution.py:249
  26.4 1.7 %collective-permute-start.8 = (bf16[64,8,128]{2,1,0:T(8,128)(2,1)S(1)}, bf16[64,8,128]{2,1,0:T(8,128)(2,1)S(1)}, u32[]{:S(2)}, u32[]{:S(2)}) collective-permute-start(bf16[64,8,128]{2,1,0:T(8,128)(2,1)S(1)} %get-tuple-element.30.ratio_ref), channel_id=1, source_target_pairs={{0,8},{8,0},{16,24},{24,16},{1,9},{9,1},{17,25},{25,17},{2,10},{10... | collective-permute-start | bytes 393224 | tf_op jit(solution)/shard_map/ppermute | solution.py:261
  28.1 0.2 collective-permute-done.10.came_ref
  28.3 1.7 %collective-permute-start.11 = (bf16[64,8,128]{2,1,0:T(8,128)(2,1)S(1)}, bf16[64,8,128]{2,1,0:T(8,128)(2,1)S(1)}, u32[]{:S(2)}, u32[]{:S(2)}) collective-permute-start(bf16[64,8,128]{2,1,0:T(8,128)(2,1)S(1)} %get-tuple-element.36), channel_id=1, source_target_pairs={{0,16},{8,24},{16,0},{24,8},{1,17},{9,25},{17,1},{25,9},{2,18},{10... | collective-permute-start | bytes 393224 | tf_op jit(solution)/shard_map/ppermute | solution.py:261
  30.1 1.4 %collective-permute-done.8.came_ref = bf16[64,8,128]{2,1,0:T(8,128)(2,1)S(1)} collective-permute-done((bf16[64,8,128]{2,1,0:T(8,128)(2,1)S(1)}, bf16[64,8,128]{2,1,0:T(8,128)(2,1)S(1)}, u32[]{:S(2)}, u32[]{:S(2)}) %collective-permute-start.8) | collective-permute-done | bytes 131104 | tf_op jit(solution)/shard_map/ppermute | solution.py:261
  31.5 1.8 %collective-permute-start.9 = (bf16[64,8,128]{2,1,0:T(8,128)(2,1)S(1)}, bf16[64,8,128]{2,1,0:T(8,128)(2,1)S(1)}, u32[]{:S(2)}, u32[]{:S(2)}) collective-permute-start(bf16[64,8,128]{2,1,0:T(8,128)(2,1)S(1)} %get-tuple-element.32), channel_id=1, source_target_pairs={{0,16},{8,24},{16,0},{24,8},{1,17},{9,25},{17,1},{25,9},{2,18},{10... | collective-permute-start | bytes 393224 | tf_op jit(solution)/shard_map/ppermute | solution.py:261
  33.2 0.9 %collective-permute-done.11.came_ref = bf16[64,8,128]{2,1,0:T(8,128)(2,1)S(1)} collective-permute-done((bf16[64,8,128]{2,1,0:T(8,128)(2,1)S(1)}, bf16[64,8,128]{2,1,0:T(8,128)(2,1)S(1)}, u32[]{:S(2)}, u32[]{:S(2)}) %collective-permute-start.11) | collective-permute-done | bytes 131104 | tf_op jit(solution)/shard_map/ppermute | solution.py:261
  34.2 0.7 %shard_map.56.refs_0_ = bf16[128,8,128]{2,1,0:T(8,128)(2,1)} custom-call(f32[64,8,128]{2,1,0:T(8,128)S(1)} %get-tuple-element.33.means_ref, f32[64,8,128]{2,1,0:T(8,128)S(1)} %get-tuple-element.35.sum_ref, bf16[64,8,128]{2,1,0:T(8,128)(2,1)S(1)} %collective-permute-done.11.came_ref), custom_call_target="tpu_custom_call" | custom-call | tf_op jit(solution)/shard_map/pallas_call | solution.py:249
  34.9 1.6 %collective-permute-done.9.came_ref = bf16[64,8,128]{2,1,0:T(8,128)(2,1)S(1)} collective-permute-done((bf16[64,8,128]{2,1,0:T(8,128)(2,1)S(1)}, bf16[64,8,128]{2,1,0:T(8,128)(2,1)S(1)}, u32[]{:S(2)}, u32[]{:S(2)}) %collective-permute-start.9) | collective-permute-done | bytes 131104 | tf_op jit(solution)/shard_map/ppermute | solution.py:261
  36.5 0.7 %shard_map.57 = bf16[128,8,128]{2,1,0:T(8,128)(2,1)} custom-call(f32[64,8,128]{2,1,0:T(8,128)S(1)} %get-tuple-element.29.means_ref, f32[64,8,128]{2,1,0:T(8,128)S(1)} %get-tuple-element.31.sum_ref, bf16[64,8,128]{2,1,0:T(8,128)(2,1)S(1)} %collective-permute-done.9.came_ref, bf16[128,8,128]{2,1,0:T(8,128)(2,1)} %shard_map.56.refs_0_), custom_call_target="tpu_custom_call", output_to_operand_aliasing={{}: (3, {})} | custom-call | tf_op jit(solution)/shard_map/pallas_call | solution.py:249
  (6 shorter events, 0.2 us)
Async XLA Ops:
  1.9 6.0 %copy-start = (f32[1,128,2,512]{3,2,1,0:T(2,128)S(1)}, f32[1,128,2,512]{3,2,1,0:T(2,128)}, u32[]{:S(2)}) copy-start(f32[1,128,2,512]{3,2,1,0:T(2,128)} %param.7) | copy-start | bytes 1572868
  2.1 5.9 %collective-permute-start = (bf16[440,8,128]{2,1,0:T(8,128)(2,1)S(1)}, bf16[440,8,128]{2,1,0:T(8,128)(2,1)S(1)}, u32[]{:S(2)}, u32[]{:S(2)}) collective-permute-start(bf16[440,8,128]{2,1,0:T(8,128)(2,1)S(1)} %shard_map.47), channel_id=1, source_target_pairs={{0,1},{1,0},{2,3},{3,2},{4,5},{5,4},{6,7},{7,6},{8,9},{9,8},{10,11... | collective-permute-start | bytes 2703368 | tf_op jit(solution)/shard_map/ppermute | solution.py:261
  2.6 2.3 %collective-permute-start.1 = (bf16[72,8,128]{2,1,0:T(8,128)(2,1)S(1)}, bf16[72,8,128]{2,1,0:T(8,128)(2,1)S(1)}, u32[]{:S(2)}, u32[]{:S(2)}) collective-permute-start(bf16[72,8,128]{2,1,0:T(8,128)(2,1)S(1)} %get-tuple-element.25), channel_id=1, source_target_pairs={{0,1},{1,0},{2,3},{3,2},{4,5},{5,4},{6,7},{7,6},{8,9},{9,8},{10,11... | collective-permute-start | bytes 442376 | tf_op jit(solution)/shard_map/ppermute | solution.py:261
  5.0 7.7 %collective-permute-start.2 = (bf16[72,8,128]{2,1,0:T(8,128)(2,1)S(1)}, bf16[72,8,128]{2,1,0:T(8,128)(2,1)S(1)}, u32[]{:S(2)}, u32[]{:S(2)}) collective-permute-start(bf16[72,8,128]{2,1,0:T(8,128)(2,1)S(1)} %shard_map.49), channel_id=1, source_target_pairs={{0,2},{1,3},{2,0},{3,1},{4,6},{5,7},{6,4},{7,5},{8,10},{9,11},{10,... | collective-permute-start | bytes 442376 | tf_op jit(solution)/shard_map/ppermute | solution.py:261
  8.1 9.2 %collective-permute-start.4 = (bf16[56,8,128]{2,1,0:T(8,128)(2,1)S(1)}, bf16[56,8,128]{2,1,0:T(8,128)(2,1)S(1)}, u32[]{:S(2)}, u32[]{:S(2)}) collective-permute-start(bf16[56,8,128]{2,1,0:T(8,128)(2,1)S(1)} %get-tuple-element.26), channel_id=1, source_target_pairs={{0,2},{1,3},{2,0},{3,1},{4,6},{5,7},{6,4},{7,5},{8,10},{9,11},{10,... | collective-permute-start | bytes 344072 | tf_op jit(solution)/shard_map/ppermute | solution.py:261
  8.2 14.4 %collective-permute-start.6 = (bf16[72,8,128]{2,1,0:T(8,128)(2,1)S(1)}, bf16[72,8,128]{2,1,0:T(8,128)(2,1)S(1)}, u32[]{:S(2)}, u32[]{:S(2)}) collective-permute-start(bf16[72,8,128]{2,1,0:T(8,128)(2,1)S(1)} %get-tuple-element.27), channel_id=1, source_target_pairs={{0,2},{1,3},{2,0},{3,1},{4,6},{5,7},{6,4},{7,5},{8,10},{9,11},{10,... | collective-permute-start | bytes 442376 | tf_op jit(solution)/shard_map/ppermute | solution.py:261
  12.7 10.0 %collective-permute-start.3 = (bf16[72,8,128]{2,1,0:T(8,128)(2,1)S(1)}, bf16[72,8,128]{2,1,0:T(8,128)(2,1)S(1)}, u32[]{:S(2)}, u32[]{:S(2)}) collective-permute-start(bf16[72,8,128]{2,1,0:T(8,128)(2,1)S(1)} %shard_map.50), channel_id=1, source_target_pairs={{0,4},{1,5},{2,6},{3,7},{4,0},{5,1},{6,2},{7,3},{8,12},{9,13},{10,... | collective-permute-start | bytes 442376 | tf_op jit(solution)/shard_map/ppermute | solution.py:261
  15.8 10.0 %collective-permute-start.7 = (bf16[56,8,128]{2,1,0:T(8,128)(2,1)S(1)}, bf16[56,8,128]{2,1,0:T(8,128)(2,1)S(1)}, u32[]{:S(2)}, u32[]{:S(2)}) collective-permute-start(bf16[56,8,128]{2,1,0:T(8,128)(2,1)S(1)} %get-tuple-element.28), channel_id=1, source_target_pairs={{0,2},{1,3},{2,0},{3,1},{4,6},{5,7},{6,4},{7,5},{8,10},{9,11},{10,... | collective-permute-start | bytes 344072 | tf_op jit(solution)/shard_map/ppermute | solution.py:261
  17.4 8.4 %collective-permute-start.5 = (bf16[56,8,128]{2,1,0:T(8,128)(2,1)S(1)}, bf16[56,8,128]{2,1,0:T(8,128)(2,1)S(1)}, u32[]{:S(2)}, u32[]{:S(2)}) collective-permute-start(bf16[56,8,128]{2,1,0:T(8,128)(2,1)S(1)} %shard_map.51), channel_id=1, source_target_pairs={{0,4},{1,5},{2,6},{3,7},{4,0},{5,1},{6,2},{7,3},{8,12},{9,13},{10,... | collective-permute-start | bytes 344072 | tf_op jit(solution)/shard_map/ppermute | solution.py:261
  23.3 5.0 %collective-permute-start.10 = (bf16[64,8,128]{2,1,0:T(8,128)(2,1)S(1)}, bf16[64,8,128]{2,1,0:T(8,128)(2,1)S(1)}, u32[]{:S(2)}, u32[]{:S(2)}) collective-permute-start(bf16[64,8,128]{2,1,0:T(8,128)(2,1)S(1)} %get-tuple-element.34.ratio_ref), channel_id=1, source_target_pairs={{0,8},{8,0},{16,24},{24,16},{1,9},{9,1},{17,25},{25,17},{2,10},{10... | collective-permute-start | bytes 393224 | tf_op jit(solution)/shard_map/ppermute | solution.py:261
  26.4 5.0 %collective-permute-start.8 = (bf16[64,8,128]{2,1,0:T(8,128)(2,1)S(1)}, bf16[64,8,128]{2,1,0:T(8,128)(2,1)S(1)}, u32[]{:S(2)}, u32[]{:S(2)}) collective-permute-start(bf16[64,8,128]{2,1,0:T(8,128)(2,1)S(1)} %get-tuple-element.30.ratio_ref), channel_id=1, source_target_pairs={{0,8},{8,0},{16,24},{24,16},{1,9},{9,1},{17,25},{25,17},{2,10},{10... | collective-permute-start | bytes 393224 | tf_op jit(solution)/shard_map/ppermute | solution.py:261
  28.3 5.8 %collective-permute-start.11 = (bf16[64,8,128]{2,1,0:T(8,128)(2,1)S(1)}, bf16[64,8,128]{2,1,0:T(8,128)(2,1)S(1)}, u32[]{:S(2)}, u32[]{:S(2)}) collective-permute-start(bf16[64,8,128]{2,1,0:T(8,128)(2,1)S(1)} %get-tuple-element.36), channel_id=1, source_target_pairs={{0,16},{8,24},{16,0},{24,8},{1,17},{9,25},{17,1},{25,9},{2,18},{10... | collective-permute-start | bytes 393224 | tf_op jit(solution)/shard_map/ppermute | solution.py:261
  31.5 5.0 %collective-permute-start.9 = (bf16[64,8,128]{2,1,0:T(8,128)(2,1)S(1)}, bf16[64,8,128]{2,1,0:T(8,128)(2,1)S(1)}, u32[]{:S(2)}, u32[]{:S(2)}) collective-permute-start(bf16[64,8,128]{2,1,0:T(8,128)(2,1)S(1)} %get-tuple-element.32), channel_id=1, source_target_pairs={{0,16},{8,24},{16,0},{24,8},{1,17},{9,25},{17,1},{25,9},{2,18},{10... | collective-permute-start | bytes 393224 | tf_op jit(solution)/shard_map/ppermute | solution.py:261

commit v6 on v5

--- a/solution.py
+++ b/solution.py
@@ -156,7 +156,7 @@
 
 
 def box_kernel(pieces, pols, first, last, keep_ref, *refs):
-    *came_refs, means_ref, send_ref, canvas = refs
+    *came_refs, means_ref, ratio_ref, send_ref, canvas = refs
     rows, subs, _ = keep_ref.shape
     low, high = max(first - STEP, 0), min(last + STEP, rows)
     origin = first - STEP
@@ -205,6 +205,7 @@
         ratio = x[REACH : REACH + STEP] / means
         span = pl.ds(at - first, STEP)
         means_ref[span] = means
+        ratio_ref[span] = ratio
         send_ref[span] = ratio.astype(BF16)
 
     row = lax.broadcasted_iota(jnp.int32, shape, 0)
@@ -218,7 +219,7 @@
 def add_kernel(ratio_ref, came_ref, sum_ref, send_ref):
     def part(at):
         span = pl.ds(at, STEP)
-        total = ratio_ref[span].astype(F32) + came_ref[span].astype(F32)
+        total = ratio_ref[span] + came_ref[span].astype(F32)
         sum_ref[span] = total
         send_ref[span] = total.astype(BF16)
 
@@ -238,7 +239,7 @@
     for piece in range(2):
         for at in range(ends[piece], ends[piece + 1], STEP):
             span = pl.ds(at, STEP)
-            total = (sum_ref[span].astype(F32) + came_ref[span].astype(F32)) * (1.0 / dates)
+            total = (sum_ref[span] + came_ref[span].astype(F32)) * (1.0 / dates)
             out[span] = (means_ref[span] * total).astype(BF16)
         copy(piece).start()
     for piece in range(2):
@@ -336,21 +337,20 @@
         for shift, send in zip(slots[1:], sends):
             arrived.append([along(send, [(c, (c + shift) % chips) for c in range(chips)])])
 
-    bits = [1 << b for b in range(dates.bit_length() - 1)]
+    bits = [1 << b for b in range(dates.bit_length() - 1)][::-1]
 
     out = None
     for first, last in ((0, cut), (cut, rows)):
         shape = (last - first, subs, LANES)
         wide_part, thin_part = jax.ShapeDtypeStruct(shape, F32), jax.ShapeDtypeStruct(shape, BF16)
         used = [group[: 1 if last + STEP <= pieces[0] else None] for group in arrived]
-        means, send = call(
+        means, total, send = call(
             functools.partial(box_kernel, tuple(map(len, used)), pols, first, last),
-            (wide_part, thin_part),
+            (wide_part, wide_part, thin_part),
             (keep, *(piece for group in used for piece in group)),
             mib=8 if relay else 16,
             scratch=[pltpu.VMEM((last - first + 2 * STEP, subs, LANES), F32)],
         )
-        total = send
         for step, bit in enumerate(bits):
             came = permute(send, "date", [(d, d ^ bit) for d in range(dates)])
             if step + 1 < len(bits):

time: 37.4 us -> 37.4 us (level)
  no operation moved by 1% of the time
where the time goes in v6:
time: 37.4 us; the launch traced here: 37.2 us
  starting transfers between devices  18.2 us (49%)
  waiting for transfers between devices  14 us (37%)
  Pallas kernels  4.98 us (13%)
    ppermute x12, starting transfers between devices, permute(): return lax.ppermute(array, axes, pairs)  18.2 us
    ppermute x12, waiting for transfers between devices, permute(): return lax.ppermute(array, axes, pairs)  14 us
    pallas_call x12, Pallas kernels, call(): pl.pallas_call(kernel, out_shape=outs, in_specs=specs or [VMEM] * len(ins...  4.98 us
  transfers between devices with their start and end apart: 12, of which 8 were waited for; matrix products, arithmetic and copies ran while one was open for 0% of the time, Pallas kernels for 6%

profile of v6, /device:TPU:0, one launch (start us, length us, event | category | flops | bytes accessed | tf_op | source)
XLA Modules:
  0.0 37.2 jit_solution(7022223994061448486)
XLA Ops:
  0.0 1.9 %shard_map.46 = (bf16[72,8,128]{2,1,0:T(8,128)(2,1)S(1)}, f32[4,128,8,128]{3,2,1,0:T(8,128)S(1)}, f32[4,128,8,128]{3,2,1,0:T(8,128)S(1)}) custom-call(s32[16]{0:T(128)} %bitcast.18, s32[16]{0:T(128)} %lead_hbm.1, bf16[16,64,8,128]{3,2,1,0:T(8,128)(2,1)} %bitcast.17), custom_call_target="tpu_custom_call" | custom-call | tf_op jit(solution)/shard_map/pallas_call | solution.py:250
  1.9 0.0 copy-start
  1.9 0.1 shard_map.47
  2.1 0.6 %collective-permute-start = (bf16[440,8,128]{2,1,0:T(8,128)(2,1)S(1)}, bf16[440,8,128]{2,1,0:T(8,128)(2,1)S(1)}, u32[]{:S(2)}, u32[]{:S(2)}) collective-permute-start(bf16[440,8,128]{2,1,0:T(8,128)(2,1)S(1)} %shard_map.47), channel_id=1, source_target_pairs={{0,1},{1,0},{2,3},{3,2},{4,5},{5,4},{6,7},{7,6},{8,9},{9,8},{10,11... | collective-permute-start | bytes 2703368 | tf_op jit(solution)/shard_map/ppermute | solution.py:262
  2.6 0.1 collective-permute-start.1
  2.7 2.2 %collective-permute-done.1.came_ref = bf16[72,8,128]{2,1,0:T(8,128)(2,1)S(1)} collective-permute-done((bf16[72,8,128]{2,1,0:T(8,128)(2,1)S(1)}, bf16[72,8,128]{2,1,0:T(8,128)(2,1)S(1)}, u32[]{:S(2)}, u32[]{:S(2)}) %collective-permute-start.1) | collective-permute-done | bytes 147488 | tf_op jit(solution)/shard_map/ppermute | solution.py:262
  5.0 3.0 %collective-permute-start.2 = (bf16[72,8,128]{2,1,0:T(8,128)(2,1)S(1)}, bf16[72,8,128]{2,1,0:T(8,128)(2,1)S(1)}, u32[]{:S(2)}, u32[]{:S(2)}) collective-permute-start(bf16[72,8,128]{2,1,0:T(8,128)(2,1)S(1)} %shard_map.49), channel_id=1, source_target_pairs={{0,2},{1,3},{2,0},{3,1},{4,6},{5,7},{6,4},{7,5},{8,10},{9,11},{10,... | collective-permute-start | bytes 442376 | tf_op jit(solution)/shard_map/ppermute | solution.py:262
  7.9 0.0 collective-permute-done.came_ref
  7.9 0.2 shard_map.48
  8.1 0.1 collective-permute-start.4
  8.2 2.0 %collective-permute-start.6 = (bf16[72,8,128]{2,1,0:T(8,128)(2,1)S(1)}, bf16[72,8,128]{2,1,0:T(8,128)(2,1)S(1)}, u32[]{:S(2)}, u32[]{:S(2)}) collective-permute-start(bf16[72,8,128]{2,1,0:T(8,128)(2,1)S(1)} %get-tuple-element.29), channel_id=1, source_target_pairs={{0,2},{1,3},{2,0},{3,1},{4,6},{5,7},{6,4},{7,5},{8,10},{9,11},{10,... | collective-permute-start | bytes 442376 | tf_op jit(solution)/shard_map/ppermute | solution.py:262
  10.2 2.4 %collective-permute-done.2.passing_ref = bf16[72,8,128]{2,1,0:T(8,128)(2,1)S(1)} collective-permute-done((bf16[72,8,128]{2,1,0:T(8,128)(2,1)S(1)}, bf16[72,8,128]{2,1,0:T(8,128)(2,1)S(1)}, u32[]{:S(2)}, u32[]{:S(2)}) %collective-permute-start.2) | collective-permute-done | bytes 147488 | tf_op jit(solution)/shard_map/ppermute | solution.py:262
  12.7 3.1 %collective-permute-start.3 = (bf16[72,8,128]{2,1,0:T(8,128)(2,1)S(1)}, bf16[72,8,128]{2,1,0:T(8,128)(2,1)S(1)}, u32[]{:S(2)}, u32[]{:S(2)}) collective-permute-start(bf16[72,8,128]{2,1,0:T(8,128)(2,1)S(1)} %shard_map.50), channel_id=1, source_target_pairs={{0,4},{1,5},{2,6},{3,7},{4,0},{5,1},{6,2},{7,3},{8,12},{9,13},{10,... | collective-permute-start | bytes 442376 | tf_op jit(solution)/shard_map/ppermute | solution.py:262
  15.8 1.6 %collective-permute-start.7 = (bf16[56,8,128]{2,1,0:T(8,128)(2,1)S(1)}, bf16[56,8,128]{2,1,0:T(8,128)(2,1)S(1)}, u32[]{:S(2)}, u32[]{:S(2)}) collective-permute-start(bf16[56,8,128]{2,1,0:T(8,128)(2,1)S(1)} %get-tuple-element.30), channel_id=1, source_target_pairs={{0,2},{1,3},{2,0},{3,1},{4,6},{5,7},{6,4},{7,5},{8,10},{9,11},{10,... | collective-permute-start | bytes 344072 | tf_op jit(solution)/shard_map/ppermute | solution.py:262
  17.4 0.0 collective-permute-done.4.passing_ref
  17.4 0.8 %collective-permute-start.5 = (bf16[56,8,128]{2,1,0:T(8,128)(2,1)S(1)}, bf16[56,8,128]{2,1,0:T(8,128)(2,1)S(1)}, u32[]{:S(2)}, u32[]{:S(2)}) collective-permute-start(bf16[56,8,128]{2,1,0:T(8,128)(2,1)S(1)} %shard_map.51), channel_id=1, source_target_pairs={{0,4},{1,5},{2,6},{3,7},{4,0},{5,1},{6,2},{7,3},{8,12},{9,13},{10,... | collective-permute-start | bytes 344072 | tf_op jit(solution)/shard_map/ppermute | solution.py:262
  18.2 4.4 %collective-permute-done.6.refs_2_.refs_1_ = bf16[72,8,128]{2,1,0:T(8,128)(2,1)S(1)} collective-permute-done((bf16[72,8,128]{2,1,0:T(8,128)(2,1)S(1)}, bf16[72,8,128]{2,1,0:T(8,128)(2,1)S(1)}, u32[]{:S(2)}, u32[]{:S(2)}) %collective-permute-start.6) | collective-permute-done | bytes 147488 | tf_op jit(solution)/shard_map/ppermute | solution.py:262
  22.6 0.0 collective-permute-done.3.refs_0_
  22.6 0.6 %shard_map.54 = (f32[64,8,128]{2,1,0:T(8,128)S(1)}, f32[64,8,128]{2,1,0:T(8,128)S(1)}, bf16[64,8,128]{2,1,0:T(8,128)(2,1)S(1)}) custom-call(f32[128,8,128]{2,1,0:T(8,128)S(1)} %get-tuple-element.25.keep_ref, bf16[72,8,128]{2,1,0:T(8,128)(2,1)S(1)} %collective-permute-done.3.refs_0_, bf16[72,8,128]{2,1,0:T(8,128)(2,1)S(1)} %collective-permute-done.6.refs_2_.refs_1_), custom_call_target="tpu_custom_call" | custom-call | tf_op jit(solution)/shard_map/pallas_call | solution.py:250
  23.3 1.7 %collective-permute-start.10 = (bf16[64,8,128]{2,1,0:T(8,128)(2,1)S(1)}, bf16[64,8,128]{2,1,0:T(8,128)(2,1)S(1)}, u32[]{:S(2)}, u32[]{:S(2)}) collective-permute-start(bf16[64,8,128]{2,1,0:T(8,128)(2,1)S(1)} %get-tuple-element.38), channel_id=1, source_target_pairs={{0,16},{8,24},{16,0},{24,8},{1,17},{9,25},{17,1},{25,9},{2,18},{10... | collective-permute-start | bytes 393224 | tf_op jit(solution)/shard_map/ppermute | solution.py:262
  25.0 0.8 %collective-permute-done.7.refs_3_ = bf16[56,8,128]{2,1,0:T(8,128)(2,1)S(1)} collective-permute-done((bf16[56,8,128]{2,1,0:T(8,128)(2,1)S(1)}, bf16[56,8,128]{2,1,0:T(8,128)(2,1)S(1)}, u32[]{:S(2)}, u32[]{:S(2)}) %collective-permute-start.7) | collective-permute-done | bytes 114720 | tf_op jit(solution)/shard_map/ppermute | solution.py:262
  25.8 0.0 collective-permute-done.5.refs_1_
  25.8 0.6 %shard_map.52 = (f32[64,8,128]{2,1,0:T(8,128)S(1)}, f32[64,8,128]{2,1,0:T(8,128)S(1)}, bf16[64,8,128]{2,1,0:T(8,128)(2,1)S(1)}) custom-call(f32[128,8,128]{2,1,0:T(8,128)S(1)} %get-tuple-element.25.keep_ref, bf16[72,8,128]{2,1,0:T(8,128)(2,1)S(1)} %collective-permute-done.3.refs_0_, bf16[56,8,128]{2,1,0:T(8,128)(2,1)S(1)} %collective-permute-done.5.refs_1_, ...), custom_call_target="tpu_custom_call" | custom-call | tf_op jit(solution)/shard_map/pallas_call | solution.py:250
  26.4 1.8 %collective-permute-start.8 = (bf16[64,8,128]{2,1,0:T(8,128)(2,1)S(1)}, bf16[64,8,128]{2,1,0:T(8,128)(2,1)S(1)}, u32[]{:S(2)}, u32[]{:S(2)}) collective-permute-start(bf16[64,8,128]{2,1,0:T(8,128)(2,1)S(1)} %get-tuple-element.33), channel_id=1, source_target_pairs={{0,16},{8,24},{16,0},{24,8},{1,17},{9,25},{17,1},{25,9},{2,18},{10... | collective-permute-start | bytes 393224 | tf_op jit(solution)/shard_map/ppermute | solution.py:262
  28.2 0.1 collective-permute-done.10.came_ref
  28.3 1.7 %collective-permute-start.11 = (bf16[64,8,128]{2,1,0:T(8,128)(2,1)S(1)}, bf16[64,8,128]{2,1,0:T(8,128)(2,1)S(1)}, u32[]{:S(2)}, u32[]{:S(2)}) collective-permute-start(bf16[64,8,128]{2,1,0:T(8,128)(2,1)S(1)} %get-tuple-element.40), channel_id=1, source_target_pairs={{0,8},{8,0},{16,24},{24,16},{1,9},{9,1},{17,25},{25,17},{2,10},{10... | collective-permute-start | bytes 393224 | tf_op jit(solution)/shard_map/ppermute | solution.py:262
  30.0 1.4 %collective-permute-done.8.came_ref = bf16[64,8,128]{2,1,0:T(8,128)(2,1)S(1)} collective-permute-done((bf16[64,8,128]{2,1,0:T(8,128)(2,1)S(1)}, bf16[64,8,128]{2,1,0:T(8,128)(2,1)S(1)}, u32[]{:S(2)}, u32[]{:S(2)}) %collective-permute-start.8) | collective-permute-done | bytes 131104 | tf_op jit(solution)/shard_map/ppermute | solution.py:262
  31.5 1.7 %collective-permute-start.9 = (bf16[64,8,128]{2,1,0:T(8,128)(2,1)S(1)}, bf16[64,8,128]{2,1,0:T(8,128)(2,1)S(1)}, u32[]{:S(2)}, u32[]{:S(2)}) collective-permute-start(bf16[64,8,128]{2,1,0:T(8,128)(2,1)S(1)} %get-tuple-element.35), channel_id=1, source_target_pairs={{0,8},{8,0},{16,24},{24,16},{1,9},{9,1},{17,25},{25,17},{2,10},{10... | collective-permute-start | bytes 393224 | tf_op jit(solution)/shard_map/ppermute | solution.py:262
  33.2 1.0 %collective-permute-done.11.came_ref = bf16[64,8,128]{2,1,0:T(8,128)(2,1)S(1)} collective-permute-done((bf16[64,8,128]{2,1,0:T(8,128)(2,1)S(1)}, bf16[64,8,128]{2,1,0:T(8,128)(2,1)S(1)}, u32[]{:S(2)}, u32[]{:S(2)}) %collective-permute-start.11) | collective-permute-done | bytes 131104 | tf_op jit(solution)/shard_map/ppermute | solution.py:262
  34.2 0.7 %shard_map.56.refs_0_ = bf16[128,8,128]{2,1,0:T(8,128)(2,1)} custom-call(f32[64,8,128]{2,1,0:T(8,128)S(1)} %get-tuple-element.36.means_ref, f32[64,8,128]{2,1,0:T(8,128)S(1)} %get-tuple-element.39.sum_ref, bf16[64,8,128]{2,1,0:T(8,128)(2,1)S(1)} %collective-permute-done.11.came_ref), custom_call_target="tpu_custom_call" | custom-call | tf_op jit(solution)/shard_map/pallas_call | solution.py:250
  34.9 1.6 %collective-permute-done.9.came_ref = bf16[64,8,128]{2,1,0:T(8,128)(2,1)S(1)} collective-permute-done((bf16[64,8,128]{2,1,0:T(8,128)(2,1)S(1)}, bf16[64,8,128]{2,1,0:T(8,128)(2,1)S(1)}, u32[]{:S(2)}, u32[]{:S(2)}) %collective-permute-start.9) | collective-permute-done | bytes 131104 | tf_op jit(solution)/shard_map/ppermute | solution.py:262
  36.5 0.7 %shard_map.57 = bf16[128,8,128]{2,1,0:T(8,128)(2,1)} custom-call(f32[64,8,128]{2,1,0:T(8,128)S(1)} %get-tuple-element.31.means_ref, f32[64,8,128]{2,1,0:T(8,128)S(1)} %get-tuple-element.34.sum_ref, bf16[64,8,128]{2,1,0:T(8,128)(2,1)S(1)} %collective-permute-done.9.came_ref, bf16[128,8,128]{2,1,0:T(8,128)(2,1)} %shard_map.56.refs_0_), custom_call_target="tpu_custom_call", output_to_operand_aliasing={{}: (3, {})} | custom-call | tf_op jit(solution)/shard_map/pallas_call | solution.py:250
  (6 shorter events, 0.2 us)
Async XLA Ops:
  1.9 6.0 %copy-start = (f32[1,128,2,512]{3,2,1,0:T(2,128)S(1)}, f32[1,128,2,512]{3,2,1,0:T(2,128)}, u32[]{:S(2)}) copy-start(f32[1,128,2,512]{3,2,1,0:T(2,128)} %param.7) | copy-start | bytes 1572868
  2.1 5.9 %collective-permute-start = (bf16[440,8,128]{2,1,0:T(8,128)(2,1)S(1)}, bf16[440,8,128]{2,1,0:T(8,128)(2,1)S(1)}, u32[]{:S(2)}, u32[]{:S(2)}) collective-permute-start(bf16[440,8,128]{2,1,0:T(8,128)(2,1)S(1)} %shard_map.47), channel_id=1, source_target_pairs={{0,1},{1,0},{2,3},{3,2},{4,5},{5,4},{6,7},{7,6},{8,9},{9,8},{10,11... | collective-permute-start | bytes 2703368 | tf_op jit(solution)/shard_map/ppermute | solution.py:262
  2.6 2.3 %collective-permute-start.1 = (bf16[72,8,128]{2,1,0:T(8,128)(2,1)S(1)}, bf16[72,8,128]{2,1,0:T(8,128)(2,1)S(1)}, u32[]{:S(2)}, u32[]{:S(2)}) collective-permute-start(bf16[72,8,128]{2,1,0:T(8,128)(2,1)S(1)} %get-tuple-element.27), channel_id=1, source_target_pairs={{0,1},{1,0},{2,3},{3,2},{4,5},{5,4},{6,7},{7,6},{8,9},{9,8},{10,11... | collective-permute-start | bytes 442376 | tf_op jit(solution)/shard_map/ppermute | solution.py:262
  5.0 7.7 %collective-permute-start.2 = (bf16[72,8,128]{2,1,0:T(8,128)(2,1)S(1)}, bf16[72,8,128]{2,1,0:T(8,128)(2,1)S(1)}, u32[]{:S(2)}, u32[]{:S(2)}) collective-permute-start(bf16[72,8,128]{2,1,0:T(8,128)(2,1)S(1)} %shard_map.49), channel_id=1, source_target_pairs={{0,2},{1,3},{2,0},{3,1},{4,6},{5,7},{6,4},{7,5},{8,10},{9,11},{10,... | collective-permute-start | bytes 442376 | tf_op jit(solution)/shard_map/ppermute | solution.py:262
  8.1 9.2 %collective-permute-start.4 = (bf16[56,8,128]{2,1,0:T(8,128)(2,1)S(1)}, bf16[56,8,128]{2,1,0:T(8,128)(2,1)S(1)}, u32[]{:S(2)}, u32[]{:S(2)}) collective-permute-start(bf16[56,8,128]{2,1,0:T(8,128)(2,1)S(1)} %get-tuple-element.28), channel_id=1, source_target_pairs={{0,2},{1,3},{2,0},{3,1},{4,6},{5,7},{6,4},{7,5},{8,10},{9,11},{10,... | collective-permute-start | bytes 344072 | tf_op jit(solution)/shard_map/ppermute | solution.py:262
  8.2 14.4 %collective-permute-start.6 = (bf16[72,8,128]{2,1,0:T(8,128)(2,1)S(1)}, bf16[72,8,128]{2,1,0:T(8,128)(2,1)S(1)}, u32[]{:S(2)}, u32[]{:S(2)}) collective-permute-start(bf16[72,8,128]{2,1,0:T(8,128)(2,1)S(1)} %get-tuple-element.29), channel_id=1, source_target_pairs={{0,2},{1,3},{2,0},{3,1},{4,6},{5,7},{6,4},{7,5},{8,10},{9,11},{10,... | collective-permute-start | bytes 442376 | tf_op jit(solution)/shard_map/ppermute | solution.py:262
  12.7 10.0 %collective-permute-start.3 = (bf16[72,8,128]{2,1,0:T(8,128)(2,1)S(1)}, bf16[72,8,128]{2,1,0:T(8,128)(2,1)S(1)}, u32[]{:S(2)}, u32[]{:S(2)}) collective-permute-start(bf16[72,8,128]{2,1,0:T(8,128)(2,1)S(1)} %shard_map.50), channel_id=1, source_target_pairs={{0,4},{1,5},{2,6},{3,7},{4,0},{5,1},{6,2},{7,3},{8,12},{9,13},{10,... | collective-permute-start | bytes 442376 | tf_op jit(solution)/shard_map/ppermute | solution.py:262
  15.8 10.0 %collective-permute-start.7 = (bf16[56,8,128]{2,1,0:T(8,128)(2,1)S(1)}, bf16[56,8,128]{2,1,0:T(8,128)(2,1)S(1)}, u32[]{:S(2)}, u32[]{:S(2)}) collective-permute-start(bf16[56,8,128]{2,1,0:T(8,128)(2,1)S(1)} %get-tuple-element.30), channel_id=1, source_target_pairs={{0,2},{1,3},{2,0},{3,1},{4,6},{5,7},{6,4},{7,5},{8,10},{9,11},{10,... | collective-permute-start | bytes 344072 | tf_op jit(solution)/shard_map/ppermute | solution.py:262
  17.4 8.4 %collective-permute-start.5 = (bf16[56,8,128]{2,1,0:T(8,128)(2,1)S(1)}, bf16[56,8,128]{2,1,0:T(8,128)(2,1)S(1)}, u32[]{:S(2)}, u32[]{:S(2)}) collective-permute-start(bf16[56,8,128]{2,1,0:T(8,128)(2,1)S(1)} %shard_map.51), channel_id=1, source_target_pairs={{0,4},{1,5},{2,6},{3,7},{4,0},{5,1},{6,2},{7,3},{8,12},{9,13},{10,... | collective-permute-start | bytes 344072 | tf_op jit(solution)/shard_map/ppermute | solution.py:262
  23.3 5.0 %collective-permute-start.10 = (bf16[64,8,128]{2,1,0:T(8,128)(2,1)S(1)}, bf16[64,8,128]{2,1,0:T(8,128)(2,1)S(1)}, u32[]{:S(2)}, u32[]{:S(2)}) collective-permute-start(bf16[64,8,128]{2,1,0:T(8,128)(2,1)S(1)} %get-tuple-element.38), channel_id=1, source_target_pairs={{0,16},{8,24},{16,0},{24,8},{1,17},{9,25},{17,1},{25,9},{2,18},{10... | collective-permute-start | bytes 393224 | tf_op jit(solution)/shard_map/ppermute | solution.py:262
  26.4 5.0 %collective-permute-start.8 = (bf16[64,8,128]{2,1,0:T(8,128)(2,1)S(1)}, bf16[64,8,128]{2,1,0:T(8,128)(2,1)S(1)}, u32[]{:S(2)}, u32[]{:S(2)}) collective-permute-start(bf16[64,8,128]{2,1,0:T(8,128)(2,1)S(1)} %get-tuple-element.33), channel_id=1, source_target_pairs={{0,16},{8,24},{16,0},{24,8},{1,17},{9,25},{17,1},{25,9},{2,18},{10... | collective-permute-start | bytes 393224 | tf_op jit(solution)/shard_map/ppermute | solution.py:262
  28.3 5.8 %collective-permute-start.11 = (bf16[64,8,128]{2,1,0:T(8,128)(2,1)S(1)}, bf16[64,8,128]{2,1,0:T(8,128)(2,1)S(1)}, u32[]{:S(2)}, u32[]{:S(2)}) collective-permute-start(bf16[64,8,128]{2,1,0:T(8,128)(2,1)S(1)} %get-tuple-element.40), channel_id=1, source_target_pairs={{0,8},{8,0},{16,24},{24,16},{1,9},{9,1},{17,25},{25,17},{2,10},{10... | collective-permute-start | bytes 393224 | tf_op jit(solution)/shard_map/ppermute | solution.py:262
  31.5 5.0 %collective-permute-start.9 = (bf16[64,8,128]{2,1,0:T(8,128)(2,1)S(1)}, bf16[64,8,128]{2,1,0:T(8,128)(2,1)S(1)}, u32[]{:S(2)}, u32[]{:S(2)}) collective-permute-start(bf16[64,8,128]{2,1,0:T(8,128)(2,1)S(1)} %get-tuple-element.35), channel_id=1, source_target_pairs={{0,8},{8,0},{16,24},{24,16},{1,9},{9,1},{17,25},{25,17},{2,10},{10... | collective-permute-start | bytes 393224 | tf_op jit(solution)/shard_map/ppermute | solution.py:262
